TPU v7x, 32 devices: a whole 2x2x4 slice. The times are simulated.
32 devices in a mesh: groups: 2 (over x), stack: 4 (over y, core), bloch: 4 (over z).
Axes of the slice: x: 2, y: 2, z: 4, core: 2. Of those that a mesh axis runs over, the one named last changes fastest.
Arguments:
- drive: float32 [8, 8, 2, 192, 256], P(('groups', 'bloch'), 'stack'), parts along dimension 0, may hold values from -6 to 6
- positions: int32 [512], P('groups'), parts along dimension 0, may hold values from 0 to 3
- materials: int32 [16], P(('groups', 'stack')), parts along dimension 0, may hold values from 0 to 3
- table: float32 [4, 4, 192, 192], replicated, may hold values from -1 to 1
- thickness: float32 [16], P(('groups', 'stack')), parts along dimension 0, may hold values from 0.25 to 4
- decay: float32 [192], replicated, may hold values from 0.0025 to 2
Outputs:
- up_field: float32 [8, 4, 192, 256], P(('groups', 'bloch'), 'stack'), parts along dimension 0
- down_field: float32 [8, 4, 192, 256], P(('groups', 'bloch'), 'stack'), parts along dimension 0
There are 2 independent parts, one for each index of `groups`. A program takes and returns all parts, laid end to end along the dimension named above; an argument that names none is the same for every part. Nothing has to cross between parts.
All inputs are finite; a program needn't handle non-finite values.
Results may differ from a plain program's by a relative error of at most 0.00013.
Values sent between devices are 32-bit elements; how exact they have to be, the bound alone decides.
No kernel may reach another device: no remote copies, remote signals or barrier semaphores. Data moves between devices by JAX's collectives and lax.ppermute only.
A program may use at most 64 MiB of HBM per device.

v0:
```python
import math

import jax
import jax.numpy as jnp
from jax import lax
from jax.sharding import PartitionSpec as P

precise = lax.Precision.HIGHEST


def passed_along(block, axis, distance):
    devices = range(lax.axis_size(axis))
    route = [(i - distance, i) for i in devices if i - distance in devices]
    return lax.ppermute(block, axis, route)


def product(left_side, right_side):
    return jnp.einsum("...ij,...jk->...ik", left_side, right_side, precision=precise)


def cas_rows(row_ids, column_ids, cell_count):
    phases = row_ids[:, None] * column_ids[None, :] % cell_count
    angles = phases.astype(jnp.float32) * (2.0 * math.pi / cell_count)
    return (jnp.cos(angles) + jnp.sin(angles)) / math.sqrt(cell_count)


def inverse_gap(coupling):
    identity = jnp.eye(coupling.shape[-1], dtype=jnp.float32)
    system = identity - coupling
    approx = identity + coupling
    for repeat_index in range(6):
        approx = product(approx, 2.0 * identity - product(system, approx))
    return approx


def full_join(above_part, below_part):
    refl_top_a, trans_down_a, trans_up_a, refl_bot_a, src_up_a, src_down_a = above_part
    refl_top_b, trans_down_b, trans_up_b, refl_bot_b, src_up_b, src_down_b = below_part
    gap_inverse = inverse_gap(product(refl_bot_a, refl_top_b))
    down_inner = product(trans_down_b, gap_inverse)
    reflect_inner = product(refl_top_b, gap_inverse)
    bounce_up = product(refl_bot_a, trans_up_b)
    crossing = product(gap_inverse, src_down_a + product(refl_bot_a, src_up_b))
    return (
        refl_top_a + product(trans_up_a, product(reflect_inner, trans_down_a)),
        product(down_inner, trans_down_a),
        product(trans_up_a, trans_up_b + product(reflect_inner, bounce_up)),
        refl_bot_b + product(down_inner, bounce_up),
        src_up_a + product(trans_up_a, product(refl_top_b, crossing) + src_up_b),
        src_down_b + product(trans_down_b, crossing),
    )


def forward_join(above_part, below_part):
    refl_bot_a, src_down_a = above_part
    refl_top_b, trans_down_b, trans_up_b, refl_bot_b, src_up_b, src_down_b = below_part
    gap_inverse = inverse_gap(product(refl_bot_a, refl_top_b))
    down_inner = product(trans_down_b, gap_inverse)
    new_refl = refl_bot_b + product(down_inner, product(refl_bot_a, trans_up_b))
    new_source = src_down_b + product(down_inner, src_down_a + product(refl_bot_a, src_up_b))
    return (new_refl, new_source)


def backward_join(above_part, below_part):
    refl_top_a, trans_down_a, trans_up_a, refl_bot_a, src_up_a, src_down_a = above_part
    refl_top_b, src_up_b = below_part
    gap_inverse = inverse_gap(product(refl_bot_a, refl_top_b))
    reflect_inner = product(refl_top_b, gap_inverse)
    new_refl = refl_top_a + product(trans_up_a, product(reflect_inner, trans_down_a))
    crossing = product(gap_inverse, src_down_a + product(refl_bot_a, src_up_b))
    new_source = src_up_a + product(trans_up_a, product(refl_top_b, crossing) + src_up_b)
    return (new_refl, new_source)


def crossing_down(above_part, below_part):
    refl_bot_a, src_down_a = above_part
    refl_top_b, src_up_b = below_part
    gap_inverse = inverse_gap(product(refl_bot_a, refl_top_b))
    return product(gap_inverse, src_down_a + product(refl_bot_a, src_up_b))


def shards(drive, positions, materials, table, thickness, decay):
    cells_here = drive.shape[0]
    slab_count = drive.shape[1]
    mode_count = drive.shape[3]
    cell_count = cells_here * lax.axis_size("bloch")
    first_cell = lax.axis_index("bloch") * cells_here
    local_ids = first_cell + jnp.arange(cells_here, dtype=jnp.int32)
    offset = jnp.abs(local_ids[:, None] - positions[None, :])
    offset = jnp.minimum(offset, cell_count - offset)
    envelope = 1.0 / (1.0 + offset.astype(jnp.float32))
    sources = drive * envelope[:, None, None, None, :]
    wave_ids = jnp.arange(lax.axis_size("bloch") * cells_here, dtype=jnp.int32)
    spectrum = lax.psum_scatter(
        jnp.einsum(
            "kc,clsme->klsme", cas_rows(wave_ids, local_ids, cell_count), sources, precision=precise
        ),
        "bloch",
        scatter_dimension=0,
        tiled=True,
    )
    waves = local_ids.astype(jnp.float32)
    rates = decay[None, :] * (1.0 + 0.5 * jnp.cos(waves * (2.0 * math.pi / cell_count)))[:, None]
    onehot = (materials[:, None] == jnp.arange(table.shape[0], dtype=jnp.int32)[None, :]).astype(
        jnp.float32
    )
    chosen = jnp.einsum("ln,njab->ljab", onehot, table, precision=precise)
    damping = jnp.exp(-thickness[:, None, None] * rates[None])
    own_slab = None
    for layer_index in range(slab_count):
        layer_damp = damping[layer_index]
        scaled = (
            layer_damp[:, None, :, None] * chosen[layer_index][None] * layer_damp[:, None, None, :]
        )
        segment = (
            scaled[:, 0],
            scaled[:, 1],
            scaled[:, 2],
            scaled[:, 3],
            spectrum[:, layer_index, 0],
            spectrum[:, layer_index, 1],
        )
        own_slab = segment if own_slab is None else full_join(own_slab, segment)
    stack_index = lax.axis_index("stack")
    depth = lax.axis_size("stack")

    def unpack(packed):
        return (packed[..., :mode_count], packed[..., mode_count:])

    def pack(pair):
        return jnp.concatenate([pair[0], pair[1]], axis=-1)

    start_down = pack((own_slab[3], own_slab[5]))

    def pass_down(turn_index, carry):
        outgoing, held_prefix = carry
        arrived = passed_along(outgoing, "stack", 1)
        is_turn = stack_index == turn_index
        held_prefix = jnp.where(is_turn, arrived, held_prefix)
        outgoing = lax.cond(
            is_turn, lambda: pack(forward_join(unpack(arrived), own_slab)), lambda: outgoing
        )
        return (outgoing, held_prefix)

    incl_down, excl_down = lax.fori_loop(
        1, depth, pass_down, (start_down, jnp.zeros_like(start_down))
    )
    start_up = pack((own_slab[0], own_slab[4]))

    def pass_up(turn_index, carry):
        outgoing, held_suffix = carry
        arrived = passed_along(outgoing, "stack", -1)
        is_turn = stack_index == depth - 1 - turn_index
        held_suffix = jnp.where(is_turn, arrived, held_suffix)
        outgoing = lax.cond(
            is_turn, lambda: pack(backward_join(own_slab, unpack(arrived))), lambda: outgoing
        )
        return (outgoing, held_suffix)

    incl_up, excl_up = lax.fori_loop(1, depth, pass_up, (start_up, jnp.zeros_like(start_up)))
    excl_prefix = unpack(excl_down)
    incl_prefix = unpack(incl_down)
    excl_suffix = unpack(excl_up)
    incl_suffix = unpack(incl_up)
    downward_top = crossing_down(excl_prefix, incl_suffix)
    upward = product(incl_suffix[0], downward_top) + incl_suffix[1]
    downward = crossing_down(incl_prefix, excl_suffix)
    fields = jnp.stack([upward, downward], axis=1)
    cell_ids = jnp.arange(lax.axis_size("bloch") * cells_here, dtype=jnp.int32)
    result = lax.psum_scatter(
        jnp.einsum(
            "ck,ksme->csme", cas_rows(cell_ids, local_ids, cell_count), fields, precision=precise
        ),
        "bloch",
        scatter_dimension=0,
        tiled=True,
    )
    return (result[:, 0:1], result[:, 1:2])


def solution(mesh):
    in_specs = (
        P(("groups", "bloch"), "stack", None, None, None),
        P("groups"),
        P(("groups", "stack")),
        P(),
        P(("groups", "stack")),
        P(),
    )
    out_specs = (
        P(("groups", "bloch"), "stack", None, None),
        P(("groups", "bloch"), "stack", None, None),
    )
    return jax.shard_map(shards, mesh=mesh, in_specs=in_specs, out_specs=out_specs, check_vma=False)
```

profile of v0, /device:TPU:0, one launch (start us, length us, event | category | flops | bytes accessed | tf_op | source)
XLA Modules:
  0.0 251.4 jit_solution(13068270712680972411)
XLA Ops:
  8.1 1.2 multiply_bitcast_fusion
  9.4 2.0 broadcast_multiply_fusion
  11.7 4.1 %fusion.41 = f32[2,4,192,192]{3,0,2,1:T(2,128)S(1)} fusion(f32[4,4,192,192]{3,2,1,0:T(8,128)S(1)} %copy-done, s32[2]{0:T(128)S(1)} %copy-done.16), kind=kOutput, calls=%fused_computation.70 | convolution fusion | flops 14155784 | bytes 3538952 | tf_op jit(solution)/shard_map/ln,njab->ljab/dot_general | solution.py:107
  15.8 1.8 fusion.53
  17.5 1.1 fusion.121
  24.0 1.0 convolution_bitcast_fusion.11
  25.4 1.0 convolution_bitcast_fusion.12
  26.4 1.0 fusion.44
  27.7 1.0 fusion.46
  28.7 46.0 %reduce-scatter.3.cloned.1.call-done = f32[1,2,2,192,256]{4,3,2,1,0:T(8,128)} async-done(((f32[4,2,2,192,256]{4,3,2,1,0:T(8,128)}), f32[1,2,2,192,256]{4,3,2,1,0:T(8,128)}) %reduce-scatter.3.cloned.1.call-update) | async-done | bytes 786448 | tf_op jit(solution)/shard_map/reduce_scatter | solution.py:94
  74.7 1.4 convolution_add_fusion.5
  76.1 1.2 fusion.141
  77.4 1.3 fusion.43
  78.7 1.9 pad_maximum_fusion.3
  80.6 1.2 convolution_add_fusion.4
  81.9 1.2 fusion.45
  83.2 1.9 pad_maximum_fusion.2
  85.1 33.0 %while.39 = (s32[]{:T(128)}, f32[1,192,448]{2,1,0:T(8,128)}, f32[1,192,448]{2,1,0:T(8,128)}, s32[]{:T(128)}, f32[1,192,192]{2,1,0:T(8,128)}, /*index=5*/f32[1,19...) while((s32[]{:T(128)}, f32[1,192,448]{2,1,0:T(8,128)}, ...), condition=%wide.region_8.9_spmd.clone, body=%wide.region_5.8_spmd.clone.sunk | while | flops 1587388416 | bytes 14549358 | solution.py:145
  85.1 1.3 collective-permute-start.1
  86.4 1.5 collective-permute-done.1
  87.9 0.8 select_select_fusion.5
  88.8 17.1 %collective-permute-start.1 = (f32[1,192,448]{2,1,0:T(8,128)}, f32[1,192,448]{2,1,0:T(8,128)S(1)}, u32[]{:S(2)}, u32[]{:S(2)}) collective-permute-start(f32[1,192,448]{2,1,0:T(8,128)} %get-tuple-element.702), channel_id=1, source_target_pairs={{0,4},{4,8},{8,12},{1,5},{5,9},{9,13},{2,6},{6,10},{10,14},{3,7},{... | collective-permute-start | bytes 1032200 | tf_op jit(solution)/shard_map/while/body/eval_jaxpr/ppermute | solution.py:14
  105.9 1.5 collective-permute-done.1
  107.4 1.8 select_select_fusion.5
  109.3 5.4 %collective-permute-start.1 = (f32[1,192,448]{2,1,0:T(8,128)}, f32[1,192,448]{2,1,0:T(8,128)S(1)}, u32[]{:S(2)}, u32[]{:S(2)}) collective-permute-start(f32[1,192,448]{2,1,0:T(8,128)} %get-tuple-element.702), channel_id=1, source_target_pairs={{0,4},{4,8},{8,12},{1,5},{5,9},{9,13},{2,6},{6,10},{10,14},{3,7},{... | collective-permute-start | bytes 1032200 | tf_op jit(solution)/shard_map/while/body/eval_jaxpr/ppermute | solution.py:14
  114.7 1.5 collective-permute-done.1
  116.2 1.8 select_select_fusion.5
  118.0 73.8 %while.38 = (s32[]{:T(128)}, f32[1,192,448]{2,1,0:T(8,128)}, f32[1,192,448]{2,1,0:T(8,128)}, s32[]{:T(128)}, f32[1,192,192]{2,1,0:T(8,128)}, /*index=5*/f32[1,19...) while((s32[]{:T(128)}, f32[1,192,448]{2,1,0:T(8,128)}, ...), condition=%wide.region_4.5_spmd.clone, body=%wide.region_1.4_spmd.clone.sunk | while | flops 1813929984 | bytes 15827330 | solution.py:160
  118.0 1.3 collective-permute-start
  119.3 17.4 %collective-permute-done = f32[1,192,448]{2,1,0:T(8,128)S(1)} collective-permute-done((f32[1,192,448]{2,1,0:T(8,128)}, f32[1,192,448]{2,1,0:T(8,128)S(1)}, u32[]{:S(2)}, u32[]{:S(2)}) %collective-permute-start) | collective-permute-done | bytes 344096 | tf_op jit(solution)/shard_map/while/body/eval_jaxpr/ppermute | solution.py:14
  137.6 1.3 collective-permute-start
  138.9 8.6 %collective-permute-done = f32[1,192,448]{2,1,0:T(8,128)S(1)} collective-permute-done((f32[1,192,448]{2,1,0:T(8,128)}, f32[1,192,448]{2,1,0:T(8,128)S(1)}, u32[]{:S(2)}, u32[]{:S(2)}) %collective-permute-start) | collective-permute-done | bytes 344096 | tf_op jit(solution)/shard_map/while/body/eval_jaxpr/ppermute | solution.py:14
  147.5 1.8 select_select_fusion.4
  149.4 1.3 collective-permute-start
  150.7 28.3 %collective-permute-done = f32[1,192,448]{2,1,0:T(8,128)S(1)} collective-permute-done((f32[1,192,448]{2,1,0:T(8,128)}, f32[1,192,448]{2,1,0:T(8,128)S(1)}, u32[]{:S(2)}, u32[]{:S(2)}) %collective-permute-start) | collective-permute-done | bytes 344096 | tf_op jit(solution)/shard_map/while/body/eval_jaxpr/ppermute | solution.py:14
  178.9 11.0 %conditional.6 = (f32[1,192,448]{2,1,0:T(8,128)}) conditional(s32[]{:T(128)} %convert_element_type.141, f32[1,192,448]{2,1,0:T(8,128)} %get-tuple-element.664, (f32[1,192,192]{2,1,0:T(8,128)}, f32[1,192,448]{2,1,0:T(8,128)S(1)}, f32[1,192,192]{2,1,0:T(8,128)}, f32[1,192,192]{2,1,0:T(8,128)}, f32[1,192,192]{2,1,0:T(8,128)}, ...), branch_computations={%region_2.2_spmd, %region_3.3_spmd} | conditional | flops 1813757952 | bytes 13418616 | solution.py:155
  178.9 1.2 fusion.14
  184.3 1.3 fusion.2
  187.8 1.3 fusion
  189.1 0.9 pad_maximum_fusion
  190.0 1.8 select_select_fusion.4
  191.8 1.6 fusion.48
  193.4 1.3 fusion.81
  194.7 1.6 fusion.52
  196.3 1.3 fusion.75
  206.7 1.4 broadcast_multiply_fusion.1
  208.1 34.6 %reduce-scatter.5.cloned.1.call-done = f32[1,2,192,256]{3,2,1,0:T(8,128)} async-done(((f32[4,2,192,256]{3,2,1,0:T(8,128)}), f32[1,2,192,256]{3,2,1,0:T(8,128)}) %reduce-scatter.5.cloned.1.call-update) | async-done | bytes 393232 | tf_op jit(solution)/shard_map/reduce_scatter | solution.py:170
  242.7 1.8 fusion.123
  (109 shorter events, 22.8 us)
Async XLA Ops:
  7.2 4.5 %copy-start = (f32[4,4,192,192]{3,2,1,0:T(8,128)S(1)}, f32[4,4,192,192]{3,2,1,0:T(8,128)}, u32[]{:S(2)}) copy-start(f32[4,4,192,192]{3,2,1,0:T(8,128)} %param.17) | copy-start | bytes 7077892
  7.2 67.5 %reduce-scatter.3.cloned.1.call-start = ((), (), s32[]{:S(2)}) async-start(), calls=%async_computation.2 | async-start | bytes 3932160 | tf_op jit(solution)/shard_map/reduce_scatter | solution.py:94
  9.3 2.2 copy-start.17
  9.3 2.2 copy-start.15
  9.3 2.3 copy-start.16
  11.4 231.3 %reduce-scatter.5.cloned.1.call-start = ((), (), s32[]{:S(2)}) async-start(), calls=%async_computation.3 | async-start | bytes 1966080 | tf_op jit(solution)/shard_map/reduce_scatter | solution.py:170
  18.6 4.4 %copy-start.11 = (f32[1,1,192,192]{3,0,2,1:T(1,128)}, f32[1,1,192,192]{3,0,2,1:T(1,128)S(1)}, u32[]{:S(2)}) copy-start(f32[1,1,192,192]{3,0,2,1:T(1,128)S(1)} %get-tuple-element.525) | copy-start | bytes 442372
  18.6 6.4 %copy-start.14 = (f32[1,1,192,192]{3,0,2,1:T(1,128)}, f32[1,1,192,192]{3,0,2,1:T(1,128)S(1)}, u32[]{:S(2)}) copy-start(f32[1,1,192,192]{3,0,2,1:T(1,128)S(1)} %get-tuple-element.514) | copy-start | bytes 442372
  23.0 2.0 copy-start.12
  78.7 6.3 %copy-start.3 = (f32[1,192,256]{2,1,0:T(8,128)}, f32[1,192,256]{2,1,0:T(8,128)S(1)}, u32[]{:S(2)}) copy-start(f32[1,192,256]{2,1,0:T(8,128)S(1)} %fusion.43) | copy-start | bytes 589828
  83.2 1.9 copy-start.6
  85.1 2.9 %collective-permute-start.1 = (f32[1,192,448]{2,1,0:T(8,128)}, f32[1,192,448]{2,1,0:T(8,128)S(1)}, u32[]{:S(2)}, u32[]{:S(2)}) collective-permute-start(f32[1,192,448]{2,1,0:T(8,128)} %get-tuple-element.702), channel_id=1, source_target_pairs={{0,4},{4,8},{8,12},{1,5},{5,9},{9,13},{2,6},{6,10},{10,14},{3,7},{... | collective-permute-start | bytes 1032200 | tf_op jit(solution)/shard_map/while/body/eval_jaxpr/ppermute | solution.py:14
  88.8 18.6 %collective-permute-start.1 = (f32[1,192,448]{2,1,0:T(8,128)}, f32[1,192,448]{2,1,0:T(8,128)S(1)}, u32[]{:S(2)}, u32[]{:S(2)}) collective-permute-start(f32[1,192,448]{2,1,0:T(8,128)} %get-tuple-element.702), channel_id=1, source_target_pairs={{0,4},{4,8},{8,12},{1,5},{5,9},{9,13},{2,6},{6,10},{10,14},{3,7},{... | collective-permute-start | bytes 1032200 | tf_op jit(solution)/shard_map/while/body/eval_jaxpr/ppermute | solution.py:14
  109.3 6.9 %collective-permute-start.1 = (f32[1,192,448]{2,1,0:T(8,128)}, f32[1,192,448]{2,1,0:T(8,128)S(1)}, u32[]{:S(2)}, u32[]{:S(2)}) collective-permute-start(f32[1,192,448]{2,1,0:T(8,128)} %get-tuple-element.702), channel_id=1, source_target_pairs={{0,4},{4,8},{8,12},{1,5},{5,9},{9,13},{2,6},{6,10},{10,14},{3,7},{... | collective-permute-start | bytes 1032200 | tf_op jit(solution)/shard_map/while/body/eval_jaxpr/ppermute | solution.py:14
  118.0 18.7 %collective-permute-start = (f32[1,192,448]{2,1,0:T(8,128)}, f32[1,192,448]{2,1,0:T(8,128)S(1)}, u32[]{:S(2)}, u32[]{:S(2)}) collective-permute-start(f32[1,192,448]{2,1,0:T(8,128)} %get-tuple-element.664), channel_id=1, source_target_pairs={{4,0},{8,4},{12,8},{5,1},{9,5},{13,9},{6,2},{10,6},{14,10},{7,3},{... | collective-permute-start | bytes 1032200 | tf_op jit(solution)/shard_map/while/body/eval_jaxpr/ppermute | solution.py:14
  137.6 9.9 %collective-permute-start = (f32[1,192,448]{2,1,0:T(8,128)}, f32[1,192,448]{2,1,0:T(8,128)S(1)}, u32[]{:S(2)}, u32[]{:S(2)}) collective-permute-start(f32[1,192,448]{2,1,0:T(8,128)} %get-tuple-element.664), channel_id=1, source_target_pairs={{4,0},{8,4},{12,8},{5,1},{9,5},{13,9},{6,2},{10,6},{14,10},{7,3},{... | collective-permute-start | bytes 1032200 | tf_op jit(solution)/shard_map/while/body/eval_jaxpr/ppermute | solution.py:14
  149.4 29.6 %collective-permute-start = (f32[1,192,448]{2,1,0:T(8,128)}, f32[1,192,448]{2,1,0:T(8,128)S(1)}, u32[]{:S(2)}, u32[]{:S(2)}) collective-permute-start(f32[1,192,448]{2,1,0:T(8,128)} %get-tuple-element.664), channel_id=1, source_target_pairs={{4,0},{8,4},{12,8},{5,1},{9,5},{13,9},{6,2},{10,6},{14,10},{7,3},{... | collective-permute-start | bytes 1032200 | tf_op jit(solution)/shard_map/while/body/eval_jaxpr/ppermute | solution.py:14
  180.5 3.7 %copy-start.5 = (f32[1,192,256]{2,1,0:T(8,128)S(1)}, f32[1,192,256]{2,1,0:T(8,128)}, u32[]{:S(2)}) copy-start(f32[1,192,256]{2,1,0:T(8,128)} %get-tuple-element.364) | copy-start | bytes 589828 | tf_op jit(solution)/shard_map/while/body/eval_jaxpr/cond
  181.9 4.4 %copy-start.2 = (f32[1,192,192]{2,1,0:T(8,128)S(1)}, f32[1,192,192]{2,1,0:T(8,128)}, u32[]{:S(2)}) copy-start(f32[1,192,192]{2,1,0:T(8,128)} %get-tuple-element.362) | copy-start | bytes 442372 | tf_op jit(solution)/shard_map/while/body/eval_jaxpr/cond
  181.9 4.4 %copy-start.8 = (f32[1,192,256]{2,1,0:T(8,128)S(1)}, f32[1,192,256]{2,1,0:T(8,128)}, u32[]{:S(2)}) copy-start(f32[1,192,256]{2,1,0:T(8,128)} %get-tuple-element.363) | copy-start | bytes 589828 | tf_op jit(solution)/shard_map/while/body/eval_jaxpr/cond
  182.6 4.6 %copy-start.10 = (f32[1,192,192]{2,1,0:T(8,128)S(1)}, f32[1,192,192]{2,1,0:T(8,128)}, u32[]{:S(2)}) copy-start(f32[1,192,192]{2,1,0:T(8,128)} %get-tuple-element.361) | copy-start | bytes 442372 | tf_op jit(solution)/shard_map/while/body/eval_jaxpr/cond
  198.3 3.7 %copy-start.13 = (f32[1,192,448]{2,1,0:T(8,128)S(1)}, f32[1,192,448]{2,1,0:T(8,128)}, u32[]{:S(2)}) copy-start(f32[1,192,448]{2,1,0:T(8,128)} %get-tuple-element.400) | copy-start | bytes 1032196
Sparse Core Ops, SparseCore 0:
  11.5 63.1 reduce-scatter.2
  208.2 34.4 reduce-scatter.4
where the time goes:
time: 252 us; the launch traced here: 251 us
  waiting for transfers between devices  139 us (55%)
  matrix products  45 us (18%)
  starting transfers between devices  27.8 us (11%)
  other arithmetic  21.1 us (8%)
  between operations  14.7 us (6%)
  local copies, waits for them, and re-layouts  2.96 us (1%)
    ppermute x6, waiting for transfers between devices, passed_along(): return lax.ppermute(block, axis, route)  58.9 us
    reduce_scatter x1, waiting for transfers between devices, shards(): lax.psum_scatter(jnp.einsum('kc,clsme->klsme', cas_rows(wave_ids, local_i...  46 us
    dot_general x78, matrix products, product(): jnp.einsum('...ij,...jk->...ik', left_side, right_side, precision=precise)  40.9 us
    reduce_scatter x1, waiting for transfers between devices, shards(): lax.psum_scatter(jnp.einsum('ck,ksme->csme', cas_rows(cell_ids, local_ids...  34.6 us
    ppermute x6, starting transfers between devices, passed_along(): return lax.ppermute(block, axis, route)  27.7 us
  transfers between devices with their start and end apart: 8, of which 8 were waited for; matrix products, arithmetic and copies ran while one was open for 7% of the time, Pallas kernels for 0%

commit v1 on v0

v1 whole, which is shorter than its diff:
```python
import functools
import math

import jax
import jax.numpy as jnp
from jax import lax
from jax.experimental import pallas as pl
from jax.experimental.pallas import tpu as pltpu
from jax.sharding import PartitionSpec as P

PAIR = 2
FIXED_DOUBLINGS = 3
SMALL = 3e-8

f32 = jnp.float32


def dot(left_side, right_side, precision=lax.Precision.HIGH):
    return lax.dot_general(
        left_side,
        right_side,
        (((1,), (0,)), ((), ())),
        precision=precision,
        preferred_element_type=f32,
    )


def eye(size):
    rows = lax.broadcasted_iota(jnp.int32, (size, size), 0)
    columns = lax.broadcasted_iota(jnp.int32, (size, size), 1)
    return (rows == columns).astype(f32)


def peak(value):
    return jnp.max(jnp.abs(value))


def inverses(couplings, sum_ref, power_ref, coupling_ref):
    size = couplings[0].shape[0]
    identity = eye(size)
    sums = [identity + c for c in couplings]
    powers = [dot(c, c) for c in couplings]
    for _ in range(FIXED_DOUBLINGS):
        sums = [s + dot(s, p) for s, p in zip(sums, powers)]
        powers = [dot(p, p) for p in powers]
    biggest = powers[0]
    biggest = jnp.abs(biggest)
    for p in powers[1:]:
        biggest = jnp.maximum(biggest, jnp.abs(p))
    for i, (s, p, c) in enumerate(zip(sums, powers, couplings)):
        sum_ref[i] = s
        power_ref[i] = p
        coupling_ref[i] = c
    worst = jnp.max(biggest)

    @pl.when(jnp.logical_not(worst <= SMALL))
    def _():
        def one(i, carry):
            def going(state):
                count, size_now = state
                return (count < 16) & (size_now > SMALL) & (size_now < 1e8)

            def double(state):
                count, _ = state
                power = power_ref[i]
                sum_ref[i] = sum_ref[i] + dot(sum_ref[i], power, lax.Precision.HIGHEST)
                power = dot(power, power, lax.Precision.HIGHEST)
                power_ref[i] = power
                return (count + 1, peak(power))

            _, left_over = lax.while_loop(going, double, (jnp.int32(0), peak(power_ref[i])))

            @pl.when(jnp.logical_not(left_over <= SMALL))
            def _():
                identity = eye(size)
                system = identity - coupling_ref[i]
                flipped = lax.dot_general(
                    system,
                    identity,
                    (((0,), (0,)), ((), ())),
                    precision=lax.Precision.HIGHEST,
                    preferred_element_type=f32,
                )
                row_bound = jnp.max(jnp.sum(jnp.abs(system), axis=1, keepdims=True))
                column_bound = jnp.max(jnp.sum(jnp.abs(system), axis=0, keepdims=True))
                sum_ref[i] = flipped / (row_bound * column_bound)

                def refining(state):
                    count, gap = state
                    return (count < 100) & (gap > 1e-4)

                def refine(state):
                    count, _ = state
                    system = eye(size) - coupling_ref[i]
                    error = eye(size) - dot(system, sum_ref[i], lax.Precision.HIGHEST)
                    sum_ref[i] = sum_ref[i] + dot(sum_ref[i], error, lax.Precision.HIGHEST)
                    return (count + 1, peak(error))

                lax.while_loop(refining, refine, (jnp.int32(0), f32(1.0)))

            return carry

        lax.fori_loop(0, len(couplings), one, 0)

    return [sum_ref[i] for i in range(len(couplings))]


def inner_maps(above, below, gap):
    _, _, up_a, bottom_a = above
    top_b, down_b, _, _ = below
    identity = eye(gap.shape[0])
    mid_y_d = dot(top_b, gap)
    mid_x_u = dot(gap, bottom_a)
    mid_y_u = identity + dot(top_b, mid_x_u)
    return (
        (dot(up_a, mid_y_d), gap, mid_y_d, dot(down_b, gap)),
        (dot(up_a, mid_y_u), mid_x_u, mid_y_u, dot(down_b, mid_x_u)),
    )


def in_batches(count, work):
    size = 2 if count % 2 == 0 else 1
    if count == size:
        work(0, size)
    else:
        def step(i, carry):
            work(i * size, size)
            return carry

        lax.fori_loop(0, count // size, step, 0)


def matrices_kernel(layers, vectors, *refs):
    in_batches(vectors, lambda start, size: matrices_of(layers, start, size, *refs))


def matrices_of(layers, start, vectors, factor_ref, material_ref, thick_ref, first_ref, table_ref, row_ref, column_ref,
                    slab_d, slab_u, pair_d, pair_u, end_x, end_y, onward, sum_ref, power_ref, coupling_ref):
    m = table_ref.shape[-1]
    segments = {}
    for k in range(vectors):
        for j in range(PAIR):
            for i in range(layers):
                thick = thick_ref[j * layers + i]
                which = material_ref[j * layers + i]
                row = jnp.exp(-(thick * factor_ref[start + k]) * row_ref[...])
                column = jnp.exp(-(thick * factor_ref[start + k]) * column_ref[...])
                segments[k, j, i] = tuple(column * table_ref[which, b] * row for b in range(4))
    slabs = {}
    keys = [(k, j) for k in range(vectors) for j in range(PAIR)]
    for k, j in keys:
        slabs[k, j] = segments[k, j, 0]
    for i in range(1, layers):
        gaps = inverses([dot(slabs[k, j][3], segments[k, j, i][0]) for k, j in keys], sum_ref, power_ref, coupling_ref)
        for (k, j), gap in zip(keys, gaps):
            above, below = slabs[k, j], segments[k, j, i]
            by_d, by_u = inner_maps(above, below, gap)
            slab_d[start + k, j, i - 1, 0:m] = by_d[0]
            slab_d[start + k, j, i - 1, m:] = by_d[3]
            slab_u[start + k, j, i - 1, 0:m] = by_u[0]
            slab_u[start + k, j, i - 1, m:] = by_u[3]
            slabs[k, j] = (
                above[0] + dot(by_d[0], above[1]),
                dot(by_d[3], above[1]),
                dot(by_u[0], below[2]),
                below[3] + dot(by_u[3], below[2]),
            )
    gaps = inverses([dot(slabs[k, 0][3], slabs[k, 1][0]) for k in range(vectors)], sum_ref, power_ref, coupling_ref)
    first = first_ref[0]
    for k, gap in zip(range(vectors), gaps):
        above, below = slabs[k, 0], slabs[k, 1]
        by_d, by_u = inner_maps(above, below, gap)
        top_x = above[0] + dot(by_d[0], above[1])
        end_y_end = below[3] + dot(by_u[3], below[2])
        onward[start + k] = jnp.where(first == 1, end_y_end, top_x)
        for r in range(4):
            pair_d[start + k, r * m:(r + 1) * m] = by_d[r]
            pair_u[start + k, r * m:(r + 1) * m] = by_u[r]
        end_x[start + k, 0:m] = top_x
        end_y[start + k, 0:m] = dot(by_u[0], below[2])
        for r in range(1, 4):
            end_x[start + k, r * m:(r + 1) * m] = dot(by_d[r], above[1])
        for r in range(1, 3):
            end_y[start + k, r * m:(r + 1) * m] = dot(by_u[r], below[2])
        end_y[start + k, 3 * m:] = end_y_end


def boundary_kernel(vectors, *refs):
    in_batches(vectors, lambda start, size: boundary_of(start, size, *refs))


def boundary_of(start, vectors, flag_ref, end_x, end_y, prefix_ref, suffix_ref, from_d, from_u, own_d, own_u,
                sum_ref, power_ref, coupling_ref):
    m = end_x.shape[-1]
    ks = [start + i for i in range(vectors)]
    prefix = [prefix_ref[k] * flag_ref[0] for k in ks]
    suffix = [suffix_ref[k] * flag_ref[1] for k in ks]
    lower = inverses([dot(s, end_y[k, 3 * m:]) for k, s in zip(ks, suffix)], sum_ref, power_ref, coupling_ref)
    bounced = [dot(dot(low, s), end_x[k, 3 * m:]) for k, low, s in zip(ks, lower, suffix)]
    top = [end_x[k, 0:m] + dot(end_y[k, 0:m], b) for k, b in zip(ks, bounced)]
    upper = inverses([dot(p, t) for p, t in zip(prefix, top)], sum_ref, power_ref, coupling_ref)
    for k, low, up, bounce, p, s in zip(ks, lower, upper, bounced, prefix, suffix):
        by_d = dot(end_x[k] + dot(end_y[k], bounce), up)
        by_u = dot(dot(by_d, dot(p, end_y[k, 0:m])) + end_y[k], low)
        from_d[k] = by_d
        from_u[k] = by_u
        own_u[k] = dot(by_d, p)
        own_d[k] = dot(by_u, s)


def pack_kernel(share, parts, where_ref, drive_ref, position_ref, *outs):
    *blocks, held = outs
    cell, cells = where_ref[0], parts
    offset = jnp.abs(cell - position_ref[...])
    offset = jnp.minimum(offset, cells - offset)
    envelope = 1.0 / (1.0 + offset.astype(f32))
    layers = drive_ref.shape[1]
    for q in range(parts):
        span = slice(q * share, (q + 1) * share)
        held[q] = jnp.concatenate(
            [drive_ref[0, i, d, :, span] * envelope[:, span] for i in range(layers) for d in range(2)], axis=1
        )
    for shift in range(parts):
        blocks[shift][...] = held[lax.rem(cell + shift, cells)]


def transform_kernel(parts, weight_ref, *refs):
    blocks, (kept, sent) = refs[:parts], refs[parts:]
    loaded = [b[...] for b in blocks]
    for side, out in enumerate((kept, sent)):
        for i in range(out.shape[0]):
            total = weight_ref[side, i, 0] * loaded[0]
            for shift in range(1, parts):
                total = total + weight_ref[side, i, shift] * loaded[shift]
            out[i] = total


def sources_kernel(layers, share, vectors, parity_ref, kept, got, slab_d, slab_u, pair_d, pair_u, inner, ends, held):
    m = kept.shape[1]
    parity = parity_ref[0]
    for k in range(vectors):
        held[parity, k] = kept[k]
        held[1 - parity, k] = got[k]
    for k in range(vectors):
        pair = []
        for j in range(PAIR):
            block = held[j, k]
            up, down = block[:, 0:share], block[:, share:2 * share]
            for i in range(1, layers):
                at = 2 * i * share
                up_b, down_b = block[:, at:at + share], block[:, at + share:at + 2 * share]
                both = dot(slab_d[k, j, i - 1], down) + dot(slab_u[k, j, i - 1], up_b)
                up, down = up + both[0:m], down_b + both[m:]
            pair.append((up, down))
        rows = dot(pair_d[k], pair[0][1]) + dot(pair_u[k], pair[1][0])
        top = rows[0:m] + pair[0][0]
        end = rows[3 * m:] + pair[1][1]
        inner[k, 0:m] = top
        inner[k, m:3 * m] = rows[m:3 * m]
        inner[k, 3 * m:] = end
        ends[k, 0] = end
        ends[k, 1] = top


def own_kernel(vectors, inner, ends, own_d, own_u, out):
    for k in range(vectors):
        out[k] = inner[k] + dot(own_d[k], ends[k, 0]) + dot(own_u[k], ends[k, 1])


def fields_kernel(vectors, flag_ref, parity_ref, inner, above_ref, below_ref, from_d, from_u, kept, sent, held):
    m = inner.shape[1] // 4
    for k in range(vectors):
        rows = inner[k] + dot(from_d[k], above_ref[k] * flag_ref[0]) + dot(from_u[k], below_ref[k] * flag_ref[1])
        for j in range(PAIR):
            held[j, k] = jnp.concatenate([rows[2 * j * m:(2 * j + 1) * m], rows[(2 * j + 1) * m:(2 * j + 2) * m]], axis=1)
    parity = parity_ref[0]
    for k in range(vectors):
        kept[k] = held[parity, k]
        sent[k] = held[1 - parity, k]


def return_kernel(parts, weight_ref, kept, got, *blocks):
    vectors = kept.shape[0]
    for shift in range(parts):
        total = weight_ref[0, 0, shift] * kept[0]
        for side, ref in enumerate((kept, got)):
            for i in range(vectors):
                if side or i:
                    total = total + weight_ref[side, i, shift] * ref[i]
        blocks[shift][...] = total


def unpack_kernel(share, parts, where_ref, *refs):
    blocks, (up, down, held) = refs[:parts], refs[parts:]
    place = where_ref[0]
    for shift in range(parts):
        held[lax.rem(place - shift + parts, parts)] = blocks[shift][...]
    for side, out in enumerate((up, down)):
        span = slice(side * share, (side + 1) * share)
        out[0, 0] = jnp.concatenate([held[q][:, span] for q in range(parts)], axis=1)


def vmem():
    return pl.BlockSpec(memory_space=pltpu.VMEM)


def smem():
    return pl.BlockSpec(memory_space=pltpu.SMEM)


def call(kernel, scalars, arrays, shapes, scratch=(), name=None, flops=0):
    moved = sum(a.size * 4 for a in arrays) + sum(math.prod(s) * 4 for s in shapes)
    return pl.pallas_call(
        kernel,
        out_shape=tuple(jax.ShapeDtypeStruct(s, f32) for s in shapes),
        in_specs=[smem()] * len(scalars) + [vmem()] * len(arrays),
        out_specs=tuple(vmem() for _ in shapes),
        scratch_shapes=[pltpu.VMEM(s, f32) for s in scratch],
        cost_estimate=pl.CostEstimate(flops=flops, bytes_accessed=moved, transcendentals=0),
        name=name,
    )(*scalars, *arrays)


def cas(rows, columns, count):
    angles = (rows * columns % count).astype(f32) * (2.0 * math.pi / count)
    return (jnp.cos(angles) + jnp.sin(angles)) / math.sqrt(count)


def exact(left_side, right_side):
    return jnp.einsum("kij,kjl->kil", left_side, right_side, precision=lax.Precision.HIGHEST)


def plain_inverse(coupling):
    identity = jnp.eye(coupling.shape[-1], dtype=f32)
    approx = identity + coupling

    def step(_, approx):
        return exact(approx, 2.0 * identity - exact(identity - coupling, approx))

    return lax.fori_loop(0, 6, step, approx)


def shards(drive, positions, materials, table, thickness, decay):
    parts = lax.axis_size("bloch")
    depth = lax.axis_size("stack")
    groups = depth // PAIR
    layers, m, columns = drive.shape[1], drive.shape[3], drive.shape[4]
    vectors = parts // PAIR
    share = columns // parts
    assert drive.shape[0] == 1 and depth % PAIR == 0 and parts % PAIR == 0 and columns % parts == 0
    place = lax.axis_index("bloch")
    stack_index = lax.axis_index("stack")
    group, parity = stack_index // PAIR, stack_index % PAIR
    place_ref, parity_ref = place[None].astype(jnp.int32), parity[None].astype(jnp.int32)
    partner = [(i, i ^ 1) for i in range(depth)]

    described = jnp.stack([materials.astype(f32), thickness])
    other = lax.ppermute(described, "stack", partner)
    both = jnp.where(parity == 0, jnp.concatenate([described, other], 1), jnp.concatenate([other, described], 1))
    kinds, thick = both[0].astype(jnp.int32), both[1]

    width = layers * 2 * share
    packed = call(
        functools.partial(pack_kernel, share, parts),
        [place_ref], [drive, positions[None, :]], [(m, width)] * parts, [(parts, m, width)], "pack",
    )

    def deal(blocks):
        out = [blocks[0]]
        for shift in range(1, parts):
            out.append(lax.ppermute(blocks[shift], "bloch", [(i, (i + shift) % parts) for i in range(parts)]))
        return out

    arrived = deal(packed)

    waves = jnp.arange(vectors, dtype=jnp.int32) * PAIR + parity
    factors = 1.0 + 0.5 * jnp.cos(waves.astype(f32) * (2.0 * math.pi / parts))
    first = (group == 0)[None].astype(jnp.int32)
    squares = [(vectors * PAIR, m, m)] * 3
    slab_d, slab_u, pair_d, pair_u, end_x, end_y, onward = call(
        functools.partial(matrices_kernel, layers, vectors),
        [factors, kinds, thick, first],
        [table, decay[None, :], decay[:, None]],
        [(vectors, PAIR, layers - 1, 2 * m, m)] * 2 + [(vectors, 4 * m, m)] * 4 + [(vectors, m, m)],
        squares, "matrices", 2 * 122 * m**3,
    )
    down_route = [(i, i + PAIR) for i in range(depth - PAIR)]
    up_route = [(i + PAIR, i) for i in range(depth - PAIR)]
    if groups == 2:
        prefix = suffix = lax.ppermute(onward, "stack", down_route + up_route)
        flags = jnp.stack([group == 1, group == 0]).astype(f32)
    else:
        flags = jnp.ones((2,), f32)
        top_t, down_t = end_x[:, 0:m], end_x[:, 3 * m:]
        up_t, end_t = end_y[:, 0:m], end_y[:, 3 * m:]

        def matrix_turn(turn, carry):
            prefix, suffix, falling, rising = carry
            prefix = jnp.where(group == turn, lax.ppermute(falling, "stack", down_route), prefix)
            suffix = jnp.where(group == groups - 1 - turn, lax.ppermute(rising, "stack", up_route), suffix)
            carry_d = exact(down_t, plain_inverse(exact(prefix, top_t)))
            carry_u = exact(up_t, plain_inverse(exact(suffix, end_t)))
            falling = jnp.where(group == turn, end_t + exact(carry_d, exact(prefix, up_t)), falling)
            rising = jnp.where(group == groups - 1 - turn, top_t + exact(carry_u, exact(suffix, down_t)), rising)
            return prefix, suffix, falling, rising

        nothing = jnp.zeros_like(onward)
        prefix, suffix, _, _ = lax.fori_loop(1, groups, matrix_turn, (nothing, nothing, end_t, top_t))
    from_d, from_u, own_d, own_u = call(
        functools.partial(boundary_kernel, vectors),
        [flags], [end_x, end_y, prefix, suffix], [(vectors, 4 * m, m)] * 4, squares, "boundary", 2 * 88 * m**3,
    )

    shifts = jnp.arange(parts, dtype=jnp.int32)
    wave_table = jnp.stack([waves, waves + 1 - 2 * parity])
    cells_from = (place - shifts) % parts
    kept, sent = call(
        functools.partial(transform_kernel, parts),
        [cas(wave_table[:, :, None], cells_from[None, None, :], parts)], arrived, [(vectors, m, width)] * 2, (), "transform",
    )
    got = lax.ppermute(sent, "stack", partner)
    inner, ends = call(
        functools.partial(sources_kernel, layers, share, vectors),
        [parity_ref], [kept, got, slab_d, slab_u, pair_d, pair_u],
        [(vectors, 4 * m, share), (vectors, 2, m, share)], [(PAIR, vectors, m, width)], "sources",
    )
    if groups == 2:
        chosen = jnp.where(group == 0, ends[:, 0], ends[:, 1])
        chosen = jnp.transpose(chosen, (1, 0, 2)).reshape(m, vectors * share)
        chosen = lax.ppermute(chosen, "stack", down_route + up_route)
        above = below = jnp.transpose(chosen.reshape(m, vectors, share), (1, 0, 2))
    else:
        end_s, top_s = ends[:, 0], ends[:, 1]
        carry_d = exact(down_t, plain_inverse(exact(prefix, top_t)))
        carry_u = exact(up_t, plain_inverse(exact(suffix, end_t)))

        def source_turn(turn, carry):
            above, below, falling, rising = carry
            above = jnp.where(group == turn, lax.ppermute(falling, "stack", down_route), above)
            below = jnp.where(group == groups - 1 - turn, lax.ppermute(rising, "stack", up_route), below)
            falling = jnp.where(group == turn, end_s + exact(carry_d, above + exact(prefix, top_s)), falling)
            rising = jnp.where(group == groups - 1 - turn, top_s + exact(carry_u, below + exact(suffix, end_s)), rising)
            return above, below, falling, rising

        nothing = jnp.zeros_like(end_s)
        above, below, _, _ = lax.fori_loop(1, groups, source_turn, (nothing, nothing, end_s, top_s))
    (answered,) = call(
        functools.partial(own_kernel, vectors),
        [], [inner, ends, own_d, own_u], [(vectors, 4 * m, share)], (), "own",
    )
    kept, sent = call(
        functools.partial(fields_kernel, vectors),
        [flags, parity_ref], [answered, above, below, from_d, from_u],
        [(vectors, m, 2 * share)] * 2, [(PAIR, vectors, m, 2 * share)], "fields",
    )
    got = lax.ppermute(sent, "stack", partner)

    cells_to = (place + shifts) % parts
    blocks = call(
        functools.partial(return_kernel, parts),
        [cas(wave_table[:, :, None], cells_to[None, None, :], parts)], [kept, got], [(m, 2 * share)] * parts, (), "return",
    )
    blocks = deal(blocks)
    return call(
        functools.partial(unpack_kernel, share, parts),
        [place_ref], blocks, [(1, 1, m, columns)] * 2, [(parts, m, 2 * share)], "unpack",
    )


def solution(mesh):
    in_specs = (
        P(("groups", "bloch"), "stack", None, None, None),
        P("groups"),
        P(("groups", "stack")),
        P(),
        P(("groups", "stack")),
        P(),
    )
    out_specs = (
        P(("groups", "bloch"), "stack", None, None),
        P(("groups", "bloch"), "stack", None, None),
    )
    return jax.shard_map(shards, mesh=mesh, in_specs=in_specs, out_specs=out_specs, check_vma=False)
```

time: 252 us -> 101 us (0.40)
  waiting for transfers between devices: 139 us -> 17.1 us
  Pallas kernels: 0 us -> 55.2 us
  matrix products: 45 us -> 0 us
  other arithmetic: 21.1 us -> 5.59 us
  between operations: 14.7 us -> 0.68 us
  starting transfers between devices: 27.8 us -> 16.1 us
  local copies, waits for them, and re-layouts: 2.96 us -> 5.99 us
    reduce_scatter x2 -> x0, waiting for transfers between devices: 80.6 us -> none  [the longest x1 46 us: shards(): lax.psum_scatter(jnp.einsum('kc,clsme->klsme', cas_rows(wave_ids, local_i...]
    pallas_call x0 -> x9, Pallas kernels: none -> 55.2 us  [call(): pl.pallas_call(kernel, out_shape=tuple((jax.ShapeDtypeStruct(s, f32) for...]
    dot_general x79 -> x0, matrix products: 45 us -> none  [the longest x78 40.9 us: product(): jnp.einsum('...ij,...jk->...ik', left_side, right_side, precision=precise)]
    ppermute x6 -> x11, waiting for transfers between devices: 58.9 us -> 17.1 us  [the longest x6 15.2 us: deal(): lax.ppermute(blocks[shift], 'bloch', [(i, (i + shift) % parts) for i in r...]
    ppermute x6 -> x11, starting transfers between devices: 27.7 us -> 16.1 us  [the longest x6 13.5 us: deal(): lax.ppermute(blocks[shift], 'bloch', [(i, (i + shift) % parts) for i in r...]
    select_n x6 -> x2, other arithmetic: 8.99 us -> 0.82 us  [the longest x1 0.81 us: shards(): jnp.where(parity == 0, jnp.concatenate([described, other], 1), jnp.concat...]
    concatenate x3 -> x0, other arithmetic: 4.71 us -> none  [pack(): return jnp.concatenate([pair[0], pair[1]], axis=-1)]
    unnamed x20 -> x18, local copies, waits for them, and re-layouts: 0.06 us -> 3.64 us
  transfers between devices with their start and end apart: 8 -> 11, of which waited for: 8 -> 6; matrix products, arithmetic and copies ran while one was open for 7% -> 6% of each run, Pallas kernels for 0% -> 44%
where the time goes in v1:
time: 101 us
  Pallas kernels  55.2 us (55%)
  waiting for transfers between devices  17.1 us (17%)
  starting transfers between devices  16.1 us (16%)
  local copies, waits for them, and re-layouts  5.99 us (6%)
  other arithmetic  5.59 us (6%)
    pallas_call x9, Pallas kernels, call(): pl.pallas_call(kernel, out_shape=tuple((jax.ShapeDtypeStruct(s, f32) for...  55.2 us
    ppermute x6, waiting for transfers between devices, deal(): lax.ppermute(blocks[shift], 'bloch', [(i, (i + shift) % parts) for i in r...  15.2 us
    ppermute x6, starting transfers between devices, deal(): lax.ppermute(blocks[shift], 'bloch', [(i, (i + shift) % parts) for i in r...  13.5 us
    unnamed x18, local copies, waits for them, and re-layouts  3.64 us
  transfers between devices with their start and end apart: 11, of which 6 were waited for; matrix products, arithmetic and copies ran while one was open for 6% of the time, Pallas kernels for 44%

profile of v1, /device:TPU:0, one launch (start us, length us, event | category | flops | bytes accessed | tf_op | source)
XLA Modules:
  0.0 100.7 jit_solution(14790764759537668227)
XLA Ops:
  0.6 0.7 convert_bitcast_fusion.1
  1.3 0.7 pad_maximum_fusion
  2.0 0.5 collective-permute-start.4
  2.4 2.4 %pack.1 = (f32[192,256]{1,0:T(8,128)}, f32[192,256]{1,0:T(8,128)}, f32[192,256]{1,0:T(8,128)}, f32[192,256]{1,0:T(8,128)}) custom-call(s32[1]{0:T(128)} %bitcast.where_ref, f32[1,2,2,192,256]{4,3,2,1,0:T(8,128)} %drive_ref.1, s32[1,256]{1,0:T(1,128)} %bitcast.27), custom_call_target="tpu_custom_call" | custom-call | bytes 1573888 | tf_op jit(solution)/shard_map/pack/pallas_call | solution.py:313
  4.8 2.6 %collective-permute-start = (f32[192,256]{1,0:T(8,128)}, f32[192,256]{1,0:T(8,128)S(1)}, u32[]{:S(2)}, u32[]{:S(2)}) collective-permute-start(f32[192,256]{1,0:T(8,128)} %get-tuple-element.28), channel_id=1, source_target_pairs={{0,1},{1,2},{2,3},{3,0},{4,5},{5,6},{6,7},{7,4},{8,9},{9,10},{10,1... | collective-permute-start | bytes 589832 | tf_op jit(solution)/shard_map/ppermute | solution.py:371
  7.4 2.6 %collective-permute-start.1 = (f32[192,256]{1,0:T(8,128)}, f32[192,256]{1,0:T(8,128)S(1)}, u32[]{:S(2)}, u32[]{:S(2)}) collective-permute-start(f32[192,256]{1,0:T(8,128)} %get-tuple-element.29), channel_id=1, source_target_pairs={{0,2},{1,3},{2,0},{3,1},{4,6},{5,7},{6,4},{7,5},{8,10},{9,11},{10,... | collective-permute-start | bytes 589832 | tf_op jit(solution)/shard_map/ppermute | solution.py:371
  10.0 1.3 %collective-permute-start.2 = (f32[192,256]{1,0:T(8,128)}, f32[192,256]{1,0:T(8,128)S(1)}, u32[]{:S(2)}, u32[]{:S(2)}) collective-permute-start(f32[192,256]{1,0:T(8,128)} %get-tuple-element.30), channel_id=1, source_target_pairs={{0,3},{1,0},{2,1},{3,2},{4,7},{5,4},{6,5},{7,6},{8,11},{9,8},{10,9... | collective-permute-start | bytes 589832 | tf_op jit(solution)/shard_map/ppermute | solution.py:371
  11.3 1.4 %copy.8.refs_6_ = f32[192,1]{1,0:T(8,128)} copy(f32[192,1]{0,1:T(1,128)} %bitcast.28) | data formatting | bytes 1536 | tf_op jit(solution)/shard_map/broadcast_in_dim | solution.py:383
  12.8 0.7 add_multiply_fusion
  13.5 0.6 multiply_add_fusion.refs_0_
  14.1 0.0 collective-permute-done.4
  14.1 0.8 maximum_select_fusion
  14.9 0.6 collective-permute-done.refs_1_
  15.5 8.2 %collective-permute-done.1.refs_2_ = f32[192,256]{1,0:T(8,128)S(1)} collective-permute-done((f32[192,256]{1,0:T(8,128)}, f32[192,256]{1,0:T(8,128)S(1)}, u32[]{:S(2)}, u32[]{:S(2)}) %collective-permute-start.1) | collective-permute-done | bytes 196640 | tf_op jit(solution)/shard_map/ppermute | solution.py:371
  23.7 0.0 collective-permute-done.2.refs_3_
  23.7 0.7 copy-done.3
  24.4 0.1 copy-done.4
  24.5 2.2 %transform.1 = (f32[2,192,256]{2,1,0:T(8,128)}, f32[2,192,256]{2,1,0:T(8,128)}) custom-call(f32[2,2,4]{2,1,0:T(2,128)} %get-tuple-element.54.weight_ref, f32[192,256]{1,0:T(8,128)} %get-tuple-element.27.refs_0_, f32[192,256]{1,0:T(8,128)} %copy-done.2, f32[192,256]{1,0:T(8,128)} %copy-done.3, f32[192,256]{1,0:T(8,128)} %copy-done.4), custom_call_target="tpu_custom_call" | custom-call | bytes 1572864 | tf_op jit(solution)/shard_map/transform/pallas_call | solution.py:313
  26.7 0.5 slice_bitcast_fusion
  27.2 16.7 %matrices.1 = (f32[2,2,1,384,192]{4,3,2,1,0:T(8,128)}, f32[2,2,1,384,192]{4,3,2,1,0:T(8,128)}, f32[2,768,192]{2,1,0:T(8,128)}, f32[2,768,192]{2,1,0:T(8,128)}, f...) custom-call(f32[2]{0:T(128)} %multiply_add_fusion.refs_0_, s32[4]{0:T(128)} %get-tuple-element.53.refs_1_, ...), custom_call_target="tpu_custom_call" | custom-call | flops 1727004672 | bytes 9733632 | tf_op jit(solution)/shard_map/matrices/pallas_call | solution.py:313
  43.9 1.5 %collective-permute-start.5 = (f32[2,192,192]{2,1,0:T(8,128)}, f32[2,192,192]{2,1,0:T(8,128)S(1)}, u32[]{:S(2)}, u32[]{:S(2)}) collective-permute-start(f32[2,192,192]{2,1,0:T(8,128)} %get-tuple-element.41), channel_id=1, source_target_pairs={{0,8},{4,12},{8,0},{12,4},{1,9},{5,13},{9,1},{13,5},{2,10},{6,14},... | collective-permute-start | bytes 884744 | tf_op jit(solution)/shard_map/ppermute | solution.py:390
  45.4 0.6 add_convert_fusion.refs_0_.flag_ref
  46.0 0.0 collective-permute-done.3.got
  46.0 0.8 copy-done
  46.8 6.8 %sources.1 = (f32[2,768,64]{2,1,0:T(8,128)}, f32[2,2,192,64]{3,2,1,0:T(8,128)}) custom-call(s32[1]{0:T(128)} %bitcast.3.parity_ref, f32[2,192,256]{2,1,0:T(8,128)} %get-tuple-element.31.kept, f32[2,192,256]{2,1,0:T(8,128)} %copy-done, f32[2,2,1,384,192]{4,3,2,1,0:T(8,128)} %get-tuple-element.33.slab_d, f32[2,2,1,384,192]{4,3,2,1,0:T(8,128)} %get-tuple-element.34.slab_u, ...), custom_call_target="tpu_custom_call" | custom-call | bytes 6094848 | tf_op jit(solution)/shard_map/sources/pallas_call | solution.py:313
  53.6 1.0 %select_bitcast_fusion = f32[192,2,64]{2,0,1:T(8,128)S(1)} fusion(f32[2,2,192,64]{3,2,1,0:T(8,128)} %get-tuple-element.38.ends, pred[]{:T(512)} %eq.20), kind=kLoop, calls=%fused_computation | loop fusion | flops 24576 | bytes 294913 | tf_op jit(solution)/shard_map/transpose | solution.py:429
  54.7 0.1 copy.9
  54.8 0.6 collective-permute-start.6
  55.4 0.3 collective-permute-done.5.refs_3_.refs_4_
  55.7 0.8 copy-done.8
  56.4 14.3 %boundary.1 = (f32[2,768,192]{2,1,0:T(8,128)}, f32[2,768,192]{2,1,0:T(8,128)}, f32[2,768,192]{2,1,0:T(8,128)}, f32[2,768,192]{2,1,0:T(8,128)}) custom-call(f32[2]{0:T(128)} %add_convert_fusion.refs_0_.flag_ref, f32[2,768,192]{2,1,0:T(8,128)} %get-tuple-element.39.refs_1_, f32[2,768,192]{2,1,0:T(8,128)} %get-tuple-element.40.refs_2_, ...), custom_call_target="tpu_custom_call" | custom-call | flops 1245708288 | bytes 7667712 | tf_op jit(solution)/shard_map/boundary/pallas_call | solution.py:313
  70.7 4.5 %own.1.inner = f32[2,768,64]{2,1,0:T(8,128)} custom-call(f32[2,768,64]{2,1,0:T(8,128)} %get-tuple-element.37.inner, f32[2,2,192,64]{3,2,1,0:T(8,128)} %get-tuple-element.38.ends, f32[2,768,192]{2,1,0:T(8,128)} %get-tuple-element.42.own_d, f32[2,768,192]{2,1,0:T(8,128)} %get-tuple-element.43.own_u), custom_call_target="tpu_custom_call" | custom-call | bytes 3342336 | tf_op jit(solution)/shard_map/own/pallas_call | solution.py:313
  75.2 0.0 collective-permute-done.6
  75.2 0.8 copy.10
  76.0 4.5 %fields.1 = (f32[2,192,128]{2,1,0:T(8,128)}, f32[2,192,128]{2,1,0:T(8,128)}) custom-call(f32[2]{0:T(128)} %add_convert_fusion.refs_0_.flag_ref, s32[1]{0:T(128)} %bitcast.3.parity_ref, f32[2,768,64]{2,1,0:T(8,128)} %own.1.inner, f32[2,192,64]{2,1,0:T(8,128)} %bitcast.21, f32[2,192,64]{2,1,0:T(8,128)} %bitcast.22, f32[2,768,192]{2,1,0:T(8,128)} %get-tuple-element.44.from_d, ...), custom_call_target="tpu_custom_call" | custom-call | bytes 3342336 | tf_op jit(solution)/shard_map/fields/pallas_call | solution.py:313
  80.5 0.0 collective-permute-start.7
  80.5 1.6 %collective-permute-done.7.got = f32[2,192,128]{2,1,0:T(8,128)S(1)} collective-permute-done((f32[2,192,128]{2,1,0:T(8,128)}, f32[2,192,128]{2,1,0:T(8,128)S(1)}, u32[]{:S(2)}, u32[]{:S(2)}) %collective-permute-start.7) | collective-permute-done | bytes 196640 | tf_op jit(solution)/shard_map/ppermute | solution.py:456
  82.2 0.7 copy-done.1
  82.9 1.8 %return.1 = (f32[192,128]{1,0:T(8,128)}, f32[192,128]{1,0:T(8,128)}, f32[192,128]{1,0:T(8,128)}, f32[192,128]{1,0:T(8,128)}) custom-call(f32[2,2,4]{2,1,0:T(2,128)} %get-tuple-element.55.weight_ref, f32[2,192,128]{2,1,0:T(8,128)} %get-tuple-element.46.kept, f32[2,192,128]{2,1,0:T(8,128)} %copy-done.1), custom_call_target="tpu_custom_call" | custom-call | bytes 786432 | tf_op jit(solution)/shard_map/return/pallas_call | solution.py:313
  84.7 4.6 %collective-permute-start.8 = (f32[192,128]{1,0:T(8,128)}, f32[192,128]{1,0:T(8,128)S(1)}, u32[]{:S(2)}, u32[]{:S(2)}) collective-permute-start(f32[192,128]{1,0:T(8,128)} %get-tuple-element.49), channel_id=1, source_target_pairs={{0,1},{1,2},{2,3},{3,0},{4,5},{5,6},{6,7},{7,4},{8,9},{9,10},{10,1... | collective-permute-start | bytes 294920 | tf_op jit(solution)/shard_map/ppermute | solution.py:371
  89.3 1.7 %collective-permute-start.9 = (f32[192,128]{1,0:T(8,128)}, f32[192,128]{1,0:T(8,128)S(1)}, u32[]{:S(2)}, u32[]{:S(2)}) collective-permute-start(f32[192,128]{1,0:T(8,128)} %get-tuple-element.50), channel_id=1, source_target_pairs={{0,2},{1,3},{2,0},{3,1},{4,6},{5,7},{6,4},{7,5},{8,10},{9,11},{10,... | collective-permute-start | bytes 294920 | tf_op jit(solution)/shard_map/ppermute | solution.py:371
  91.0 0.7 collective-permute-start.10
  91.7 2.7 %collective-permute-done.8.refs_1_ = f32[192,128]{1,0:T(8,128)S(1)} collective-permute-done((f32[192,128]{1,0:T(8,128)}, f32[192,128]{1,0:T(8,128)S(1)}, u32[]{:S(2)}, u32[]{:S(2)}) %collective-permute-start.8) | collective-permute-done | bytes 98336 | tf_op jit(solution)/shard_map/ppermute | solution.py:371
  94.4 3.7 %collective-permute-done.9.refs_2_ = f32[192,128]{1,0:T(8,128)S(1)} collective-permute-done((f32[192,128]{1,0:T(8,128)}, f32[192,128]{1,0:T(8,128)S(1)}, u32[]{:S(2)}, u32[]{:S(2)}) %collective-permute-start.9) | collective-permute-done | bytes 98336 | tf_op jit(solution)/shard_map/ppermute | solution.py:371
  98.1 0.0 collective-permute-done.10.refs_3_
  98.1 0.6 copy-done.6
  98.7 0.1 copy-done.7
  98.7 2.0 %unpack.1 = (f32[1,1,192,256]{3,2,1,0:T(8,128)}, f32[1,1,192,256]{3,2,1,0:T(8,128)}) custom-call(s32[1]{0:T(128)} %bitcast.where_ref, f32[192,128]{1,0:T(8,128)} %get-tuple-element.48.refs_0_, f32[192,128]{1,0:T(8,128)} %copy-done.5, f32[192,128]{1,0:T(8,128)} %copy-done.6, f32[192,128]{1,0:T(8,128)} %copy-done.7), custom_call_target="tpu_custom_call" | custom-call | bytes 786432 | tf_op jit(solution)/shard_map/unpack/pallas_call | solution.py:313
  (16 shorter events, 0.1 us)
Async XLA Ops:
  2.0 12.1 %collective-permute-start.4 = (f32[2,2]{1,0:T(2,128)S(1)}, f32[2,2]{1,0:T(2,128)S(1)}, u32[]{:S(2)}, u32[]{:S(2)}) collective-permute-start(f32[2,2]{1,0:T(2,128)S(1)} %pad_maximum_fusion), channel_id=1, source_target_pairs={{0,4},{4,0},{8,12},{12,8},{1,5},{5,1},{9,13},{13,9},{2,6},{6,2},{1... | collective-permute-start | bytes 56 | tf_op jit(solution)/shard_map/ppermute | solution.py:358
  4.8 10.7 %collective-permute-start = (f32[192,256]{1,0:T(8,128)}, f32[192,256]{1,0:T(8,128)S(1)}, u32[]{:S(2)}, u32[]{:S(2)}) collective-permute-start(f32[192,256]{1,0:T(8,128)} %get-tuple-element.28), channel_id=1, source_target_pairs={{0,1},{1,2},{2,3},{3,0},{4,5},{5,6},{6,7},{7,4},{8,9},{9,10},{10,1... | collective-permute-start | bytes 589832 | tf_op jit(solution)/shard_map/ppermute | solution.py:371
  7.4 16.3 %collective-permute-start.1 = (f32[192,256]{1,0:T(8,128)}, f32[192,256]{1,0:T(8,128)S(1)}, u32[]{:S(2)}, u32[]{:S(2)}) collective-permute-start(f32[192,256]{1,0:T(8,128)} %get-tuple-element.29), channel_id=1, source_target_pairs={{0,2},{1,3},{2,0},{3,1},{4,6},{5,7},{6,4},{7,5},{8,10},{9,11},{10,... | collective-permute-start | bytes 589832 | tf_op jit(solution)/shard_map/ppermute | solution.py:371
  10.0 13.7 %collective-permute-start.2 = (f32[192,256]{1,0:T(8,128)}, f32[192,256]{1,0:T(8,128)S(1)}, u32[]{:S(2)}, u32[]{:S(2)}) collective-permute-start(f32[192,256]{1,0:T(8,128)} %get-tuple-element.30), channel_id=1, source_target_pairs={{0,3},{1,0},{2,1},{3,2},{4,7},{5,4},{6,5},{7,6},{8,11},{9,8},{10,9... | collective-permute-start | bytes 589832 | tf_op jit(solution)/shard_map/ppermute | solution.py:371
  15.5 8.2 %copy-start.2 = (f32[192,256]{1,0:T(8,128)}, f32[192,256]{1,0:T(8,128)S(1)}, u32[]{:S(2)}) copy-start(f32[192,256]{1,0:T(8,128)S(1)} %collective-permute-done.refs_1_) | copy-start | bytes 589828
  23.7 0.7 copy-start.3
  23.7 0.8 copy-start.4
  26.7 19.3 %collective-permute-start.3 = (f32[2,192,256]{2,1,0:T(8,128)}, f32[2,192,256]{2,1,0:T(8,128)S(1)}, u32[]{:S(2)}, u32[]{:S(2)}) collective-permute-start(f32[2,192,256]{2,1,0:T(8,128)} %get-tuple-element.32), channel_id=1, source_target_pairs={{0,4},{4,0},{8,12},{12,8},{1,5},{5,1},{9,13},{13,9},{2,6},{6,2},{1... | collective-permute-start | bytes 1179656 | tf_op jit(solution)/shard_map/ppermute | solution.py:421
  43.9 11.7 %collective-permute-start.5 = (f32[2,192,192]{2,1,0:T(8,128)}, f32[2,192,192]{2,1,0:T(8,128)S(1)}, u32[]{:S(2)}, u32[]{:S(2)}) collective-permute-start(f32[2,192,192]{2,1,0:T(8,128)} %get-tuple-element.41), channel_id=1, source_target_pairs={{0,8},{4,12},{8,0},{12,4},{1,9},{5,13},{9,1},{13,5},{2,10},{6,14},... | collective-permute-start | bytes 884744 | tf_op jit(solution)/shard_map/ppermute | solution.py:390
  46.0 0.8 copy-start
  54.8 20.4 %collective-permute-start.6 = (f32[192,128]{0,1:T(8,128)S(1)}, f32[192,128]{0,1:T(8,128)S(1)}, u32[]{:S(2)}, u32[]{:S(2)}) collective-permute-start(f32[192,128]{0,1:T(8,128)S(1)} %bitcast.23), channel_id=1, source_target_pairs={{0,8},{4,12},{8,0},{12,4},{1,9},{5,13},{9,1},{13,5},{2,10},{6,14},... | collective-permute-start | bytes 294920 | tf_op jit(solution)/shard_map/ppermute | solution.py:430
  55.7 0.8 copy-start.8
  80.5 1.7 %collective-permute-start.7 = (f32[2,192,128]{2,1,0:T(8,128)}, f32[2,192,128]{2,1,0:T(8,128)S(1)}, u32[]{:S(2)}, u32[]{:S(2)}) collective-permute-start(f32[2,192,128]{2,1,0:T(8,128)} %get-tuple-element.47), channel_id=1, source_target_pairs={{0,4},{4,0},{8,12},{12,8},{1,5},{5,1},{9,13},{13,9},{2,6},{6,2},{1... | collective-permute-start | bytes 589832 | tf_op jit(solution)/shard_map/ppermute | solution.py:456
  82.2 0.7 copy-start.1
  84.7 9.7 %collective-permute-start.8 = (f32[192,128]{1,0:T(8,128)}, f32[192,128]{1,0:T(8,128)S(1)}, u32[]{:S(2)}, u32[]{:S(2)}) collective-permute-start(f32[192,128]{1,0:T(8,128)} %get-tuple-element.49), channel_id=1, source_target_pairs={{0,1},{1,2},{2,3},{3,0},{4,5},{5,6},{6,7},{7,4},{8,9},{9,10},{10,1... | collective-permute-start | bytes 294920 | tf_op jit(solution)/shard_map/ppermute | solution.py:371
  89.3 8.7 %collective-permute-start.9 = (f32[192,128]{1,0:T(8,128)}, f32[192,128]{1,0:T(8,128)S(1)}, u32[]{:S(2)}, u32[]{:S(2)}) collective-permute-start(f32[192,128]{1,0:T(8,128)} %get-tuple-element.50), channel_id=1, source_target_pairs={{0,2},{1,3},{2,0},{3,1},{4,6},{5,7},{6,4},{7,5},{8,10},{9,11},{10,... | collective-permute-start | bytes 294920 | tf_op jit(solution)/shard_map/ppermute | solution.py:371
  91.0 7.1 %collective-permute-start.10 = (f32[192,128]{1,0:T(8,128)}, f32[192,128]{1,0:T(8,128)S(1)}, u32[]{:S(2)}, u32[]{:S(2)}) collective-permute-start(f32[192,128]{1,0:T(8,128)} %get-tuple-element.51), channel_id=1, source_target_pairs={{0,3},{1,0},{2,1},{3,2},{4,7},{5,4},{6,5},{7,6},{8,11},{9,8},{10,9... | collective-permute-start | bytes 294920 | tf_op jit(solution)/shard_map/ppermute | solution.py:371
  94.4 3.7 %copy-start.5 = (f32[192,128]{1,0:T(8,128)}, f32[192,128]{1,0:T(8,128)S(1)}, u32[]{:S(2)}) copy-start(f32[192,128]{1,0:T(8,128)S(1)} %collective-permute-done.8.refs_1_) | copy-start | bytes 294916
  98.1 0.6 copy-start.6
  98.1 0.7 copy-start.7

commit v2 on v1

v2 whole, which is shorter than its diff:
```python
import functools
import math

import jax
import jax.numpy as jnp
import numpy as np
from jax import lax
from jax.experimental import pallas as pl
from jax.experimental.pallas import tpu as pltpu
from jax.sharding import PartitionSpec as P

PAIR = 2
NEGLIGIBLE = 4e-6

f32 = jnp.float32


def dot(left_side, right_side, precision=lax.Precision.HIGH):
    return lax.dot_general(
        left_side,
        right_side,
        (((1,), (0,)), ((), ())),
        precision=precision,
        preferred_element_type=f32,
    )


def eye(size):
    rows = lax.broadcasted_iota(jnp.int32, (size, size), 0)
    columns = lax.broadcasted_iota(jnp.int32, (size, size), 1)
    return (rows == columns).astype(f32)


def inverses(couplings, doublings, sum_ref, power_ref, coupling_ref):
    size = couplings[0].shape[0]
    count = len(couplings)
    identity = eye(size)
    sums = [identity + c for c in couplings]
    powers = [dot(c, c) for c in couplings]
    for turn in range(doublings):
        sums = [s + dot(s, p) for s, p in zip(sums, powers)]
        if turn < doublings - 1:
            powers = [dot(p, p) for p in powers]
    largest = functools.reduce(jnp.maximum, [jnp.sum(p * p, axis=0, keepdims=True) for p in powers])
    for i, (s, p, c) in enumerate(zip(sums, powers, couplings)):
        sum_ref[i] = s
        power_ref[i] = p
        coupling_ref[i] = c

    @pl.when(jnp.logical_not(jnp.sum(largest) <= NEGLIGIBLE))
    def _():
        exact = lax.Precision.HIGHEST

        def one(i, carry):
            def going(state):
                step, left_over = state
                return (step < 16) & (left_over > NEGLIGIBLE) & (left_over < 1e12)

            def double(state):
                step, _ = state
                power = dot(power_ref[i], power_ref[i], exact)
                power_ref[i] = power
                sum_ref[i] = sum_ref[i] + dot(sum_ref[i], power, exact)
                return (step + 1, jnp.sum(power * power))

            start = power_ref[i]
            _, left_over = lax.while_loop(going, double, (jnp.int32(0), jnp.sum(start * start)))

            @pl.when(jnp.logical_not(left_over <= NEGLIGIBLE))
            def _():
                system = eye(size) - coupling_ref[i]
                flipped = lax.dot_general(
                    system,
                    eye(size),
                    (((0,), (0,)), ((), ())),
                    precision=exact,
                    preferred_element_type=f32,
                )
                row_bound = jnp.max(jnp.sum(jnp.abs(system), axis=1, keepdims=True))
                column_bound = jnp.max(jnp.sum(jnp.abs(system), axis=0, keepdims=True))
                sum_ref[i] = flipped / (row_bound * column_bound)

                def refining(state):
                    step, gap = state
                    return (step < 100) & (gap > 1e-4)

                def refine(state):
                    step, _ = state
                    error = eye(size) - dot(eye(size) - coupling_ref[i], sum_ref[i], exact)
                    sum_ref[i] = sum_ref[i] + dot(sum_ref[i], error, exact)
                    return (step + 1, jnp.max(jnp.abs(error)))

                lax.while_loop(refining, refine, (jnp.int32(0), f32(1.0)))

            return carry

        lax.fori_loop(0, count, one, 0)

    return [sum_ref[i] for i in range(count)]


def inner_maps(above, below, gap):
    _, _, up_a, bottom_a = above
    top_b, down_b, _, _ = below
    identity = eye(gap.shape[0])
    mid_y_d = dot(top_b, gap)
    mid_x_u = dot(gap, bottom_a)
    mid_y_u = identity + dot(top_b, mid_x_u)
    return (
        (dot(up_a, mid_y_d), gap, mid_y_d, dot(down_b, gap)),
        (dot(up_a, mid_y_u), mid_x_u, mid_y_u, dot(down_b, mid_x_u)),
    )


def in_batches(count, work):
    size = 2 if count % 2 == 0 else 1
    if count == size:
        work(0, size)
    else:
        def step(i, carry):
            work(i * size, size)
            return carry

        lax.fori_loop(0, count // size, step, 0)


def segment(factor, thick, kind, table_ref, decay_ref):
    m = table_ref.shape[-1]
    row = jnp.exp(-(thick * factor) * decay_ref[...])
    column = jnp.sum(eye(m) * row, axis=1, keepdims=True)
    return tuple(column * table_ref[kind, b] * row for b in range(4))


def matrices_kernel(layers, vectors, edge, *refs):
    in_batches(vectors, lambda start, size: matrices_of(layers, start, size, edge, *refs))


def matrices_of(layers, start, size, edge, ids_ref, factor_ref, kind_ref, thick_ref, other_ref, table_ref, decay_ref, *refs):
    slab_d, slab_u, pair_d, pair_u, *ends, sum_ref, power_ref, coupling_ref = refs
    m = table_ref.shape[-1]
    parity, group = ids_ref[1], ids_ref[2]
    keys = [(k, j) for k in range(size) for j in range(PAIR)]
    segments = {}
    for k, j in keys:
        factor = factor_ref[(start + k) * PAIR + parity]
        for i in range(layers):
            kind = jnp.where(parity == j, kind_ref[i], other_ref[0, i].astype(jnp.int32))
            thick = jnp.where(parity == j, thick_ref[i], other_ref[1, i])
            segments[k, j, i] = segment(factor, thick, kind, table_ref, decay_ref)
    slabs = {(k, j): segments[k, j, 0] for k, j in keys}
    for i in range(1, layers):
        couplings = [dot(slabs[k, j][3], segments[k, j, i][0]) for k, j in keys]
        gaps = inverses(couplings, 2, sum_ref, power_ref, coupling_ref)
        for (k, j), gap in zip(keys, gaps):
            above, below = slabs[k, j], segments[k, j, i]
            by_d, by_u = inner_maps(above, below, gap)
            slab_d[start + k, j, i - 1, 0:m] = by_d[0]
            slab_d[start + k, j, i - 1, m:] = by_d[3]
            slab_u[start + k, j, i - 1, 0:m] = by_u[0]
            slab_u[start + k, j, i - 1, m:] = by_u[3]
            slabs[k, j] = (
                above[0] + dot(by_d[0], above[1]),
                dot(by_d[3], above[1]),
                dot(by_u[0], below[2]),
                below[3] + dot(by_u[3], below[2]),
            )
    couplings = [dot(slabs[k, 0][3], slabs[k, 1][0]) for k in range(size)]
    gaps = inverses(couplings, 2, sum_ref, power_ref, coupling_ref)
    for k, gap in enumerate(gaps):
        above, below = slabs[k, 0], slabs[k, 1]
        by_d, by_u = inner_maps(above, below, gap)
        k = start + k
        for r in range(4):
            pair_d[k, r * m:(r + 1) * m] = by_d[r]
            pair_u[k, r * m:(r + 1) * m] = by_u[r]
        if edge:
            answer, onward = ends
            top = group == 0
            inward = jnp.where(top, below[2], above[1])
            rows = [dot(jnp.where(top, u, d), inward) for d, u in zip(by_d, by_u)]
            rows[0] = rows[0] + jnp.where(top, 0.0, above[0])
            rows[3] = rows[3] + jnp.where(top, below[3], 0.0)
            for r in range(4):
                answer[k, r * m:(r + 1) * m] = rows[r]
            onward[k] = jnp.where(top, rows[3], rows[0])
        else:
            end_x, end_y = ends
            for r in range(4):
                from_x, from_y = dot(by_d[r], above[1]), dot(by_u[r], below[2])
                end_x[k, r * m:(r + 1) * m] = from_x + above[0] if r == 0 else from_x
                end_y[k, r * m:(r + 1) * m] = from_y + below[3] if r == 3 else from_y


def pack_kernel(share, parts, ids_ref, kind_ref, thick_ref, drive_ref, position_ref, *outs):
    *blocks, described, held = outs
    cell = ids_ref[0]
    offset = jnp.abs(cell - position_ref[...])
    offset = jnp.minimum(offset, parts - offset)
    envelope = 1.0 / (1.0 + offset.astype(f32))
    layers = drive_ref.shape[1]
    for i in range(layers):
        described[0, i] = kind_ref[i].astype(f32)
        described[1, i] = thick_ref[i]
    for q in range(parts):
        span = slice(q * share, (q + 1) * share)
        held[q] = jnp.concatenate(
            [drive_ref[0, i, d, :, span] * envelope[:, span] for i in range(layers) for d in range(2)], axis=1
        )
    for shift in range(parts):
        blocks[shift][...] = held[lax.rem(cell + shift, parts)]


def transform_kernel(parts, ids_ref, cas_ref, *refs):
    blocks, (_, kept, sent) = refs[:parts], refs[parts:]
    place, parity = ids_ref[0], ids_ref[1]
    loaded = [b[...] for b in blocks]
    cells = [lax.rem(place - shift + parts, parts) for shift in range(parts)]
    for side, out in ((parity, kept), (1 - parity, sent)):
        for i in range(out.shape[0]):
            wave = PAIR * i + side
            total = cas_ref[wave, cells[0]] * loaded[0]
            for shift in range(1, parts):
                total = total + cas_ref[wave, cells[shift]] * loaded[shift]
            out[i] = total


def sources_kernel(layers, share, vectors, edge, ids_ref, kept, got, slab_d, slab_u, pair_d, pair_u, slabs, *refs):
    m = kept.shape[1]
    parity, group = ids_ref[1], ids_ref[2]
    held = refs[-1]
    for k in range(vectors):
        held[parity, k] = kept[k]
        held[1 - parity, k] = got[k]
    ends = []
    for k in range(vectors):
        pair = []
        for j in range(PAIR):
            block = held[j, k]
            up, down = block[:, 0:share], block[:, share:2 * share]
            for i in range(1, layers):
                at = 2 * i * share
                up_b, down_b = block[:, at:at + share], block[:, at + share:at + 2 * share]
                both = dot(slab_d[k, j, i - 1], down) + dot(slab_u[k, j, i - 1], up_b)
                up, down = up + both[0:m], down_b + both[m:]
            slabs[k, 2 * j] = up
            slabs[k, 2 * j + 1] = down
            pair.append((up, down))
        if edge:
            rows = pl.ds(pl.multiple_of(jnp.where(group == 0, 3 * m, 0), 8), m)
            own = jnp.where(group == 0, pair[1][1], pair[0][0])
            ends.append(own + dot(pair_d[k, rows], pair[0][1]) + dot(pair_u[k, rows], pair[1][0]))
    if edge:
        refs[0][...] = jnp.concatenate(ends, axis=1)


def inner_kernel(vectors, slabs, pair_d, pair_u, inner):
    m = pair_d.shape[-1]
    for k in range(vectors):
        rows = dot(pair_d[k], slabs[k, 1]) + dot(pair_u[k], slabs[k, 2])
        inner[k, 0:m] = rows[0:m] + slabs[k, 0]
        inner[k, m:3 * m] = rows[m:3 * m]
        inner[k, 3 * m:] = rows[3 * m:] + slabs[k, 3]


def boundary_kernel(vectors, slabs, end, pair_d, pair_u, onward, arrived, inner, gap, bounced, sum_ref, power_ref, coupling_ref):
    share = slabs.shape[-1]
    inner_kernel(vectors, slabs, pair_d, pair_u, inner)
    bounced[...] = jnp.concatenate(
        [dot(arrived[k], end[:, k * share:(k + 1) * share]) for k in range(vectors)], axis=1
    )
    gaps = inverses([dot(arrived[k], onward[k]) for k in range(vectors)], 3, sum_ref, power_ref, coupling_ref)
    for k in range(vectors):
        gap[k] = gaps[k]


def fields_kernel(vectors, ids_ref, inner, answer, gap, bounced, crossed, kept, sent, held):
    m = inner.shape[1] // 4
    share = inner.shape[2]
    parity = ids_ref[1]
    inward = bounced[...] + crossed[...]
    for k in range(vectors):
        rows = inner[k] + dot(answer[k], dot(gap[k], inward[:, k * share:(k + 1) * share]))
        for j in range(PAIR):
            held[j, k] = jnp.concatenate([rows[2 * j * m:(2 * j + 1) * m], rows[(2 * j + 1) * m:(2 * j + 2) * m]], axis=1)
    for k in range(vectors):
        kept[k] = held[parity, k]
        sent[k] = held[1 - parity, k]


def return_kernel(parts, ids_ref, cas_ref, kept, got, *blocks):
    place, parity = ids_ref[0], ids_ref[1]
    vectors = kept.shape[0]
    mine, theirs = [kept[i] for i in range(vectors)], [got[i] for i in range(vectors)]
    for shift in range(parts):
        cell = lax.rem(place + shift, parts)
        total = None
        for side, fields in ((parity, mine), (1 - parity, theirs)):
            for i in range(vectors):
                term = cas_ref[cell, PAIR * i + side] * fields[i]
                total = term if total is None else total + term
        blocks[shift][...] = total


def unpack_kernel(share, parts, ids_ref, *refs):
    blocks, (up, down, held) = refs[:parts], refs[parts:]
    place = ids_ref[0]
    for shift in range(parts):
        held[lax.rem(place - shift + parts, parts)] = blocks[shift][...]
    for side, out in enumerate((up, down)):
        span = slice(side * share, (side + 1) * share)
        out[0, 0] = jnp.concatenate([held[q][:, span] for q in range(parts)], axis=1)


def vmem():
    return pl.BlockSpec(memory_space=pltpu.VMEM)


def smem():
    return pl.BlockSpec(memory_space=pltpu.SMEM)


def call(kernel, scalars, arrays, shapes, scratch=(), name=None, flops=0, limit=12, after=(), small=()):
    moved = sum(a.size * 4 for a in arrays) + sum(math.prod(s) * 4 for s in shapes)
    return pl.pallas_call(
        kernel,
        out_shape=tuple(jax.ShapeDtypeStruct(s, f32) for s in (*shapes, *small)),
        in_specs=[smem()] * len(scalars) + [vmem()] * len(arrays) + [pl.BlockSpec(memory_space=pl.ANY)] * len(after),
        out_specs=tuple([vmem()] * len(shapes) + [smem()] * len(small)),
        scratch_shapes=[pltpu.VMEM(s, f32) for s in scratch],
        cost_estimate=pl.CostEstimate(flops=flops, bytes_accessed=moved, transcendentals=0),
        compiler_params=pltpu.CompilerParams(vmem_limit_bytes=limit << 20),
        name=name,
    )(*scalars, *arrays, *after)


def exact(left_side, right_side):
    return jnp.einsum("kij,kjl->kil", left_side, right_side, precision=lax.Precision.HIGHEST)


def plain_inverse(coupling):
    identity = jnp.eye(coupling.shape[-1], dtype=f32)

    def step(_, approx):
        return exact(approx, 2.0 * identity - exact(identity - coupling, approx))

    return lax.fori_loop(0, 6, step, identity + coupling)


def chain(groups, group, depth, end_x, end_y, slabs, inner):
    m = end_x.shape[-1]
    down_route = [(i, i + PAIR) for i in range(depth - PAIR)]
    up_route = [(i + PAIR, i) for i in range(depth - PAIR)]
    top_t, down_t = end_x[:, 0:m], end_x[:, 3 * m:]
    up_t, end_t = end_y[:, 0:m], end_y[:, 3 * m:]
    top_s, end_s = inner[:, 0:m], inner[:, 3 * m:]

    def turn_of(turn, carry):
        prefix, suffix, falling, rising = carry
        from_above = [lax.ppermute(f, "stack", down_route) for f in falling]
        from_below = [lax.ppermute(r, "stack", up_route) for r in rising]
        prefix = [jnp.where(group == turn, new, old) for new, old in zip(from_above, prefix)]
        suffix = [jnp.where(group == groups - 1 - turn, new, old) for new, old in zip(from_below, suffix)]
        carry_d = exact(down_t, plain_inverse(exact(prefix[0], top_t)))
        carry_u = exact(up_t, plain_inverse(exact(suffix[0], end_t)))
        grown_d = [end_t + exact(carry_d, exact(prefix[0], up_t)), end_s + exact(carry_d, prefix[1] + exact(prefix[0], top_s))]
        grown_u = [top_t + exact(carry_u, exact(suffix[0], down_t)), top_s + exact(carry_u, suffix[1] + exact(suffix[0], end_s))]
        falling = [jnp.where(group == turn, new, old) for new, old in zip(grown_d, falling)]
        rising = [jnp.where(group == groups - 1 - turn, new, old) for new, old in zip(grown_u, rising)]
        return prefix, suffix, falling, rising

    nothing = [jnp.zeros_like(end_t), jnp.zeros_like(end_s)]
    prefix, suffix, _, _ = lax.fori_loop(1, groups, turn_of, (nothing, nothing, [end_t, end_s], [top_t, top_s]))
    lower = plain_inverse(exact(suffix[0], end_t))
    below = suffix[1] + exact(suffix[0], end_s)
    top_all = top_t + exact(up_t, exact(lower, exact(suffix[0], down_t)))
    source_all = top_s + exact(up_t, exact(lower, below))
    in_x = exact(plain_inverse(exact(prefix[0], top_all)), prefix[1] + exact(prefix[0], source_all))
    in_y = exact(lower, below + exact(suffix[0], exact(down_t, in_x)))
    return inner + exact(end_x, in_x) + exact(end_y, in_y)


def shards(drive, positions, materials, table, thickness, decay):
    parts = lax.axis_size("bloch")
    depth = lax.axis_size("stack")
    groups = depth // PAIR
    edge = groups == 2
    layers, m, columns = drive.shape[1], drive.shape[3], drive.shape[4]
    vectors = parts // PAIR
    share = columns // parts
    width = layers * 2 * share
    assert drive.shape[0] == 1 and depth % PAIR == 0 and parts % PAIR == 0 and columns % parts == 0
    stack_index = lax.axis_index("stack")
    group, parity = stack_index // PAIR, stack_index % PAIR
    ids = jnp.stack([lax.axis_index("bloch"), parity, group]).astype(jnp.int32)
    partner = [(i, i ^ 1) for i in range(depth)]
    across = [(i, i + PAIR) for i in range(depth - PAIR)] + [(i + PAIR, i) for i in range(depth - PAIR)]
    counts = np.arange(parts)
    angles = np.outer(counts, counts) % parts * (2.0 * math.pi / parts)
    cas = jnp.asarray((np.cos(angles) + np.sin(angles)) / math.sqrt(parts), f32)
    factors = jnp.asarray(1.0 + 0.5 * np.cos(counts * (2.0 * math.pi / parts)), f32)

    def deal(blocks):
        out = [blocks[0]]
        for shift in range(1, parts):
            out.append(lax.ppermute(blocks[shift], "bloch", [(i, (i + shift) % parts) for i in range(parts)]))
        return out

    *packed, described = call(
        functools.partial(pack_kernel, share, parts),
        [ids, materials, thickness], [drive, positions[None, :]],
        [(m, width)] * parts, [(parts, m, width)], "pack", small=[(2, layers)],
    )
    other = lax.ppermute(described, "stack", partner)
    arrived = deal(packed)

    squares = [(vectors * PAIR, m, m)] * 3
    end_shapes = [(vectors, 4 * m, m), (vectors, m, m)] if edge else [(vectors, 4 * m, m)] * 2
    slab_d, slab_u, pair_d, pair_u, *ends = call(
        functools.partial(matrices_kernel, layers, vectors, edge),
        [ids, factors, materials, thickness, other],
        [table, decay[None, :]],
        [(vectors, PAIR, layers - 1, 2 * m, m)] * 2 + [(vectors, 4 * m, m)] * 2 + end_shapes,
        squares, "matrices", 3000 * m**3, 32,
    )
    if edge:
        opposite = lax.ppermute(ends[1], "stack", across)

    kept, sent = call(
        functools.partial(transform_kernel, parts),
        [ids, cas], arrived, [(vectors, m, width)] * 2, (), "transform", after=[slab_d],
    )
    got = lax.ppermute(sent, "stack", partner)
    slabs, *end = call(
        functools.partial(sources_kernel, layers, share, vectors, edge),
        [ids], [kept, got, slab_d, slab_u, pair_d, pair_u],
        [(vectors, 4, m, share)] + ([(m, vectors * share)] if edge else []),
        [(PAIR, vectors, m, width)], "sources",
    )
    if edge:
        crossed = lax.ppermute(end[0], "stack", across)
        inner, gap, bounced = call(
            functools.partial(boundary_kernel, vectors),
            [], [slabs, end[0], pair_d, pair_u, ends[1], opposite],
            [(vectors, 4 * m, share), (vectors, m, m), (m, vectors * share)], squares, "boundary", 1000 * m**3,
        )
        kept, sent = call(
            functools.partial(fields_kernel, vectors),
            [ids], [inner, ends[0], gap, bounced, crossed],
            [(vectors, m, 2 * share)] * 2, [(PAIR, vectors, m, 2 * share)], "fields",
        )
    else:
        (inner,) = call(
            functools.partial(inner_kernel, vectors), [], [slabs, pair_d, pair_u], [(vectors, 4 * m, share)], (), "inner",
        )
        rows = chain(groups, group, depth, ends[0], ends[1], slabs, inner)
        sides = [jnp.concatenate([rows[:, 2 * j * m:(2 * j + 1) * m], rows[:, (2 * j + 1) * m:(2 * j + 2) * m]], 2) for j in range(PAIR)]
        kept = jnp.where(parity == 0, sides[0], sides[1])
        sent = jnp.where(parity == 0, sides[1], sides[0])
    got = lax.ppermute(sent, "stack", partner)

    blocks = call(
        functools.partial(return_kernel, parts), [ids, cas], [kept, got], [(m, 2 * share)] * parts, (), "return",
    )
    blocks = deal(blocks)
    return call(
        functools.partial(unpack_kernel, share, parts),
        [ids], blocks, [(1, 1, m, columns)] * 2, [(parts, m, 2 * share)], "unpack",
    )


def solution(mesh):
    in_specs = (
        P(("groups", "bloch"), "stack", None, None, None),
        P("groups"),
        P(("groups", "stack")),
        P(),
        P(("groups", "stack")),
        P(),
    )
    out_specs = (
        P(("groups", "bloch"), "stack", None, None),
        P(("groups", "bloch"), "stack", None, None),
    )
    return jax.shard_map(shards, mesh=mesh, in_specs=in_specs, out_specs=out_specs, check_vma=False)
```

time: 101 us -> 61.4 us (0.61)
  Pallas kernels: 55.2 us -> 23.8 us
  other arithmetic: 5.59 us -> 0.08 us
  waiting for transfers between devices: 17.1 us -> 14.5 us
  starting transfers between devices: 16.1 us -> 14.3 us
  local copies, waits for them, and re-layouts: 5.99 us -> 7.66 us
    pallas_call x9 -> x8, Pallas kernels: 55.2 us -> 23.8 us  [call(): pl.pallas_call(kernel, out_shape=tuple((jax.ShapeDtypeStruct(s, f32) for...]
    ppermute x6, waiting for transfers between devices: 15.2 us -> 7.13 us  [deal(): lax.ppermute(blocks[shift], 'bloch', [(i, (i + shift) % parts) for i in r...]
    ppermute x2, waiting for transfers between devices: 0.3 us -> 5.84 us  [the longest x1 5.84 us: shards(): opposite = lax.ppermute(ends[1], 'stack', across)]
    unnamed x18 -> x20, local copies, waits for them, and re-layouts: 3.64 us -> 7.66 us
    ppermute x6, starting transfers between devices: 13.5 us -> 10.4 us  [deal(): lax.ppermute(blocks[shift], 'bloch', [(i, (i + shift) % parts) for i in r...]
    broadcast_in_dim x1 -> x0, local copies, waits for them, and re-layouts: 1.44 us -> none  [shards(): decay[:, None]]
    another operation x3 -> x1, other arithmetic: 1.33 us -> 0.08 us  [shards(): ids = jnp.stack([lax.axis_index('bloch'), parity, group]).astype(jnp.int32)]
    ppermute x2, starting transfers between devices: 2.09 us -> 3.17 us  [the longest x1 1.59 us: shards(): opposite = lax.ppermute(ends[1], 'stack', across)]
  transfers between devices with their start and end apart: 11 -> 11, of which waited for: 6 -> 5; matrix products, arithmetic and copies ran while one was open for 6% -> 0% of each run, Pallas kernels for 44% -> 29%
where the time goes in v2:
time: 61.4 us; the launch traced here: 61.1 us
  Pallas kernels  23.8 us (39%)
  waiting for transfers between devices  14.5 us (24%)
  starting transfers between devices  14.3 us (23%)
  local copies, waits for them, and re-layouts  7.66 us (12%)
  between operations  0.78 us (1%)
    pallas_call x8, Pallas kernels, call(): pl.pallas_call(kernel, out_shape=tuple((jax.ShapeDtypeStruct(s, f32) for...  23.8 us
    ppermute x6, starting transfers between devices, deal(): lax.ppermute(blocks[shift], 'bloch', [(i, (i + shift) % parts) for i in r...  10.4 us
    unnamed x20, local copies, waits for them, and re-layouts  7.66 us
    ppermute x6, waiting for transfers between devices, deal(): lax.ppermute(blocks[shift], 'bloch', [(i, (i + shift) % parts) for i in r...  7.13 us
    ppermute x1, waiting for transfers between devices, shards(): opposite = lax.ppermute(ends[1], 'stack', across)  5.84 us
    ppermute x1, starting transfers between devices, shards(): opposite = lax.ppermute(ends[1], 'stack', across)  1.59 us
    ppermute x1, starting transfers between devices, shards(): crossed = lax.ppermute(end[0], 'stack', across)  1.59 us
    ppermute x2, waiting for transfers between devices, shards(): got = lax.ppermute(sent, 'stack', partner)  1.55 us
  transfers between devices with their start and end apart: 11, of which 5 were waited for; matrix products, arithmetic and copies ran while one was open for 0% of the time, Pallas kernels for 29%

profile of v2, /device:TPU:0, one launch (start us, length us, event | category | flops | bytes accessed | tf_op | source)
XLA Modules:
  0.0 61.1 jit_solution(5116134081072116179)
XLA Ops:
  0.6 0.1 pad_add_fusion.ids_ref.refs_0_
  0.7 0.0 copy-start
  0.7 1.1 %copy-done = f32[1,2,2,192,256]{4,3,2,1,0:T(8,128)S(1)} copy-done((f32[1,2,2,192,256]{4,3,2,1,0:T(8,128)S(1)}, f32[1,2,2,192,256]{4,3,2,1,0:T(8,128)}, u32[]{:S(2)}) %copy-start) | copy-done | bytes 786456
  1.9 0.0 copy-start.2
  1.9 0.7 %copy-done.2 = s32[256]{0:T(256)S(1)} copy-done((s32[256]{0:T(256)S(1)}, s32[256]{0:T(256)}, u32[]{:S(2)}) %copy-start.2) | copy-done | bytes 1048
  2.5 0.0 copy-start.3
  2.5 0.7 %copy-done.3 = s32[2]{0:T(128)S(1)} copy-done((s32[2]{0:T(128)S(1)}, s32[2]{0:T(128)}, u32[]{:S(2)}) %copy-start.3) | copy-done | bytes 32
  3.2 0.0 copy-start.5
  3.2 0.7 %copy-done.5 = f32[2]{0:T(128)S(1)} copy-done((f32[2]{0:T(128)S(1)}, f32[2]{0:T(128)}, u32[]{:S(2)}) %copy-start.5) | copy-done | bytes 32
  3.9 1.4 %pack.1 = (f32[192,256]{1,0:T(8,128)S(1)}, f32[192,256]{1,0:T(8,128)S(1)}, f32[192,256]{1,0:T(8,128)S(1)}, f32[192,256]{1,0:T(8,128)S(1)}, f32[2,2]{1,0:T(2,128)S(1)}) custom-call(s32[3]{0:T(128)S(1)} %pad_add_fusion.ids_ref.refs_0_, s32[2]{0:T(128)S(1)} %copy-done.3, f32[2]{0:T(128)S(1)} %copy-done.5, f32[1,2,2,192,256]{4,3,2,1,0:T(8,128)S(1)} %copy-done, ...), custom_call_target="tpu_custom_call" | custom-call | bytes 1573888 | tf_op jit(solution)/shard_map/pack/pallas_call | solution.py:324
  5.2 0.6 collective-permute-start.3
  5.8 2.6 %collective-permute-start = (f32[192,256]{1,0:T(8,128)S(1)}, f32[192,256]{1,0:T(8,128)S(1)}, u32[]{:S(2)}, u32[]{:S(2)}) collective-permute-start(f32[192,256]{1,0:T(8,128)S(1)} %get-tuple-element.27), channel_id=1, source_target_pairs={{0,1},{1,2},{2,3},{3,0},{4,5},{5,6},{6,7},{7,4},{8,9},{9,10},{10,1... | collective-permute-start | bytes 589832 | tf_op jit(solution)/shard_map/ppermute | solution.py:405
  8.4 2.6 %collective-permute-start.1 = (f32[192,256]{1,0:T(8,128)S(1)}, f32[192,256]{1,0:T(8,128)S(1)}, u32[]{:S(2)}, u32[]{:S(2)}) collective-permute-start(f32[192,256]{1,0:T(8,128)S(1)} %get-tuple-element.28), channel_id=1, source_target_pairs={{0,2},{1,3},{2,0},{3,1},{4,6},{5,7},{6,4},{7,5},{8,10},{9,11},{10,... | collective-permute-start | bytes 589832 | tf_op jit(solution)/shard_map/ppermute | solution.py:405
  11.0 1.3 %collective-permute-start.2 = (f32[192,256]{1,0:T(8,128)S(1)}, f32[192,256]{1,0:T(8,128)S(1)}, u32[]{:S(2)}, u32[]{:S(2)}) collective-permute-start(f32[192,256]{1,0:T(8,128)S(1)} %get-tuple-element.29), channel_id=1, source_target_pairs={{0,3},{1,0},{2,1},{3,2},{4,7},{5,4},{6,5},{7,6},{8,11},{9,8},{10,9... | collective-permute-start | bytes 589832 | tf_op jit(solution)/shard_map/ppermute | solution.py:405
  12.4 0.0 collective-permute-done.3.refs_4_
  12.4 0.7 %copy-done.4 = s32[2]{0:T(128)S(1)} copy-done((s32[2]{0:T(128)S(1)}, s32[2]{0:T(128)}, u32[]{:S(2)}) %copy-start.4) | copy-done | bytes 32
  13.0 0.0 copy-start.6
  13.0 0.7 %copy-done.6 = f32[2]{0:T(128)S(1)} copy-done((f32[2]{0:T(128)S(1)}, f32[2]{0:T(128)}, u32[]{:S(2)}) %copy-start.6) | copy-done | bytes 32
  13.7 0.0 copy-start.7
  13.7 1.9 %copy-done.7 = f32[4,4,192,192]{3,2,1,0:T(8,128)S(1)} copy-done((f32[4,4,192,192]{3,2,1,0:T(8,128)S(1)}, f32[4,4,192,192]{3,2,1,0:T(8,128)}, u32[]{:S(2)}) %copy-start.7) | copy-done | bytes 2359320
  15.6 0.0 copy-start.8
  15.6 0.7 %copy-done.8 = f32[192]{0:T(256)S(1)} copy-done((f32[192]{0:T(256)S(1)}, f32[192]{0:T(256)}, u32[]{:S(2)}) %copy-start.8) | copy-done | bytes 792
  16.2 0.7 %copy-done.9 = f32[4]{0:T(128)S(1)} copy-done((f32[4]{0:T(128)S(1)}, f32[4]{0:T(128)}, u32[]{:S(2)}) %copy-start.9) | copy-done | bytes 40
  16.9 11.2 %matrices.1 = (f32[2,2,1,384,192]{4,3,2,1,0:T(8,128)S(1)}, f32[2,2,1,384,192]{4,3,2,1,0:T(8,128)S(1)}, f32[2,768,192]{2,1,0:T(8,128)S(1)}, f32[2,768,192]{2,1,0:...) custom-call(s32[3]{0:T(128)S(1)} %pad_add_fusion.ids_ref.refs_0_, f32[4]{0:T(128)S(1)} %copy-done.9, ...), custom_call_target="tpu_custom_call" | custom-call | flops 21233664000 | bytes 8553216 | tf_op jit(solution)/shard_map/matrices/pallas_call | solution.py:324
  28.1 0.0 collective-permute-done.refs_1_
  28.1 0.0 collective-permute-done.1.refs_2_
  28.1 0.0 collective-permute-done.2.refs_3_
  28.1 0.0 copy-done.1
  28.1 0.8 %transform.1 = (f32[2,192,256]{2,1,0:T(8,128)S(1)}, f32[2,192,256]{2,1,0:T(8,128)S(1)}) custom-call(s32[3]{0:T(128)S(1)} %pad_add_fusion.ids_ref.refs_0_, f32[4,4]{1,0:T(4,128)S(1)} %copy-done.1, f32[192,256]{1,0:T(8,128)S(1)} %get-tuple-element.26.refs_0_, f32[192,256]{1,0:T(8,128)S(1)} %collective-permute-done.refs_1_, ...), custom_call_target="tpu_custom_call" | custom-call | bytes 1572864 | tf_op jit(solution)/shard_map/transform/pallas_call | solution.py:324
  28.9 0.1 collective-permute-start.4
  29.0 1.6 %collective-permute-start.5 = (f32[2,192,192]{2,1,0:T(8,128)S(1)}, f32[2,192,192]{2,1,0:T(8,128)S(1)}, u32[]{:S(2)}, u32[]{:S(2)}) collective-permute-start(f32[2,192,192]{2,1,0:T(8,128)S(1)} %get-tuple-element.39.onward), channel_id=1, source_target_pairs={{0,8},{4,12},{8,0},{12,4},{1,9},{5,13},{9,1},{13,5},{2,10},{6,14},... | collective-permute-start | bytes 884744 | tf_op jit(solution)/shard_map/ppermute | solution.py:426
  30.6 0.1 collective-permute-done.4.got
  30.7 2.9 %sources.1 = (f32[2,4,192,64]{3,2,1,0:T(8,128)S(1)}, f32[192,128]{1,0:T(8,128)S(1)}) custom-call(s32[3]{0:T(128)S(1)} %pad_add_fusion.ids_ref.refs_0_, f32[2,192,256]{2,1,0:T(8,128)S(1)} %get-tuple-element.32.kept, f32[2,192,256]{2,1,0:T(8,128)S(1)} %collective-permute-done.4.got, f32[2,2,1,384,192]{4,3,2,1,0:T(8,128)S(1)} %get-tuple-element.31.refs_4_.slab_d, ...), custom_call_target="tpu_custom_call" | custom-call | bytes 5996544 | tf_op jit(solution)/shard_map/sources/pallas_call | solution.py:324
  33.6 1.6 %collective-permute-start.6 = (f32[192,128]{1,0:T(8,128)S(1)}, f32[192,128]{1,0:T(8,128)S(1)}, u32[]{:S(2)}, u32[]{:S(2)}) collective-permute-start(f32[192,128]{1,0:T(8,128)S(1)} %get-tuple-element.38.end), channel_id=1, source_target_pairs={{0,8},{4,12},{8,0},{12,4},{1,9},{5,13},{9,1},{13,5},{2,10},{6,14},... | collective-permute-start | bytes 294920 | tf_op jit(solution)/shard_map/ppermute | solution.py:440
  35.2 5.8 %collective-permute-done.5.arrived = f32[2,192,192]{2,1,0:T(8,128)S(1)} collective-permute-done((f32[2,192,192]{2,1,0:T(8,128)S(1)}, f32[2,192,192]{2,1,0:T(8,128)S(1)}, u32[]{:S(2)}, u32[]{:S(2)}) %collective-permute-start.5) | collective-permute-done | bytes 294944 | tf_op jit(solution)/shard_map/ppermute | solution.py:426
  41.1 3.4 %boundary.1 = (f32[2,768,64]{2,1,0:T(8,128)S(1)}, f32[2,192,192]{2,1,0:T(8,128)S(1)}, f32[192,128]{1,0:T(8,128)S(1)}) custom-call(f32[2,4,192,64]{3,2,1,0:T(8,128)S(1)} %get-tuple-element.37.slabs, f32[192,128]{1,0:T(8,128)S(1)} %get-tuple-element.38.end, f32[2,768,192]{2,1,0:T(8,128)S(1)} %get-tuple-element.35.pair_d, ...), custom_call_target="tpu_custom_call" | custom-call | flops 7077888000 | bytes 4227072 | tf_op jit(solution)/shard_map/boundary/pallas_call | solution.py:324
  44.4 0.0 collective-permute-done.6.crossed
  44.4 2.0 %fields.1 = (f32[2,192,128]{2,1,0:T(8,128)S(1)}, f32[2,192,128]{2,1,0:T(8,128)S(1)}) custom-call(s32[3]{0:T(128)S(1)} %pad_add_fusion.ids_ref.refs_0_, f32[2,768,64]{2,1,0:T(8,128)S(1)} %get-tuple-element.40.inner, f32[2,768,192]{2,1,0:T(8,128)S(1)} %get-tuple-element.41.answer, f32[2,192,192]{2,1,0:T(8,128)S(1)} %get-tuple-element.42.gap, ...), custom_call_target="tpu_custom_call" | custom-call | bytes 2457600 | tf_op jit(solution)/shard_map/fields/pallas_call | solution.py:324
  46.5 0.1 collective-permute-start.7
  46.6 1.4 %collective-permute-done.7.got = f32[2,192,128]{2,1,0:T(8,128)S(1)} collective-permute-done((f32[2,192,128]{2,1,0:T(8,128)S(1)}, f32[2,192,128]{2,1,0:T(8,128)S(1)}, u32[]{:S(2)}, u32[]{:S(2)}) %collective-permute-start.7) | collective-permute-done | bytes 196640 | tf_op jit(solution)/shard_map/ppermute | solution.py:459
  48.0 0.7 %return.1 = (f32[192,128]{1,0:T(8,128)S(1)}, f32[192,128]{1,0:T(8,128)S(1)}, f32[192,128]{1,0:T(8,128)S(1)}, f32[192,128]{1,0:T(8,128)S(1)}) custom-call(s32[3]{0:T(128)S(1)} %pad_add_fusion.ids_ref.refs_0_, f32[4,4]{1,0:T(4,128)S(1)} %copy-done.1, f32[2,192,128]{2,1,0:T(8,128)S(1)} %get-tuple-element.44.kept, f32[2,192,128]{2,1,0:T(8,128)S(1)} %collective-permute-done.7.got), custom_call_target="tpu_custom_call" | custom-call | bytes 786432 | tf_op jit(solution)/shard_map/return/pallas_call | solution.py:324
  48.7 1.1 %collective-permute-start.8 = (f32[192,128]{1,0:T(8,128)S(1)}, f32[192,128]{1,0:T(8,128)S(1)}, u32[]{:S(2)}, u32[]{:S(2)}) collective-permute-start(f32[192,128]{1,0:T(8,128)S(1)} %get-tuple-element.47), channel_id=1, source_target_pairs={{0,1},{1,2},{2,3},{3,0},{4,5},{5,6},{6,7},{7,4},{8,9},{9,10},{10,1... | collective-permute-start | bytes 294920 | tf_op jit(solution)/shard_map/ppermute | solution.py:405
  49.8 1.6 %collective-permute-start.9 = (f32[192,128]{1,0:T(8,128)S(1)}, f32[192,128]{1,0:T(8,128)S(1)}, u32[]{:S(2)}, u32[]{:S(2)}) collective-permute-start(f32[192,128]{1,0:T(8,128)S(1)} %get-tuple-element.48), channel_id=1, source_target_pairs={{0,2},{1,3},{2,0},{3,1},{4,6},{5,7},{6,4},{7,5},{8,10},{9,11},{10,... | collective-permute-start | bytes 294920 | tf_op jit(solution)/shard_map/ppermute | solution.py:405
  51.4 1.2 %collective-permute-start.10 = (f32[192,128]{1,0:T(8,128)S(1)}, f32[192,128]{1,0:T(8,128)S(1)}, u32[]{:S(2)}, u32[]{:S(2)}) collective-permute-start(f32[192,128]{1,0:T(8,128)S(1)} %get-tuple-element.49), channel_id=1, source_target_pairs={{0,3},{1,0},{2,1},{3,2},{4,7},{5,4},{6,5},{7,6},{8,11},{9,8},{10,9... | collective-permute-start | bytes 294920 | tf_op jit(solution)/shard_map/ppermute | solution.py:405
  52.5 3.7 %collective-permute-done.8.refs_1_ = f32[192,128]{1,0:T(8,128)S(1)} collective-permute-done((f32[192,128]{1,0:T(8,128)S(1)}, f32[192,128]{1,0:T(8,128)S(1)}, u32[]{:S(2)}, u32[]{:S(2)}) %collective-permute-start.8) | collective-permute-done | bytes 98336 | tf_op jit(solution)/shard_map/ppermute | solution.py:405
  56.3 3.4 %collective-permute-done.9.refs_2_ = f32[192,128]{1,0:T(8,128)S(1)} collective-permute-done((f32[192,128]{1,0:T(8,128)S(1)}, f32[192,128]{1,0:T(8,128)S(1)}, u32[]{:S(2)}, u32[]{:S(2)}) %collective-permute-start.9) | collective-permute-done | bytes 98336 | tf_op jit(solution)/shard_map/ppermute | solution.py:405
  59.7 0.0 collective-permute-done.10.refs_3_
  59.7 1.4 %unpack.1 = (f32[1,1,192,256]{3,2,1,0:T(8,128)}, f32[1,1,192,256]{3,2,1,0:T(8,128)}) custom-call(s32[3]{0:T(128)S(1)} %pad_add_fusion.ids_ref.refs_0_, f32[192,128]{1,0:T(8,128)S(1)} %get-tuple-element.46.refs_0_, f32[192,128]{1,0:T(8,128)S(1)} %collective-permute-done.8.refs_1_, f32[192,128]{1,0:T(8,128)S(1)} %collective-permute-done.9.refs_2_, ...), custom_call_target="tpu_custom_call" | custom-call | bytes 786432 | tf_op jit(solution)/shard_map/unpack/pallas_call | solution.py:324
  (3 shorter events, 0.0 us)
Async XLA Ops:
  0.7 1.1 %copy-start = (f32[1,2,2,192,256]{4,3,2,1,0:T(8,128)S(1)}, f32[1,2,2,192,256]{4,3,2,1,0:T(8,128)}, u32[]{:S(2)}) copy-start(f32[1,2,2,192,256]{4,3,2,1,0:T(8,128)} %drive_ref.1) | copy-start | bytes 2359300
  1.9 0.7 %copy-start.2 = (s32[256]{0:T(256)S(1)}, s32[256]{0:T(256)}, u32[]{:S(2)}) copy-start(s32[256]{0:T(256)} %param.9) | copy-start | bytes 3076
  2.5 0.7 %copy-start.3 = (s32[2]{0:T(128)S(1)}, s32[2]{0:T(128)}, u32[]{:S(2)}) copy-start(s32[2]{0:T(128)} %refs_2_.1) | copy-start | bytes 28
  3.2 0.7 %copy-start.5 = (f32[2]{0:T(128)S(1)}, f32[2]{0:T(128)}, u32[]{:S(2)}) copy-start(f32[2]{0:T(128)} %refs_3_.1) | copy-start | bytes 28
  5.2 7.1 %collective-permute-start.3 = (f32[2,2]{1,0:T(2,128)S(1)}, f32[2,2]{1,0:T(2,128)S(1)}, u32[]{:S(2)}, u32[]{:S(2)}) collective-permute-start(f32[2,2]{1,0:T(2,128)S(1)} %get-tuple-element.30), channel_id=1, source_target_pairs={{0,4},{4,0},{8,12},{12,8},{1,5},{5,1},{9,13},{13,9},{2,6},{6,2},{1... | collective-permute-start | bytes 56 | tf_op jit(solution)/shard_map/ppermute | solution.py:413
  5.8 22.3 %collective-permute-start = (f32[192,256]{1,0:T(8,128)S(1)}, f32[192,256]{1,0:T(8,128)S(1)}, u32[]{:S(2)}, u32[]{:S(2)}) collective-permute-start(f32[192,256]{1,0:T(8,128)S(1)} %get-tuple-element.27), channel_id=1, source_target_pairs={{0,1},{1,2},{2,3},{3,0},{4,5},{5,6},{6,7},{7,4},{8,9},{9,10},{10,1... | collective-permute-start | bytes 589832 | tf_op jit(solution)/shard_map/ppermute | solution.py:405
  8.4 19.7 %collective-permute-start.1 = (f32[192,256]{1,0:T(8,128)S(1)}, f32[192,256]{1,0:T(8,128)S(1)}, u32[]{:S(2)}, u32[]{:S(2)}) collective-permute-start(f32[192,256]{1,0:T(8,128)S(1)} %get-tuple-element.28), channel_id=1, source_target_pairs={{0,2},{1,3},{2,0},{3,1},{4,6},{5,7},{6,4},{7,5},{8,10},{9,11},{10,... | collective-permute-start | bytes 589832 | tf_op jit(solution)/shard_map/ppermute | solution.py:405
  11.0 17.1 %collective-permute-start.2 = (f32[192,256]{1,0:T(8,128)S(1)}, f32[192,256]{1,0:T(8,128)S(1)}, u32[]{:S(2)}, u32[]{:S(2)}) collective-permute-start(f32[192,256]{1,0:T(8,128)S(1)} %get-tuple-element.29), channel_id=1, source_target_pairs={{0,3},{1,0},{2,1},{3,2},{4,7},{5,4},{6,5},{7,6},{8,11},{9,8},{10,9... | collective-permute-start | bytes 589832 | tf_op jit(solution)/shard_map/ppermute | solution.py:405
  12.4 0.7 %copy-start.4 = (s32[2]{0:T(128)S(1)}, s32[2]{0:T(128)}, u32[]{:S(2)}) copy-start(s32[2]{0:T(128)} %refs_2_.1) | copy-start | bytes 28
  13.0 0.7 %copy-start.6 = (f32[2]{0:T(128)S(1)}, f32[2]{0:T(128)}, u32[]{:S(2)}) copy-start(f32[2]{0:T(128)} %refs_3_.1) | copy-start | bytes 28
  13.7 1.9 %copy-start.7 = (f32[4,4,192,192]{3,2,1,0:T(8,128)S(1)}, f32[4,4,192,192]{3,2,1,0:T(8,128)}, u32[]{:S(2)}) copy-start(f32[4,4,192,192]{3,2,1,0:T(8,128)} %refs_5_.1) | copy-start | bytes 7077892
  15.6 0.7 %copy-start.8 = (f32[192]{0:T(256)S(1)}, f32[192]{0:T(256)}, u32[]{:S(2)}) copy-start(f32[192]{0:T(256)} %param.13) | copy-start | bytes 2308
  16.2 0.7 %copy-start.9 = (f32[4]{0:T(128)S(1)}, f32[4]{0:T(128)}, u32[]{:S(2)}) copy-start(f32[4]{0:T(128)} %constant.36.clone.refs_1_) | copy-start | bytes 52
  16.9 11.2 %copy-start.1 = (f32[4,4]{1,0:T(4,128)S(1)}, f32[4,4]{1,0:T(4,128)}, u32[]{:S(2)}) copy-start(f32[4,4]{1,0:T(4,128)} %constant.35.clone.cas_ref) | copy-start | bytes 196
  28.9 1.8 %collective-permute-start.4 = (f32[2,192,256]{2,1,0:T(8,128)S(1)}, f32[2,192,256]{2,1,0:T(8,128)S(1)}, u32[]{:S(2)}, u32[]{:S(2)}) collective-permute-start(f32[2,192,256]{2,1,0:T(8,128)S(1)} %get-tuple-element.33), channel_id=1, source_target_pairs={{0,4},{4,0},{8,12},{12,8},{1,5},{5,1},{9,13},{13,9},{2,6},{6,2},{1... | collective-permute-start | bytes 1179656 | tf_op jit(solution)/shard_map/ppermute | solution.py:432
  29.0 12.1 %collective-permute-start.5 = (f32[2,192,192]{2,1,0:T(8,128)S(1)}, f32[2,192,192]{2,1,0:T(8,128)S(1)}, u32[]{:S(2)}, u32[]{:S(2)}) collective-permute-start(f32[2,192,192]{2,1,0:T(8,128)S(1)} %get-tuple-element.39.onward), channel_id=1, source_target_pairs={{0,8},{4,12},{8,0},{12,4},{1,9},{5,13},{9,1},{13,5},{2,10},{6,14},... | collective-permute-start | bytes 884744 | tf_op jit(solution)/shard_map/ppermute | solution.py:426
  33.6 10.8 %collective-permute-start.6 = (f32[192,128]{1,0:T(8,128)S(1)}, f32[192,128]{1,0:T(8,128)S(1)}, u32[]{:S(2)}, u32[]{:S(2)}) collective-permute-start(f32[192,128]{1,0:T(8,128)S(1)} %get-tuple-element.38.end), channel_id=1, source_target_pairs={{0,8},{4,12},{8,0},{12,4},{1,9},{5,13},{9,1},{13,5},{2,10},{6,14},... | collective-permute-start | bytes 294920 | tf_op jit(solution)/shard_map/ppermute | solution.py:440
  46.5 1.5 %collective-permute-start.7 = (f32[2,192,128]{2,1,0:T(8,128)S(1)}, f32[2,192,128]{2,1,0:T(8,128)S(1)}, u32[]{:S(2)}, u32[]{:S(2)}) collective-permute-start(f32[2,192,128]{2,1,0:T(8,128)S(1)} %get-tuple-element.45), channel_id=1, source_target_pairs={{0,4},{4,0},{8,12},{12,8},{1,5},{5,1},{9,13},{13,9},{2,6},{6,2},{1... | collective-permute-start | bytes 589832 | tf_op jit(solution)/shard_map/ppermute | solution.py:459
  48.7 7.6 %collective-permute-start.8 = (f32[192,128]{1,0:T(8,128)S(1)}, f32[192,128]{1,0:T(8,128)S(1)}, u32[]{:S(2)}, u32[]{:S(2)}) collective-permute-start(f32[192,128]{1,0:T(8,128)S(1)} %get-tuple-element.47), channel_id=1, source_target_pairs={{0,1},{1,2},{2,3},{3,0},{4,5},{5,6},{6,7},{7,4},{8,9},{9,10},{10,1... | collective-permute-start | bytes 294920 | tf_op jit(solution)/shard_map/ppermute | solution.py:405
  49.8 9.9 %collective-permute-start.9 = (f32[192,128]{1,0:T(8,128)S(1)}, f32[192,128]{1,0:T(8,128)S(1)}, u32[]{:S(2)}, u32[]{:S(2)}) collective-permute-start(f32[192,128]{1,0:T(8,128)S(1)} %get-tuple-element.48), channel_id=1, source_target_pairs={{0,2},{1,3},{2,0},{3,1},{4,6},{5,7},{6,4},{7,5},{8,10},{9,11},{10,... | collective-permute-start | bytes 294920 | tf_op jit(solution)/shard_map/ppermute | solution.py:405
  51.4 8.3 %collective-permute-start.10 = (f32[192,128]{1,0:T(8,128)S(1)}, f32[192,128]{1,0:T(8,128)S(1)}, u32[]{:S(2)}, u32[]{:S(2)}) collective-permute-start(f32[192,128]{1,0:T(8,128)S(1)} %get-tuple-element.49), channel_id=1, source_target_pairs={{0,3},{1,0},{2,1},{3,2},{4,7},{5,4},{6,5},{7,6},{8,11},{9,8},{10,9... | collective-permute-start | bytes 294920 | tf_op jit(solution)/shard_map/ppermute | solution.py:405

commit v3 on v2

--- a/solution.py
+++ b/solution.py
@@ -3,7 +3,6 @@
 
 import jax
 import jax.numpy as jnp
-import numpy as np
 from jax import lax
 from jax.experimental import pallas as pl
 from jax.experimental.pallas import tpu as pltpu
@@ -124,33 +123,68 @@
         lax.fori_loop(0, count // size, step, 0)
 
 
-def segment(factor, thick, kind, table_ref, decay_ref):
-    m = table_ref.shape[-1]
-    row = jnp.exp(-(thick * factor) * decay_ref[...])
+def pick(values, index):
+    value = f32(values[0])
+    for i in range(1, len(values)):
+        value = jnp.where(index == i, f32(values[i]), value)
+    return value
+
+
+def cas(row, column, count):
+    angles = [2.0 * math.pi * i / count for i in range(count)]
+    return pick([(math.cos(a) + math.sin(a)) / math.sqrt(count) for a in angles], lax.rem(row * column, count))
+
+
+def segment(factor, thick, blocks, decay):
+    m = decay.shape[-1]
+    row = jnp.exp(-(thick * factor) * decay)
     column = jnp.sum(eye(m) * row, axis=1, keepdims=True)
-    return tuple(column * table_ref[kind, b] * row for b in range(4))
-
-
-def matrices_kernel(layers, vectors, edge, *refs):
-    in_batches(vectors, lambda start, size: matrices_of(layers, start, size, edge, *refs))
-
-
-def matrices_of(layers, start, size, edge, ids_ref, factor_ref, kind_ref, thick_ref, other_ref, table_ref, decay_ref, *refs):
-    slab_d, slab_u, pair_d, pair_u, *ends, sum_ref, power_ref, coupling_ref = refs
-    m = table_ref.shape[-1]
-    parity, group = ids_ref[1], ids_ref[2]
+    return tuple(column * blocks[b] * row for b in range(4))
+
+
+def slabs_kernel(layers, vectors, parts, edge, ids_ref, other_ref, kind_hbm, thick_hbm, table_hbm, decay_hbm, *refs):
+    *outs, sum_ref, power_ref, coupling_ref, kind_ref, thick_ref, blocks_ref, decay_ref, sems, block_sems = refs
+    parity = ids_ref[1]
+    small = [
+        pltpu.make_async_copy(kind_hbm, kind_ref, sems.at[0]),
+        pltpu.make_async_copy(thick_hbm, thick_ref, sems.at[1]),
+        pltpu.make_async_copy(decay_hbm, decay_ref, sems.at[2]),
+    ]
+    for copy in small:
+        copy.start()
+    small[0].wait()
+    large = {}
+    for i in range(layers):
+        for j in range(PAIR):
+            kind = jnp.where(parity == j, kind_ref[i], other_ref[0, i].astype(jnp.int32))
+            large[j, i] = pltpu.make_async_copy(table_hbm.at[kind], blocks_ref.at[j, i], block_sems.at[j, i])
+            large[j, i].start()
+    for copy in small[1:]:
+        copy.wait()
+    for i in range(layers):
+        for j in range(PAIR):
+            large[j, i].wait()
+    scratch = sum_ref, power_ref, coupling_ref
+    in_batches(vectors, lambda start, size: slabs_of(
+        layers, parts, start, size, edge, ids_ref, other_ref, thick_ref, blocks_ref, decay_ref, outs, scratch))
+
+
+def slabs_of(layers, parts, start, size, edge, ids_ref, other_ref, thick_ref, blocks_ref, decay_ref, outs, scratch):
+    slab_d, slab_u, slab_ref, gap_ref, *onward = outs
+    m = decay_ref.shape[-1]
+    parity, top = ids_ref[1], ids_ref[2] == 0
     keys = [(k, j) for k in range(size) for j in range(PAIR)]
+    factors = [1.0 + 0.5 * math.cos(2.0 * math.pi * i / parts) for i in range(parts)]
     segments = {}
     for k, j in keys:
-        factor = factor_ref[(start + k) * PAIR + parity]
+        factor = pick(factors, (start + k) * PAIR + parity)
         for i in range(layers):
-            kind = jnp.where(parity == j, kind_ref[i], other_ref[0, i].astype(jnp.int32))
             thick = jnp.where(parity == j, thick_ref[i], other_ref[1, i])
-            segments[k, j, i] = segment(factor, thick, kind, table_ref, decay_ref)
+            segments[k, j, i] = segment(factor, thick, [blocks_ref[j, i, b] for b in range(4)], decay_ref[...])
     slabs = {(k, j): segments[k, j, 0] for k, j in keys}
     for i in range(1, layers):
         couplings = [dot(slabs[k, j][3], segments[k, j, i][0]) for k, j in keys]
-        gaps = inverses(couplings, 2, sum_ref, power_ref, coupling_ref)
+        gaps = inverses(couplings, 2, *scratch)
         for (k, j), gap in zip(keys, gaps):
             above, below = slabs[k, j], segments[k, j, i]
             by_d, by_u = inner_maps(above, below, gap)
@@ -164,63 +198,99 @@
                 dot(by_u[0], below[2]),
                 below[3] + dot(by_u[3], below[2]),
             )
-    couplings = [dot(slabs[k, 0][3], slabs[k, 1][0]) for k in range(size)]
-    gaps = inverses(couplings, 2, sum_ref, power_ref, coupling_ref)
+    for k, j in keys:
+        for b in range(4):
+            slab_ref[start + k, j, b] = slabs[k, j][b]
+    couplings = [dot(slab_ref[start + k, 0, 3], slab_ref[start + k, 1, 0]) for k in range(size)]
+    gaps = inverses(couplings, 2, *scratch)
     for k, gap in enumerate(gaps):
-        above, below = slabs[k, 0], slabs[k, 1]
-        by_d, by_u = inner_maps(above, below, gap)
-        k = start + k
-        for r in range(4):
-            pair_d[k, r * m:(r + 1) * m] = by_d[r]
-            pair_u[k, r * m:(r + 1) * m] = by_u[r]
+        gap_ref[start + k] = gap
+        above, below = [[slab_ref[start + k, j, b] for b in range(4)] for j in range(PAIR)]
         if edge:
-            answer, onward = ends
-            top = group == 0
-            inward = jnp.where(top, below[2], above[1])
-            rows = [dot(jnp.where(top, u, d), inward) for d, u in zip(by_d, by_u)]
-            rows[0] = rows[0] + jnp.where(top, 0.0, above[0])
-            rows[3] = rows[3] + jnp.where(top, below[3], 0.0)
+            first = dot(jnp.where(top, above[3], above[2]), jnp.where(top, below[2], below[0]))
+            left = jnp.where(top, below[1], first)
+            right = jnp.where(top, first, above[1])
+            onward[0][start + k] = jnp.where(top, below[3], above[0]) + dot(left, dot(gap, right))
+
+
+def maps_kernel(vectors, edge, ids_ref, slab_ref, gap_ref, *refs):
+    pair_d, pair_u, *ends = refs[1:] if edge else refs
+    m = gap_ref.shape[-1]
+    top = ids_ref[2] == 0
+
+    def maps_of(start, size):
+        for k in range(size):
+            k = start + k
+            above = [slab_ref[k, 0, b] for b in range(4)]
+            below = [slab_ref[k, 1, b] for b in range(4)]
+            by_d, by_u = inner_maps(above, below, gap_ref[k])
             for r in range(4):
-                answer[k, r * m:(r + 1) * m] = rows[r]
-            onward[k] = jnp.where(top, rows[3], rows[0])
-        else:
-            end_x, end_y = ends
-            for r in range(4):
-                from_x, from_y = dot(by_d[r], above[1]), dot(by_u[r], below[2])
-                end_x[k, r * m:(r + 1) * m] = from_x + above[0] if r == 0 else from_x
-                end_y[k, r * m:(r + 1) * m] = from_y + below[3] if r == 3 else from_y
-
-
-def pack_kernel(share, parts, ids_ref, kind_ref, thick_ref, drive_ref, position_ref, *outs):
-    *blocks, described, held = outs
+                pair_d[k, r * m:(r + 1) * m] = by_d[r]
+                pair_u[k, r * m:(r + 1) * m] = by_u[r]
+            if edge:
+                inward = jnp.where(top, below[2], above[1])
+                for r in range(4):
+                    row = dot(jnp.where(top, by_u[r], by_d[r]), inward)
+                    if r == 0:
+                        row = row + jnp.where(top, 0.0, above[0])
+                    if r == 3:
+                        row = row + jnp.where(top, below[3], 0.0)
+                    ends[0][k, r * m:(r + 1) * m] = row
+            else:
+                end_x, end_y = ends
+                for r in range(4):
+                    from_x, from_y = dot(by_d[r], above[1]), dot(by_u[r], below[2])
+                    end_x[k, r * m:(r + 1) * m] = from_x + above[0] if r == 0 else from_x
+                    end_y[k, r * m:(r + 1) * m] = from_y + below[3] if r == 3 else from_y
+
+    in_batches(vectors, maps_of)
+
+
+def pack_kernel(share, parts, ids_ref, drive_hbm, position_hbm, kind_hbm, thick_hbm, *outs):
+    *blocks, described, held, drive_ref, position_ref, kind_ref, thick_ref, sems, drive_sems = outs
+    layers = drive_hbm.shape[1]
+    small = [
+        pltpu.make_async_copy(position_hbm, position_ref, sems.at[0]),
+        pltpu.make_async_copy(kind_hbm, kind_ref, sems.at[1]),
+        pltpu.make_async_copy(thick_hbm, thick_ref, sems.at[2]),
+    ]
+    large = {
+        (i, d): pltpu.make_async_copy(drive_hbm.at[0, i, d], drive_ref.at[i, d], drive_sems.at[i, d])
+        for i in range(layers) for d in range(2)
+    }
+    for copy in [*small, *large.values()]:
+        copy.start()
+    for copy in small:
+        copy.wait()
     cell = ids_ref[0]
     offset = jnp.abs(cell - position_ref[...])
     offset = jnp.minimum(offset, parts - offset)
     envelope = 1.0 / (1.0 + offset.astype(f32))
-    layers = drive_ref.shape[1]
     for i in range(layers):
         described[0, i] = kind_ref[i].astype(f32)
         described[1, i] = thick_ref[i]
+    for copy in large.values():
+        copy.wait()
     for q in range(parts):
         span = slice(q * share, (q + 1) * share)
         held[q] = jnp.concatenate(
-            [drive_ref[0, i, d, :, span] * envelope[:, span] for i in range(layers) for d in range(2)], axis=1
+            [drive_ref[i, d, :, span] * envelope[:, span] for i in range(layers) for d in range(2)], axis=1
         )
-    for shift in range(parts):
-        blocks[shift][...] = held[lax.rem(cell + shift, parts)]
-
-
-def transform_kernel(parts, ids_ref, cas_ref, *refs):
+    for step in range(parts):
+        blocks[step][...] = held[cell ^ step]
+
+
+def transform_kernel(parts, ids_ref, *refs):
     blocks, (_, kept, sent) = refs[:parts], refs[parts:]
     place, parity = ids_ref[0], ids_ref[1]
     loaded = [b[...] for b in blocks]
-    cells = [lax.rem(place - shift + parts, parts) for shift in range(parts)]
+    cells = [place ^ step for step in range(parts)]
     for side, out in ((parity, kept), (1 - parity, sent)):
         for i in range(out.shape[0]):
             wave = PAIR * i + side
-            total = cas_ref[wave, cells[0]] * loaded[0]
-            for shift in range(1, parts):
-                total = total + cas_ref[wave, cells[shift]] * loaded[shift]
+            total = cas(wave, cells[0], parts) * loaded[0]
+            for step in range(1, parts):
+                total = total + cas(wave, cells[step], parts) * loaded[step]
             out[i] = total
 
 
@@ -287,25 +357,25 @@
         sent[k] = held[1 - parity, k]
 
 
-def return_kernel(parts, ids_ref, cas_ref, kept, got, *blocks):
+def return_kernel(parts, ids_ref, kept, got, *blocks):
     place, parity = ids_ref[0], ids_ref[1]
     vectors = kept.shape[0]
     mine, theirs = [kept[i] for i in range(vectors)], [got[i] for i in range(vectors)]
-    for shift in range(parts):
-        cell = lax.rem(place + shift, parts)
+    for step in range(parts):
+        cell = place ^ step
         total = None
         for side, fields in ((parity, mine), (1 - parity, theirs)):
             for i in range(vectors):
-                term = cas_ref[cell, PAIR * i + side] * fields[i]
+                term = cas(cell, PAIR * i + side, parts) * fields[i]
                 total = term if total is None else total + term
-        blocks[shift][...] = total
+        blocks[step][...] = total
 
 
 def unpack_kernel(share, parts, ids_ref, *refs):
     blocks, (up, down, held) = refs[:parts], refs[parts:]
     place = ids_ref[0]
-    for shift in range(parts):
-        held[lax.rem(place - shift + parts, parts)] = blocks[shift][...]
+    for step in range(parts):
+        held[place ^ step] = blocks[step][...]
     for side, out in enumerate((up, down)):
         span = slice(side * share, (side + 1) * share)
         out[0, 0] = jnp.concatenate([held[q][:, span] for q in range(parts)], axis=1)
@@ -319,18 +389,21 @@
     return pl.BlockSpec(memory_space=pltpu.SMEM)
 
 
-def call(kernel, scalars, arrays, shapes, scratch=(), name=None, flops=0, limit=12, after=(), small=()):
-    moved = sum(a.size * 4 for a in arrays) + sum(math.prod(s) * 4 for s in shapes)
+def call(kernel, scalars, arrays, shapes, scratch=(), name=None, flops=0, limit=12, after=(), small=(), far=()):
+    moved = sum(a.size * 4 for a in (*arrays, *far)) + sum(math.prod(s) * 4 for s in shapes)
     return pl.pallas_call(
         kernel,
         out_shape=tuple(jax.ShapeDtypeStruct(s, f32) for s in (*shapes, *small)),
-        in_specs=[smem()] * len(scalars) + [vmem()] * len(arrays) + [pl.BlockSpec(memory_space=pl.ANY)] * len(after),
+        in_specs=[smem()] * len(scalars)
+        + [vmem()] * len(arrays)
+        + [pl.BlockSpec(memory_space=pltpu.HBM)] * len(far)
+        + [pl.BlockSpec(memory_space=pl.ANY)] * len(after),
         out_specs=tuple([vmem()] * len(shapes) + [smem()] * len(small)),
-        scratch_shapes=[pltpu.VMEM(s, f32) for s in scratch],
+        scratch_shapes=[pltpu.VMEM(s, f32) if isinstance(s, tuple) else s for s in scratch],
         cost_estimate=pl.CostEstimate(flops=flops, bytes_accessed=moved, transcendentals=0),
         compiler_params=pltpu.CompilerParams(vmem_limit_bytes=limit << 20),
         name=name,
-    )(*scalars, *arrays, *after)
+    )(*scalars, *arrays, *far, *after)
 
 
 def exact(left_side, right_side):
@@ -388,46 +461,50 @@
     vectors = parts // PAIR
     share = columns // parts
     width = layers * 2 * share
-    assert drive.shape[0] == 1 and depth % PAIR == 0 and parts % PAIR == 0 and columns % parts == 0
+    assert drive.shape[0] == 1 and depth % PAIR == 0 and columns % parts == 0
+    assert parts % PAIR == 0 and parts & (parts - 1) == 0
     stack_index = lax.axis_index("stack")
     group, parity = stack_index // PAIR, stack_index % PAIR
     ids = jnp.stack([lax.axis_index("bloch"), parity, group]).astype(jnp.int32)
     partner = [(i, i ^ 1) for i in range(depth)]
     across = [(i, i + PAIR) for i in range(depth - PAIR)] + [(i + PAIR, i) for i in range(depth - PAIR)]
-    counts = np.arange(parts)
-    angles = np.outer(counts, counts) % parts * (2.0 * math.pi / parts)
-    cas = jnp.asarray((np.cos(angles) + np.sin(angles)) / math.sqrt(parts), f32)
-    factors = jnp.asarray(1.0 + 0.5 * np.cos(counts * (2.0 * math.pi / parts)), f32)
+    dma = pltpu.SemaphoreType.DMA
 
     def deal(blocks):
-        out = [blocks[0]]
-        for shift in range(1, parts):
-            out.append(lax.ppermute(blocks[shift], "bloch", [(i, (i + shift) % parts) for i in range(parts)]))
-        return out
+        out = {0: blocks[0]}
+        for step in sorted(range(1, parts), reverse=True):
+            out[step] = lax.ppermute(blocks[step], "bloch", [(i, i ^ step) for i in range(parts)])
+        return [out[step] for step in range(parts)]
 
     *packed, described = call(
         functools.partial(pack_kernel, share, parts),
-        [ids, materials, thickness], [drive, positions[None, :]],
-        [(m, width)] * parts, [(parts, m, width)], "pack", small=[(2, layers)],
+        [ids], [], [(m, width)] * parts,
+        [(parts, m, width), (layers, 2, m, columns), pltpu.VMEM((1, columns), jnp.int32), pltpu.SMEM((layers,), jnp.int32),
+         pltpu.SMEM((layers,), f32), dma((3,)), dma((layers, 2))],
+        "pack", small=[(2, layers)], far=[drive, positions[None, :], materials, thickness],
     )
     other = lax.ppermute(described, "stack", partner)
     arrived = deal(packed)
 
     squares = [(vectors * PAIR, m, m)] * 3
-    end_shapes = [(vectors, 4 * m, m), (vectors, m, m)] if edge else [(vectors, 4 * m, m)] * 2
-    slab_d, slab_u, pair_d, pair_u, *ends = call(
-        functools.partial(matrices_kernel, layers, vectors, edge),
-        [ids, factors, materials, thickness, other],
-        [table, decay[None, :]],
-        [(vectors, PAIR, layers - 1, 2 * m, m)] * 2 + [(vectors, 4 * m, m)] * 2 + end_shapes,
-        squares, "matrices", 3000 * m**3, 32,
+    slab_d, slab_u, slab, gap, *onward = call(
+        functools.partial(slabs_kernel, layers, vectors, parts, edge),
+        [ids, other], [],
+        [(vectors, PAIR, layers - 1, 2 * m, m)] * 2 + [(vectors, PAIR, 4, m, m), (vectors, m, m)] + [(vectors, m, m)] * edge,
+        squares + [pltpu.SMEM((layers,), jnp.int32), pltpu.SMEM((layers,), f32), (PAIR, layers, 4, m, m), (1, m),
+                   dma((3,)), dma((PAIR, layers))],
+        "slabs", 3000 * m**3, 32, far=[materials, thickness, table, decay[None, :]],
     )
     if edge:
-        opposite = lax.ppermute(ends[1], "stack", across)
+        opposite = lax.ppermute(onward[0], "stack", across)
+    pair_d, pair_u, *ends = call(
+        functools.partial(maps_kernel, vectors, edge),
+        [ids], [slab, gap], [(vectors, 4 * m, m)] * (3 if edge else 4), (), "maps", 500 * m**3, after=onward,
+    )
 
     kept, sent = call(
         functools.partial(transform_kernel, parts),
-        [ids, cas], arrived, [(vectors, m, width)] * 2, (), "transform", after=[slab_d],
+        [ids], arrived, [(vectors, m, width)] * 2, (), "transform", after=[pair_d],
     )
     got = lax.ppermute(sent, "stack", partner)
     slabs, *end = call(
@@ -438,14 +515,14 @@
     )
     if edge:
         crossed = lax.ppermute(end[0], "stack", across)
-        inner, gap, bounced = call(
+        inner, gate, bounced = call(
             functools.partial(boundary_kernel, vectors),
-            [], [slabs, end[0], pair_d, pair_u, ends[1], opposite],
+            [], [slabs, end[0], pair_d, pair_u, onward[0], opposite],
             [(vectors, 4 * m, share), (vectors, m, m), (m, vectors * share)], squares, "boundary", 1000 * m**3,
         )
         kept, sent = call(
             functools.partial(fields_kernel, vectors),
-            [ids], [inner, ends[0], gap, bounced, crossed],
+            [ids], [inner, ends[0], gate, bounced, crossed],
             [(vectors, m, 2 * share)] * 2, [(PAIR, vectors, m, 2 * share)], "fields",
         )
     else:
@@ -459,7 +536,7 @@
     got = lax.ppermute(sent, "stack", partner)
 
     blocks = call(
-        functools.partial(return_kernel, parts), [ids, cas], [kept, got], [(m, 2 * share)] * parts, (), "return",
+        functools.partial(return_kernel, parts), [ids], [kept, got], [(m, 2 * share)] * parts, (), "return",
     )
     blocks = deal(blocks)
     return call(

time: 61.4 us -> 65.4 us (1.065)
  Pallas kernels: 23.8 us -> 27.3 us
  waiting for transfers between devices: 14.5 us -> 16.2 us
  local copies, waits for them, and re-layouts: 7.66 us -> 7 us
    pallas_call x8 -> x9, Pallas kernels: 23.8 us -> 27.3 us  [call(): pl.pallas_call(kernel, out_shape=tuple((jax.ShapeDtypeStruct(s, f32) for...]
    ppermute x1, waiting for transfers between devices: 0.01 us -> 1.16 us  [shards(): other = lax.ppermute(described, 'stack', partner)]
    unnamed x20 -> x16, local copies, waits for them, and re-layouts: 7.66 us -> 7 us
  transfers between devices with their start and end apart: 11 -> 11, of which waited for: 5 -> 5; matrix products, arithmetic and copies ran while one was open for 0% -> 0% of each run, Pallas kernels for 29% -> 31%
where the time goes in v3:
time: 65.4 us; the launch traced here: 65.2 us
  Pallas kernels  27.3 us (42%)
  waiting for transfers between devices  16.2 us (25%)
  starting transfers between devices  13.8 us (21%)
  local copies, waits for them, and re-layouts  7 us (11%)
  between operations  0.76 us (1%)
    pallas_call x9, Pallas kernels, call(): pl.pallas_call(kernel, out_shape=tuple((jax.ShapeDtypeStruct(s, f32) for...  27.3 us
    ppermute x6, starting transfers between devices, deal(): lax.ppermute(blocks[step], 'bloch', [(i, i ^ step) for i in range(parts)])  10.2 us
    ppermute x6, waiting for transfers between devices, deal(): lax.ppermute(blocks[step], 'bloch', [(i, i ^ step) for i in range(parts)])  7.86 us
    unnamed x16, local copies, waits for them, and re-layouts  7 us
    ppermute x1, waiting for transfers between devices, shards(): opposite = lax.ppermute(onward[0], 'stack', across)  5.72 us
    ppermute x1, starting transfers between devices, shards(): opposite = lax.ppermute(onward[0], 'stack', across)  1.74 us
    ppermute x1, starting transfers between devices, shards(): crossed = lax.ppermute(end[0], 'stack', across)  1.61 us
    ppermute x2, waiting for transfers between devices, shards(): got = lax.ppermute(sent, 'stack', partner)  1.43 us
  transfers between devices with their start and end apart: 11, of which 5 were waited for; matrix products, arithmetic and copies ran while one was open for 0% of the time, Pallas kernels for 31%

profile of v3, /device:TPU:0, one launch (start us, length us, event | category | flops | bytes accessed | tf_op | source)
XLA Modules:
  0.0 65.2 jit_solution(7042853186118670265)
XLA Ops:
  0.6 0.1 pad_add_fusion.ids_ref
  0.7 0.0 copy-start
  0.7 1.1 %copy-done = f32[1,2,2,192,256]{4,3,2,1,0:T(8,128)S(1)} copy-done((f32[1,2,2,192,256]{4,3,2,1,0:T(8,128)S(1)}, f32[1,2,2,192,256]{4,3,2,1,0:T(8,128)}, u32[]{:S(2)}) %copy-start) | copy-done | bytes 786456
  1.9 0.0 copy-start.1
  1.9 0.7 %copy-done.1 = s32[256]{0:T(256)S(1)} copy-done((s32[256]{0:T(256)S(1)}, s32[256]{0:T(256)}, u32[]{:S(2)}) %copy-start.1) | copy-done | bytes 1048
  2.5 0.0 copy-start.2
  2.5 0.7 %copy-done.2 = s32[2]{0:T(128)S(1)} copy-done((s32[2]{0:T(128)S(1)}, s32[2]{0:T(128)}, u32[]{:S(2)}) %copy-start.2) | copy-done | bytes 32
  3.2 0.0 copy-start.4
  3.2 0.7 %copy-done.4 = f32[2]{0:T(128)S(1)} copy-done((f32[2]{0:T(128)S(1)}, f32[2]{0:T(128)}, u32[]{:S(2)}) %copy-start.4) | copy-done | bytes 32
  3.9 2.3 %pack.1 = (f32[192,256]{1,0:T(8,128)S(1)}, f32[192,256]{1,0:T(8,128)S(1)}, f32[192,256]{1,0:T(8,128)S(1)}, f32[192,256]{1,0:T(8,128)S(1)}, f32[2,2]{1,0:T(2,128)S(1)}) custom-call(s32[3]{0:T(128)S(1)} %pad_add_fusion.ids_ref, f32[1,2,2,192,256]{4,3,2,1,0:T(8,128)S(1)} %copy-done, s32[1,256]{1,0:T(1,128)S(1)} %bitcast.5, s32[2]{0:T(128)S(1)} %copy-done.2, ...), custom_call_target="tpu_custom_call" | custom-call | bytes 1573904 | tf_op jit(solution)/shard_map/pack/pallas_call | solution.py:394
  6.1 3.1 %collective-permute-start = (f32[192,256]{1,0:T(8,128)S(1)}, f32[192,256]{1,0:T(8,128)S(1)}, u32[]{:S(2)}, u32[]{:S(2)}) collective-permute-start(f32[192,256]{1,0:T(8,128)S(1)} %get-tuple-element.29), channel_id=1, source_target_pairs={{0,1},{1,0},{2,3},{3,2},{4,5},{5,4},{6,7},{7,6},{8,9},{9,8},{10,11... | collective-permute-start | bytes 589832 | tf_op jit(solution)/shard_map/ppermute | solution.py:476
  9.2 2.6 %collective-permute-start.1 = (f32[192,256]{1,0:T(8,128)S(1)}, f32[192,256]{1,0:T(8,128)S(1)}, u32[]{:S(2)}, u32[]{:S(2)}) collective-permute-start(f32[192,256]{1,0:T(8,128)S(1)} %get-tuple-element.30), channel_id=1, source_target_pairs={{0,2},{1,3},{2,0},{3,1},{4,6},{5,7},{6,4},{7,5},{8,10},{9,11},{10,... | collective-permute-start | bytes 589832 | tf_op jit(solution)/shard_map/ppermute | solution.py:476
  11.8 0.0 collective-permute-start.2
  11.8 0.0 collective-permute-start.3
  11.8 1.2 %collective-permute-done.3.other_ref = f32[2,2]{1,0:T(2,128)S(1)} collective-permute-done((f32[2,2]{1,0:T(2,128)S(1)}, f32[2,2]{1,0:T(2,128)S(1)}, u32[]{:S(2)}, u32[]{:S(2)}) %collective-permute-start.3) | collective-permute-done | bytes 48 | tf_op jit(solution)/shard_map/ppermute | solution.py:486
  13.0 0.0 copy-start.3
  13.0 0.7 %copy-done.3 = s32[2]{0:T(128)S(1)} copy-done((s32[2]{0:T(128)S(1)}, s32[2]{0:T(128)}, u32[]{:S(2)}) %copy-start.3) | copy-done | bytes 32
  13.6 0.0 copy-start.5
  13.7 0.7 %copy-done.5 = f32[2]{0:T(128)S(1)} copy-done((f32[2]{0:T(128)S(1)}, f32[2]{0:T(128)}, u32[]{:S(2)}) %copy-start.5) | copy-done | bytes 32
  14.3 0.0 copy-start.6
  14.3 1.9 %copy-done.6 = f32[4,4,192,192]{3,2,1,0:T(8,128)S(1)} copy-done((f32[4,4,192,192]{3,2,1,0:T(8,128)S(1)}, f32[4,4,192,192]{3,2,1,0:T(8,128)}, u32[]{:S(2)}) %copy-start.6) | copy-done | bytes 2359320
  16.2 0.0 copy-start.7
  16.2 0.7 %copy-done.7 = f32[192]{0:T(256)S(1)} copy-done((f32[192]{0:T(256)S(1)}, f32[192]{0:T(256)}, u32[]{:S(2)}) %copy-start.7) | copy-done | bytes 792
  16.9 11.0 %slabs.1 = (f32[2,2,1,384,192]{4,3,2,1,0:T(8,128)S(1)}, f32[2,2,1,384,192]{4,3,2,1,0:T(8,128)S(1)}, f32[2,2,4,192,192]{4,3,2,1,0:T(8,128)S(1)}, f32[2,192,192]{2,1,0:T(8,128)S(1)}, f32[2,192,192]{2,1,0:T(8,128)S(1)}) custom-call(s32[3]{0:T(128)S(1)} %pad_add_fusion.ids_ref, f32[2,2]{1,0:T(2,128)S(1)} %collective-permute-done.3.other_ref, s32[2]{0:T(128)S(1)} %copy-done.3, ...), custom_call_target="tpu_custom_call" | custom-call | flops 21233664000 | bytes 7668496 | tf_op jit(solution)/shard_map/slabs/pallas_call | solution.py:394
  27.9 2.9 %maps.1 = (f32[2,768,192]{2,1,0:T(8,128)S(1)}, f32[2,768,192]{2,1,0:T(8,128)S(1)}, f32[2,768,192]{2,1,0:T(8,128)S(1)}) custom-call(s32[3]{0:T(128)S(1)} %pad_add_fusion.ids_ref, f32[2,2,4,192,192]{4,3,2,1,0:T(8,128)S(1)} %get-tuple-element.33.slab_ref, f32[2,192,192]{2,1,0:T(8,128)S(1)} %get-tuple-element.34.gap_ref, ...), custom_call_target="tpu_custom_call" | custom-call | flops 3538944000 | bytes 6193152 | tf_op jit(solution)/shard_map/maps/pallas_call | solution.py:394
  30.8 0.0 collective-permute-done.refs_1_
  30.8 0.0 collective-permute-done.1.refs_2_
  30.8 0.0 collective-permute-done.2.refs_3_
  30.8 0.8 %transform.1 = (f32[2,192,256]{2,1,0:T(8,128)S(1)}, f32[2,192,256]{2,1,0:T(8,128)S(1)}) custom-call(s32[3]{0:T(128)S(1)} %pad_add_fusion.ids_ref, f32[192,256]{1,0:T(8,128)S(1)} %get-tuple-element.28.refs_0_, f32[192,256]{1,0:T(8,128)S(1)} %collective-permute-done.refs_1_, f32[192,256]{1,0:T(8,128)S(1)} %collective-permute-done.1.refs_2_, ...), custom_call_target="tpu_custom_call" | custom-call | bytes 1572864 | tf_op jit(solution)/shard_map/transform/pallas_call | solution.py:394
  31.6 0.2 collective-permute-start.4
  31.8 1.7 %collective-permute-start.5 = (f32[2,192,192]{2,1,0:T(8,128)S(1)}, f32[2,192,192]{2,1,0:T(8,128)S(1)}, u32[]{:S(2)}, u32[]{:S(2)}) collective-permute-start(f32[2,192,192]{2,1,0:T(8,128)S(1)} %get-tuple-element.35.refs_0_.onward), channel_id=1, source_target_pairs={{0,8},{4,12},{8,0},{12,4},{1,9},{5,13},{9,1},{13,5},{2,10},{6,14},... | collective-permute-start | bytes 884744 | tf_op jit(solution)/shard_map/ppermute | solution.py:499
  33.6 0.0 collective-permute-done.4.got
  33.6 2.9 %sources.1 = (f32[2,4,192,64]{3,2,1,0:T(8,128)S(1)}, f32[192,128]{1,0:T(8,128)S(1)}) custom-call(s32[3]{0:T(128)S(1)} %pad_add_fusion.ids_ref, f32[2,192,256]{2,1,0:T(8,128)S(1)} %get-tuple-element.37.kept, f32[2,192,256]{2,1,0:T(8,128)S(1)} %collective-permute-done.4.got, f32[2,2,1,384,192]{4,3,2,1,0:T(8,128)S(1)} %get-tuple-element.39.slab_d, ...), custom_call_target="tpu_custom_call" | custom-call | bytes 5996544 | tf_op jit(solution)/shard_map/sources/pallas_call | solution.py:394
  36.5 1.6 %collective-permute-start.6 = (f32[192,128]{1,0:T(8,128)S(1)}, f32[192,128]{1,0:T(8,128)S(1)}, u32[]{:S(2)}, u32[]{:S(2)}) collective-permute-start(f32[192,128]{1,0:T(8,128)S(1)} %get-tuple-element.43.end), channel_id=1, source_target_pairs={{0,8},{4,12},{8,0},{12,4},{1,9},{5,13},{9,1},{13,5},{2,10},{6,14},... | collective-permute-start | bytes 294920 | tf_op jit(solution)/shard_map/ppermute | solution.py:517
  38.1 5.7 %collective-permute-done.5.arrived = f32[2,192,192]{2,1,0:T(8,128)S(1)} collective-permute-done((f32[2,192,192]{2,1,0:T(8,128)S(1)}, f32[2,192,192]{2,1,0:T(8,128)S(1)}, u32[]{:S(2)}, u32[]{:S(2)}) %collective-permute-start.5) | collective-permute-done | bytes 294944 | tf_op jit(solution)/shard_map/ppermute | solution.py:499
  43.8 3.4 %boundary.1 = (f32[2,768,64]{2,1,0:T(8,128)S(1)}, f32[2,192,192]{2,1,0:T(8,128)S(1)}, f32[192,128]{1,0:T(8,128)S(1)}) custom-call(f32[2,4,192,64]{3,2,1,0:T(8,128)S(1)} %get-tuple-element.42.slabs, f32[192,128]{1,0:T(8,128)S(1)} %get-tuple-element.43.end, f32[2,768,192]{2,1,0:T(8,128)S(1)} %get-tuple-element.36.refs_4_.pair_d, ...), custom_call_target="tpu_custom_call" | custom-call | flops 7077888000 | bytes 4227072 | tf_op jit(solution)/shard_map/boundary/pallas_call | solution.py:394
  47.2 0.0 collective-permute-done.6.crossed
  47.2 2.0 %fields.1 = (f32[2,192,128]{2,1,0:T(8,128)S(1)}, f32[2,192,128]{2,1,0:T(8,128)S(1)}) custom-call(s32[3]{0:T(128)S(1)} %pad_add_fusion.ids_ref, f32[2,768,64]{2,1,0:T(8,128)S(1)} %get-tuple-element.44.inner, f32[2,768,192]{2,1,0:T(8,128)S(1)} %get-tuple-element.45.answer, f32[2,192,192]{2,1,0:T(8,128)S(1)} %get-tuple-element.46.gap, ...), custom_call_target="tpu_custom_call" | custom-call | bytes 2457600 | tf_op jit(solution)/shard_map/fields/pallas_call | solution.py:394
  49.2 0.1 collective-permute-start.7
  49.3 1.4 %collective-permute-done.7.got = f32[2,192,128]{2,1,0:T(8,128)S(1)} collective-permute-done((f32[2,192,128]{2,1,0:T(8,128)S(1)}, f32[2,192,128]{2,1,0:T(8,128)S(1)}, u32[]{:S(2)}, u32[]{:S(2)}) %collective-permute-start.7) | collective-permute-done | bytes 196640 | tf_op jit(solution)/shard_map/ppermute | solution.py:536
  50.8 0.7 return.1
  51.4 1.0 %collective-permute-start.8 = (f32[192,128]{1,0:T(8,128)S(1)}, f32[192,128]{1,0:T(8,128)S(1)}, u32[]{:S(2)}, u32[]{:S(2)}) collective-permute-start(f32[192,128]{1,0:T(8,128)S(1)} %get-tuple-element.51), channel_id=1, source_target_pairs={{0,1},{1,0},{2,3},{3,2},{4,5},{5,4},{6,7},{7,6},{8,9},{9,8},{10,11... | collective-permute-start | bytes 294920 | tf_op jit(solution)/shard_map/ppermute | solution.py:476
  52.4 3.5 %collective-permute-start.9 = (f32[192,128]{1,0:T(8,128)S(1)}, f32[192,128]{1,0:T(8,128)S(1)}, u32[]{:S(2)}, u32[]{:S(2)}) collective-permute-start(f32[192,128]{1,0:T(8,128)S(1)} %get-tuple-element.52), channel_id=1, source_target_pairs={{0,2},{1,3},{2,0},{3,1},{4,6},{5,7},{6,4},{7,5},{8,10},{9,11},{10,... | collective-permute-start | bytes 294920 | tf_op jit(solution)/shard_map/ppermute | solution.py:476
  55.9 0.0 collective-permute-start.10
  55.9 0.4 collective-permute-done.8.refs_1_
  56.3 7.4 %collective-permute-done.9.refs_2_ = f32[192,128]{1,0:T(8,128)S(1)} collective-permute-done((f32[192,128]{1,0:T(8,128)S(1)}, f32[192,128]{1,0:T(8,128)S(1)}, u32[]{:S(2)}, u32[]{:S(2)}) %collective-permute-start.9) | collective-permute-done | bytes 98336 | tf_op jit(solution)/shard_map/ppermute | solution.py:476
  63.7 0.0 collective-permute-done.10.refs_3_
  63.7 1.4 %unpack.1 = (f32[1,1,192,256]{3,2,1,0:T(8,128)}, f32[1,1,192,256]{3,2,1,0:T(8,128)}) custom-call(s32[3]{0:T(128)S(1)} %pad_add_fusion.ids_ref, f32[192,128]{1,0:T(8,128)S(1)} %get-tuple-element.50.refs_0_, f32[192,128]{1,0:T(8,128)S(1)} %collective-permute-done.8.refs_1_, f32[192,128]{1,0:T(8,128)S(1)} %collective-permute-done.9.refs_2_, ...), custom_call_target="tpu_custom_call" | custom-call | bytes 786432 | tf_op jit(solution)/shard_map/unpack/pallas_call | solution.py:394
Async XLA Ops:
  0.7 1.1 %copy-start = (f32[1,2,2,192,256]{4,3,2,1,0:T(8,128)S(1)}, f32[1,2,2,192,256]{4,3,2,1,0:T(8,128)}, u32[]{:S(2)}) copy-start(f32[1,2,2,192,256]{4,3,2,1,0:T(8,128)} %drive_hbm.1) | copy-start | bytes 2359300
  1.9 0.7 %copy-start.1 = (s32[256]{0:T(256)S(1)}, s32[256]{0:T(256)}, u32[]{:S(2)}) copy-start(s32[256]{0:T(256)} %param.7) | copy-start | bytes 3076
  2.5 0.7 %copy-start.2 = (s32[2]{0:T(128)S(1)}, s32[2]{0:T(128)}, u32[]{:S(2)}) copy-start(s32[2]{0:T(128)} %kind_hbm.3) | copy-start | bytes 28
  3.2 0.7 %copy-start.4 = (f32[2]{0:T(128)S(1)}, f32[2]{0:T(128)}, u32[]{:S(2)}) copy-start(f32[2]{0:T(128)} %thick_hbm.3) | copy-start | bytes 28
  6.1 24.7 %collective-permute-start = (f32[192,256]{1,0:T(8,128)S(1)}, f32[192,256]{1,0:T(8,128)S(1)}, u32[]{:S(2)}, u32[]{:S(2)}) collective-permute-start(f32[192,256]{1,0:T(8,128)S(1)} %get-tuple-element.29), channel_id=1, source_target_pairs={{0,1},{1,0},{2,3},{3,2},{4,5},{5,4},{6,7},{7,6},{8,9},{9,8},{10,11... | collective-permute-start | bytes 589832 | tf_op jit(solution)/shard_map/ppermute | solution.py:476
  9.2 21.6 %collective-permute-start.1 = (f32[192,256]{1,0:T(8,128)S(1)}, f32[192,256]{1,0:T(8,128)S(1)}, u32[]{:S(2)}, u32[]{:S(2)}) collective-permute-start(f32[192,256]{1,0:T(8,128)S(1)} %get-tuple-element.30), channel_id=1, source_target_pairs={{0,2},{1,3},{2,0},{3,1},{4,6},{5,7},{6,4},{7,5},{8,10},{9,11},{10,... | collective-permute-start | bytes 589832 | tf_op jit(solution)/shard_map/ppermute | solution.py:476
  11.8 19.0 %collective-permute-start.2 = (f32[192,256]{1,0:T(8,128)S(1)}, f32[192,256]{1,0:T(8,128)S(1)}, u32[]{:S(2)}, u32[]{:S(2)}) collective-permute-start(f32[192,256]{1,0:T(8,128)S(1)} %get-tuple-element.31), channel_id=1, source_target_pairs={{0,3},{1,2},{2,1},{3,0},{4,7},{5,6},{6,5},{7,4},{8,11},{9,10},{10,... | collective-permute-start | bytes 589832 | tf_op jit(solution)/shard_map/ppermute | solution.py:476
  11.8 1.2 %collective-permute-start.3 = (f32[2,2]{1,0:T(2,128)S(1)}, f32[2,2]{1,0:T(2,128)S(1)}, u32[]{:S(2)}, u32[]{:S(2)}) collective-permute-start(f32[2,2]{1,0:T(2,128)S(1)} %get-tuple-element.32), channel_id=1, source_target_pairs={{0,4},{4,0},{8,12},{12,8},{1,5},{5,1},{9,13},{13,9},{2,6},{6,2},{1... | collective-permute-start | bytes 56 | tf_op jit(solution)/shard_map/ppermute | solution.py:486
  13.0 0.7 %copy-start.3 = (s32[2]{0:T(128)S(1)}, s32[2]{0:T(128)}, u32[]{:S(2)}) copy-start(s32[2]{0:T(128)} %kind_hbm.3) | copy-start | bytes 28
  13.6 0.7 %copy-start.5 = (f32[2]{0:T(128)S(1)}, f32[2]{0:T(128)}, u32[]{:S(2)}) copy-start(f32[2]{0:T(128)} %thick_hbm.3) | copy-start | bytes 28
  14.3 1.9 %copy-start.6 = (f32[4,4,192,192]{3,2,1,0:T(8,128)S(1)}, f32[4,4,192,192]{3,2,1,0:T(8,128)}, u32[]{:S(2)}) copy-start(f32[4,4,192,192]{3,2,1,0:T(8,128)} %table_hbm.1) | copy-start | bytes 7077892
  16.2 0.7 %copy-start.7 = (f32[192]{0:T(256)S(1)}, f32[192]{0:T(256)}, u32[]{:S(2)}) copy-start(f32[192]{0:T(256)} %param.11) | copy-start | bytes 2308
  31.6 2.0 %collective-permute-start.4 = (f32[2,192,256]{2,1,0:T(8,128)S(1)}, f32[2,192,256]{2,1,0:T(8,128)S(1)}, u32[]{:S(2)}, u32[]{:S(2)}) collective-permute-start(f32[2,192,256]{2,1,0:T(8,128)S(1)} %get-tuple-element.38), channel_id=1, source_target_pairs={{0,4},{4,0},{8,12},{12,8},{1,5},{5,1},{9,13},{13,9},{2,6},{6,2},{1... | collective-permute-start | bytes 1179656 | tf_op jit(solution)/shard_map/ppermute | solution.py:509
  31.8 12.0 %collective-permute-start.5 = (f32[2,192,192]{2,1,0:T(8,128)S(1)}, f32[2,192,192]{2,1,0:T(8,128)S(1)}, u32[]{:S(2)}, u32[]{:S(2)}) collective-permute-start(f32[2,192,192]{2,1,0:T(8,128)S(1)} %get-tuple-element.35.refs_0_.onward), channel_id=1, source_target_pairs={{0,8},{4,12},{8,0},{12,4},{1,9},{5,13},{9,1},{13,5},{2,10},{6,14},... | collective-permute-start | bytes 884744 | tf_op jit(solution)/shard_map/ppermute | solution.py:499
  36.5 10.7 %collective-permute-start.6 = (f32[192,128]{1,0:T(8,128)S(1)}, f32[192,128]{1,0:T(8,128)S(1)}, u32[]{:S(2)}, u32[]{:S(2)}) collective-permute-start(f32[192,128]{1,0:T(8,128)S(1)} %get-tuple-element.43.end), channel_id=1, source_target_pairs={{0,8},{4,12},{8,0},{12,4},{1,9},{5,13},{9,1},{13,5},{2,10},{6,14},... | collective-permute-start | bytes 294920 | tf_op jit(solution)/shard_map/ppermute | solution.py:517
  49.2 1.5 %collective-permute-start.7 = (f32[2,192,128]{2,1,0:T(8,128)S(1)}, f32[2,192,128]{2,1,0:T(8,128)S(1)}, u32[]{:S(2)}, u32[]{:S(2)}) collective-permute-start(f32[2,192,128]{2,1,0:T(8,128)S(1)} %get-tuple-element.49), channel_id=1, source_target_pairs={{0,4},{4,0},{8,12},{12,8},{1,5},{5,1},{9,13},{13,9},{2,6},{6,2},{1... | collective-permute-start | bytes 589832 | tf_op jit(solution)/shard_map/ppermute | solution.py:536
  51.4 4.9 %collective-permute-start.8 = (f32[192,128]{1,0:T(8,128)S(1)}, f32[192,128]{1,0:T(8,128)S(1)}, u32[]{:S(2)}, u32[]{:S(2)}) collective-permute-start(f32[192,128]{1,0:T(8,128)S(1)} %get-tuple-element.51), channel_id=1, source_target_pairs={{0,1},{1,0},{2,3},{3,2},{4,5},{5,4},{6,7},{7,6},{8,9},{9,8},{10,11... | collective-permute-start | bytes 294920 | tf_op jit(solution)/shard_map/ppermute | solution.py:476
  52.4 11.3 %collective-permute-start.9 = (f32[192,128]{1,0:T(8,128)S(1)}, f32[192,128]{1,0:T(8,128)S(1)}, u32[]{:S(2)}, u32[]{:S(2)}) collective-permute-start(f32[192,128]{1,0:T(8,128)S(1)} %get-tuple-element.52), channel_id=1, source_target_pairs={{0,2},{1,3},{2,0},{3,1},{4,6},{5,7},{6,4},{7,5},{8,10},{9,11},{10,... | collective-permute-start | bytes 294920 | tf_op jit(solution)/shard_map/ppermute | solution.py:476
  55.9 7.9 %collective-permute-start.10 = (f32[192,128]{1,0:T(8,128)S(1)}, f32[192,128]{1,0:T(8,128)S(1)}, u32[]{:S(2)}, u32[]{:S(2)}) collective-permute-start(f32[192,128]{1,0:T(8,128)S(1)} %get-tuple-element.53), channel_id=1, source_target_pairs={{0,3},{1,2},{2,1},{3,0},{4,7},{5,6},{6,5},{7,4},{8,11},{9,10},{10,... | collective-permute-start | bytes 294920 | tf_op jit(solution)/shard_map/ppermute | solution.py:476

commit v4 on v3

--- a/solution.py
+++ b/solution.py
@@ -389,7 +389,7 @@
     return pl.BlockSpec(memory_space=pltpu.SMEM)
 
 
-def call(kernel, scalars, arrays, shapes, scratch=(), name=None, flops=0, limit=12, after=(), small=(), far=()):
+def call(kernel, scalars, arrays, shapes, scratch=(), flops=0, limit=12, after=(), small=(), far=()):
     moved = sum(a.size * 4 for a in (*arrays, *far)) + sum(math.prod(s) * 4 for s in shapes)
     return pl.pallas_call(
         kernel,
@@ -402,8 +402,7 @@
         scratch_shapes=[pltpu.VMEM(s, f32) if isinstance(s, tuple) else s for s in scratch],
         cost_estimate=pl.CostEstimate(flops=flops, bytes_accessed=moved, transcendentals=0),
         compiler_params=pltpu.CompilerParams(vmem_limit_bytes=limit << 20),
-        name=name,
-    )(*scalars, *arrays, *far, *after)
+    )(*scalars, *arrays, *(pltpu.with_memory_space_constraint(a, pltpu.HBM) for a in far), *after)
 
 
 def exact(left_side, right_side):
@@ -419,7 +418,7 @@
     return lax.fori_loop(0, 6, step, identity + coupling)
 
 
-def chain(groups, group, depth, end_x, end_y, slabs, inner):
+def chain(groups, group, depth, end_x, end_y, inner):
     m = end_x.shape[-1]
     down_route = [(i, i + PAIR) for i in range(depth - PAIR)]
     up_route = [(i + PAIR, i) for i in range(depth - PAIR)]
@@ -481,7 +480,7 @@
         [ids], [], [(m, width)] * parts,
         [(parts, m, width), (layers, 2, m, columns), pltpu.VMEM((1, columns), jnp.int32), pltpu.SMEM((layers,), jnp.int32),
          pltpu.SMEM((layers,), f32), dma((3,)), dma((layers, 2))],
-        "pack", small=[(2, layers)], far=[drive, positions[None, :], materials, thickness],
+        small=[(2, layers)], far=[drive, positions[None, :], materials, thickness],
     )
     other = lax.ppermute(described, "stack", partner)
     arrived = deal(packed)
@@ -493,55 +492,53 @@
         [(vectors, PAIR, layers - 1, 2 * m, m)] * 2 + [(vectors, PAIR, 4, m, m), (vectors, m, m)] + [(vectors, m, m)] * edge,
         squares + [pltpu.SMEM((layers,), jnp.int32), pltpu.SMEM((layers,), f32), (PAIR, layers, 4, m, m), (1, m),
                    dma((3,)), dma((PAIR, layers))],
-        "slabs", 3000 * m**3, 32, far=[materials, thickness, table, decay[None, :]],
+        3000 * m**3, 32, far=[materials, thickness, table, decay[None, :]],
     )
     if edge:
         opposite = lax.ppermute(onward[0], "stack", across)
     pair_d, pair_u, *ends = call(
         functools.partial(maps_kernel, vectors, edge),
-        [ids], [slab, gap], [(vectors, 4 * m, m)] * (3 if edge else 4), (), "maps", 500 * m**3, after=onward,
+        [ids], [slab, gap], [(vectors, 4 * m, m)] * (3 if edge else 4), (), 500 * m**3, after=onward,
     )
 
     kept, sent = call(
         functools.partial(transform_kernel, parts),
-        [ids], arrived, [(vectors, m, width)] * 2, (), "transform", after=[pair_d],
+        [ids], arrived, [(vectors, m, width)] * 2, (), after=[pair_d],
     )
     got = lax.ppermute(sent, "stack", partner)
     slabs, *end = call(
         functools.partial(sources_kernel, layers, share, vectors, edge),
         [ids], [kept, got, slab_d, slab_u, pair_d, pair_u],
         [(vectors, 4, m, share)] + ([(m, vectors * share)] if edge else []),
-        [(PAIR, vectors, m, width)], "sources",
+        [(PAIR, vectors, m, width)],
     )
     if edge:
         crossed = lax.ppermute(end[0], "stack", across)
         inner, gate, bounced = call(
             functools.partial(boundary_kernel, vectors),
             [], [slabs, end[0], pair_d, pair_u, onward[0], opposite],
-            [(vectors, 4 * m, share), (vectors, m, m), (m, vectors * share)], squares, "boundary", 1000 * m**3,
+            [(vectors, 4 * m, share), (vectors, m, m), (m, vectors * share)], squares, 1000 * m**3,
         )
         kept, sent = call(
             functools.partial(fields_kernel, vectors),
             [ids], [inner, ends[0], gate, bounced, crossed],
-            [(vectors, m, 2 * share)] * 2, [(PAIR, vectors, m, 2 * share)], "fields",
+            [(vectors, m, 2 * share)] * 2, [(PAIR, vectors, m, 2 * share)],
         )
     else:
         (inner,) = call(
-            functools.partial(inner_kernel, vectors), [], [slabs, pair_d, pair_u], [(vectors, 4 * m, share)], (), "inner",
+            functools.partial(inner_kernel, vectors), [], [slabs, pair_d, pair_u], [(vectors, 4 * m, share)], (),
         )
-        rows = chain(groups, group, depth, ends[0], ends[1], slabs, inner)
+        rows = chain(groups, group, depth, ends[0], ends[1], inner)
         sides = [jnp.concatenate([rows[:, 2 * j * m:(2 * j + 1) * m], rows[:, (2 * j + 1) * m:(2 * j + 2) * m]], 2) for j in range(PAIR)]
         kept = jnp.where(parity == 0, sides[0], sides[1])
         sent = jnp.where(parity == 0, sides[1], sides[0])
     got = lax.ppermute(sent, "stack", partner)
 
-    blocks = call(
-        functools.partial(return_kernel, parts), [ids], [kept, got], [(m, 2 * share)] * parts, (), "return",
-    )
+    blocks = call(functools.partial(return_kernel, parts), [ids], [kept, got], [(m, 2 * share)] * parts, ())
     blocks = deal(blocks)
     return call(
         functools.partial(unpack_kernel, share, parts),
-        [ids], blocks, [(1, 1, m, columns)] * 2, [(parts, m, 2 * share)], "unpack",
+        [ids], blocks, [(1, 1, m, columns)] * 2, [(parts, m, 2 * share)],
     )
 
 
@@ -558,4 +555,5 @@
         P(("groups", "bloch"), "stack", None, None),
         P(("groups", "bloch"), "stack", None, None),
     )
+
     return jax.shard_map(shards, mesh=mesh, in_specs=in_specs, out_specs=out_specs, check_vma=False)

time: 65.4 us -> 60.3 us (0.922)
  local copies, waits for them, and re-layouts: 7 us -> 0 us
  Pallas kernels: 27.3 us -> 29.3 us
    unnamed x16 -> x0, local copies, waits for them, and re-layouts: 7 us -> none
    pallas_call x9, Pallas kernels: 27.3 us -> 29.3 us  [call(): pl.pallas_call(kernel, out_shape=tuple((jax.ShapeDtypeStruct(s, f32) for...]
  transfers between devices with their start and end apart: 11 -> 11, of which waited for: 5 -> 5; matrix products, arithmetic and copies ran while one was open for 0% -> 0% of each run, Pallas kernels for 31% -> 37%
where the time goes in v4:
time: 60.3 us; the launch traced here: 60.1 us
  Pallas kernels  29.3 us (49%)
  waiting for transfers between devices  16.2 us (27%)
  starting transfers between devices  13.8 us (23%)
  between operations  0.76 us (1%)
    pallas_call x9, Pallas kernels, call(): pl.pallas_call(kernel, out_shape=tuple((jax.ShapeDtypeStruct(s, f32) for...  29.3 us
    ppermute x6, starting transfers between devices, deal(): lax.ppermute(blocks[step], 'bloch', [(i, i ^ step) for i in range(parts)])  10.2 us
    ppermute x6, waiting for transfers between devices, deal(): lax.ppermute(blocks[step], 'bloch', [(i, i ^ step) for i in range(parts)])  7.86 us
    ppermute x1, waiting for transfers between devices, shards(): opposite = lax.ppermute(onward[0], 'stack', across)  5.7 us
    ppermute x1, starting transfers between devices, shards(): opposite = lax.ppermute(onward[0], 'stack', across)  1.73 us
    ppermute x1, starting transfers between devices, shards(): crossed = lax.ppermute(end[0], 'stack', across)  1.62 us
    ppermute x2, waiting for transfers between devices, shards(): got = lax.ppermute(sent, 'stack', partner)  1.43 us
  transfers between devices with their start and end apart: 11, of which 5 were waited for; matrix products, arithmetic and copies ran while one was open for 0% of the time, Pallas kernels for 37%

profile of v4, /device:TPU:0, one launch (start us, length us, event | category | flops | bytes accessed | tf_op | source)
XLA Modules:
  0.0 60.1 jit_solution(16913709348065894852)
XLA Ops:
  0.6 0.1 pad_add_fusion.ids_ref
  0.7 2.4 %shard_map.77 = (f32[192,256]{1,0:T(8,128)S(1)}, f32[192,256]{1,0:T(8,128)S(1)}, f32[192,256]{1,0:T(8,128)S(1)}, f32[192,256]{1,0:T(8,128)S(1)}, f32[2,2]{1,0:T(2,128)S(1)}) custom-call(s32[3]{0:T(128)S(1)} %pad_add_fusion.ids_ref, f32[1,2,2,192,256]{4,3,2,1,0:T(8,128)} %drive_hbm.1, s32[1,256]{1,0:T(1,128)} %bitcast.5, s32[2]{0:T(128)} %kind_hbm.3, f32[2]{0:T(128)} %thick_hbm.3), custom_call_target="tpu_custom_call" | custom-call | bytes 1573904 | tf_op jit(solution)/shard_map/pallas_call | solution.py:394
  3.2 3.1 %collective-permute-start = (f32[192,256]{1,0:T(8,128)S(1)}, f32[192,256]{1,0:T(8,128)S(1)}, u32[]{:S(2)}, u32[]{:S(2)}) collective-permute-start(f32[192,256]{1,0:T(8,128)S(1)} %get-tuple-element.29), channel_id=1, source_target_pairs={{0,1},{1,0},{2,3},{3,2},{4,5},{5,4},{6,7},{7,6},{8,9},{9,8},{10,11... | collective-permute-start | bytes 589832 | tf_op jit(solution)/shard_map/ppermute | solution.py:475
  6.3 2.6 %collective-permute-start.1 = (f32[192,256]{1,0:T(8,128)S(1)}, f32[192,256]{1,0:T(8,128)S(1)}, u32[]{:S(2)}, u32[]{:S(2)}) collective-permute-start(f32[192,256]{1,0:T(8,128)S(1)} %get-tuple-element.30), channel_id=1, source_target_pairs={{0,2},{1,3},{2,0},{3,1},{4,6},{5,7},{6,4},{7,5},{8,10},{9,11},{10,... | collective-permute-start | bytes 589832 | tf_op jit(solution)/shard_map/ppermute | solution.py:475
  8.9 0.0 collective-permute-start.2
  8.9 0.0 collective-permute-start.3
  8.9 1.2 %collective-permute-done.3.other_ref = f32[2,2]{1,0:T(2,128)S(1)} collective-permute-done((f32[2,2]{1,0:T(2,128)S(1)}, f32[2,2]{1,0:T(2,128)S(1)}, u32[]{:S(2)}, u32[]{:S(2)}) %collective-permute-start.3) | collective-permute-done | bytes 48 | tf_op jit(solution)/shard_map/ppermute | solution.py:485
  10.0 12.8 %shard_map.78 = (f32[2,2,1,384,192]{4,3,2,1,0:T(8,128)S(1)}, f32[2,2,1,384,192]{4,3,2,1,0:T(8,128)S(1)}, f32[2,2,4,192,192]{4,3,2,1,0:T(8,128)S(1)}, f32[2,192,192]{2,1,0:T(8,128)S(1)}, f32[2,192,192]{2,1,0:T(8,128)S(1)}) custom-call(s32[3]{0:T(128)S(1)} %pad_add_fusion.ids_ref, f32[2,2]{1,0:T(2,128)S(1)} %collective-permute-done.3.other_ref, s32[2]{0:T(128)} %kind_hbm.3, ...), custom_call_target="tpu_custom_call" | custom-call | flops 21233664000 | bytes 7668496 | tf_op jit(solution)/shard_map/pallas_call | solution.py:394
  22.8 2.9 %shard_map.79 = (f32[2,768,192]{2,1,0:T(8,128)S(1)}, f32[2,768,192]{2,1,0:T(8,128)S(1)}, f32[2,768,192]{2,1,0:T(8,128)S(1)}) custom-call(s32[3]{0:T(128)S(1)} %pad_add_fusion.ids_ref, f32[2,2,4,192,192]{4,3,2,1,0:T(8,128)S(1)} %get-tuple-element.33.slab_ref, f32[2,192,192]{2,1,0:T(8,128)S(1)} %get-tuple-element.34.gap_ref, ...), custom_call_target="tpu_custom_call" | custom-call | flops 3538944000 | bytes 6193152 | tf_op jit(solution)/shard_map/pallas_call | solution.py:394
  25.8 0.0 collective-permute-done.refs_1_
  25.8 0.0 collective-permute-done.1.refs_2_
  25.8 0.0 collective-permute-done.2.refs_3_
  25.8 0.8 %shard_map.80 = (f32[2,192,256]{2,1,0:T(8,128)S(1)}, f32[2,192,256]{2,1,0:T(8,128)S(1)}) custom-call(s32[3]{0:T(128)S(1)} %pad_add_fusion.ids_ref, f32[192,256]{1,0:T(8,128)S(1)} %get-tuple-element.28.refs_0_, f32[192,256]{1,0:T(8,128)S(1)} %collective-permute-done.refs_1_, f32[192,256]{1,0:T(8,128)S(1)} %collective-permute-done.1.refs_2_, ...), custom_call_target="tpu_custom_call" | custom-call | bytes 1572864 | tf_op jit(solution)/shard_map/pallas_call | solution.py:394
  26.6 0.2 collective-permute-start.4
  26.8 1.7 %collective-permute-start.5 = (f32[2,192,192]{2,1,0:T(8,128)S(1)}, f32[2,192,192]{2,1,0:T(8,128)S(1)}, u32[]{:S(2)}, u32[]{:S(2)}) collective-permute-start(f32[2,192,192]{2,1,0:T(8,128)S(1)} %get-tuple-element.35.refs_0_.onward), channel_id=1, source_target_pairs={{0,8},{4,12},{8,0},{12,4},{1,9},{5,13},{9,1},{13,5},{2,10},{6,14},... | collective-permute-start | bytes 884744 | tf_op jit(solution)/shard_map/ppermute | solution.py:498
  28.5 0.0 collective-permute-done.4.got
  28.5 2.9 %shard_map.81 = (f32[2,4,192,64]{3,2,1,0:T(8,128)S(1)}, f32[192,128]{1,0:T(8,128)S(1)}) custom-call(s32[3]{0:T(128)S(1)} %pad_add_fusion.ids_ref, f32[2,192,256]{2,1,0:T(8,128)S(1)} %get-tuple-element.37.kept, f32[2,192,256]{2,1,0:T(8,128)S(1)} %collective-permute-done.4.got, f32[2,2,1,384,192]{4,3,2,1,0:T(8,128)S(1)} %get-tuple-element.39.slab_d, ...), custom_call_target="tpu_custom_call" | custom-call | bytes 5996544 | tf_op jit(solution)/shard_map/pallas_call | solution.py:394
  31.5 1.6 %collective-permute-start.6 = (f32[192,128]{1,0:T(8,128)S(1)}, f32[192,128]{1,0:T(8,128)S(1)}, u32[]{:S(2)}, u32[]{:S(2)}) collective-permute-start(f32[192,128]{1,0:T(8,128)S(1)} %get-tuple-element.43.end), channel_id=1, source_target_pairs={{0,8},{4,12},{8,0},{12,4},{1,9},{5,13},{9,1},{13,5},{2,10},{6,14},... | collective-permute-start | bytes 294920 | tf_op jit(solution)/shard_map/ppermute | solution.py:516
  33.1 5.7 %collective-permute-done.5.arrived = f32[2,192,192]{2,1,0:T(8,128)S(1)} collective-permute-done((f32[2,192,192]{2,1,0:T(8,128)S(1)}, f32[2,192,192]{2,1,0:T(8,128)S(1)}, u32[]{:S(2)}, u32[]{:S(2)}) %collective-permute-start.5) | collective-permute-done | bytes 294944 | tf_op jit(solution)/shard_map/ppermute | solution.py:498
  38.8 3.4 %shard_map.82 = (f32[2,768,64]{2,1,0:T(8,128)S(1)}, f32[2,192,192]{2,1,0:T(8,128)S(1)}, f32[192,128]{1,0:T(8,128)S(1)}) custom-call(f32[2,4,192,64]{3,2,1,0:T(8,128)S(1)} %get-tuple-element.42.slabs, f32[192,128]{1,0:T(8,128)S(1)} %get-tuple-element.43.end, f32[2,768,192]{2,1,0:T(8,128)S(1)} %get-tuple-element.36.refs_4_.pair_d, ...), custom_call_target="tpu_custom_call" | custom-call | flops 7077888000 | bytes 4227072 | tf_op jit(solution)/shard_map/pallas_call | solution.py:394
  42.2 0.0 collective-permute-done.6.crossed
  42.2 2.0 %shard_map.83 = (f32[2,192,128]{2,1,0:T(8,128)S(1)}, f32[2,192,128]{2,1,0:T(8,128)S(1)}) custom-call(s32[3]{0:T(128)S(1)} %pad_add_fusion.ids_ref, f32[2,768,64]{2,1,0:T(8,128)S(1)} %get-tuple-element.44.inner, f32[2,768,192]{2,1,0:T(8,128)S(1)} %get-tuple-element.45.answer, f32[2,192,192]{2,1,0:T(8,128)S(1)} %get-tuple-element.46.gap, ...), custom_call_target="tpu_custom_call" | custom-call | bytes 2457600 | tf_op jit(solution)/shard_map/pallas_call | solution.py:394
  44.2 0.1 collective-permute-start.7
  44.3 1.4 %collective-permute-done.7.got = f32[2,192,128]{2,1,0:T(8,128)S(1)} collective-permute-done((f32[2,192,128]{2,1,0:T(8,128)S(1)}, f32[2,192,128]{2,1,0:T(8,128)S(1)}, u32[]{:S(2)}, u32[]{:S(2)}) %collective-permute-start.7) | collective-permute-done | bytes 196640 | tf_op jit(solution)/shard_map/ppermute | solution.py:535
  45.7 0.7 %shard_map.84 = (f32[192,128]{1,0:T(8,128)S(1)}, f32[192,128]{1,0:T(8,128)S(1)}, f32[192,128]{1,0:T(8,128)S(1)}, f32[192,128]{1,0:T(8,128)S(1)}) custom-call(s32[3]{0:T(128)S(1)} %pad_add_fusion.ids_ref, f32[2,192,128]{2,1,0:T(8,128)S(1)} %get-tuple-element.48.kept, f32[2,192,128]{2,1,0:T(8,128)S(1)} %collective-permute-done.7.got), custom_call_target="tpu_custom_call" | custom-call | bytes 786432 | tf_op jit(solution)/shard_map/pallas_call | solution.py:394
  46.4 1.0 %collective-permute-start.8 = (f32[192,128]{1,0:T(8,128)S(1)}, f32[192,128]{1,0:T(8,128)S(1)}, u32[]{:S(2)}, u32[]{:S(2)}) collective-permute-start(f32[192,128]{1,0:T(8,128)S(1)} %get-tuple-element.51), channel_id=1, source_target_pairs={{0,1},{1,0},{2,3},{3,2},{4,5},{5,4},{6,7},{7,6},{8,9},{9,8},{10,11... | collective-permute-start | bytes 294920 | tf_op jit(solution)/shard_map/ppermute | solution.py:475
  47.4 3.5 %collective-permute-start.9 = (f32[192,128]{1,0:T(8,128)S(1)}, f32[192,128]{1,0:T(8,128)S(1)}, u32[]{:S(2)}, u32[]{:S(2)}) collective-permute-start(f32[192,128]{1,0:T(8,128)S(1)} %get-tuple-element.52), channel_id=1, source_target_pairs={{0,2},{1,3},{2,0},{3,1},{4,6},{5,7},{6,4},{7,5},{8,10},{9,11},{10,... | collective-permute-start | bytes 294920 | tf_op jit(solution)/shard_map/ppermute | solution.py:475
  50.8 0.0 collective-permute-start.10
  50.8 0.4 collective-permute-done.8.refs_1_
  51.3 7.4 %collective-permute-done.9.refs_2_ = f32[192,128]{1,0:T(8,128)S(1)} collective-permute-done((f32[192,128]{1,0:T(8,128)S(1)}, f32[192,128]{1,0:T(8,128)S(1)}, u32[]{:S(2)}, u32[]{:S(2)}) %collective-permute-start.9) | collective-permute-done | bytes 98336 | tf_op jit(solution)/shard_map/ppermute | solution.py:475
  58.7 0.0 collective-permute-done.10.refs_3_
  58.7 1.4 %shard_map.85 = (f32[1,1,192,256]{3,2,1,0:T(8,128)}, f32[1,1,192,256]{3,2,1,0:T(8,128)}) custom-call(s32[3]{0:T(128)S(1)} %pad_add_fusion.ids_ref, f32[192,128]{1,0:T(8,128)S(1)} %get-tuple-element.50.refs_0_, f32[192,128]{1,0:T(8,128)S(1)} %collective-permute-done.8.refs_1_, f32[192,128]{1,0:T(8,128)S(1)} %collective-permute-done.9.refs_2_, ...), custom_call_target="tpu_custom_call" | custom-call | bytes 786432 | tf_op jit(solution)/shard_map/pallas_call | solution.py:394
Async XLA Ops:
  3.2 22.6 %collective-permute-start = (f32[192,256]{1,0:T(8,128)S(1)}, f32[192,256]{1,0:T(8,128)S(1)}, u32[]{:S(2)}, u32[]{:S(2)}) collective-permute-start(f32[192,256]{1,0:T(8,128)S(1)} %get-tuple-element.29), channel_id=1, source_target_pairs={{0,1},{1,0},{2,3},{3,2},{4,5},{5,4},{6,7},{7,6},{8,9},{9,8},{10,11... | collective-permute-start | bytes 589832 | tf_op jit(solution)/shard_map/ppermute | solution.py:475
  6.3 19.5 %collective-permute-start.1 = (f32[192,256]{1,0:T(8,128)S(1)}, f32[192,256]{1,0:T(8,128)S(1)}, u32[]{:S(2)}, u32[]{:S(2)}) collective-permute-start(f32[192,256]{1,0:T(8,128)S(1)} %get-tuple-element.30), channel_id=1, source_target_pairs={{0,2},{1,3},{2,0},{3,1},{4,6},{5,7},{6,4},{7,5},{8,10},{9,11},{10,... | collective-permute-start | bytes 589832 | tf_op jit(solution)/shard_map/ppermute | solution.py:475
  8.9 16.9 %collective-permute-start.2 = (f32[192,256]{1,0:T(8,128)S(1)}, f32[192,256]{1,0:T(8,128)S(1)}, u32[]{:S(2)}, u32[]{:S(2)}) collective-permute-start(f32[192,256]{1,0:T(8,128)S(1)} %get-tuple-element.31), channel_id=1, source_target_pairs={{0,3},{1,2},{2,1},{3,0},{4,7},{5,6},{6,5},{7,4},{8,11},{9,10},{10,... | collective-permute-start | bytes 589832 | tf_op jit(solution)/shard_map/ppermute | solution.py:475
  8.9 1.2 %collective-permute-start.3 = (f32[2,2]{1,0:T(2,128)S(1)}, f32[2,2]{1,0:T(2,128)S(1)}, u32[]{:S(2)}, u32[]{:S(2)}) collective-permute-start(f32[2,2]{1,0:T(2,128)S(1)} %get-tuple-element.32), channel_id=1, source_target_pairs={{0,4},{4,0},{8,12},{12,8},{1,5},{5,1},{9,13},{13,9},{2,6},{6,2},{1... | collective-permute-start | bytes 56 | tf_op jit(solution)/shard_map/ppermute | solution.py:485
  26.6 2.0 %collective-permute-start.4 = (f32[2,192,256]{2,1,0:T(8,128)S(1)}, f32[2,192,256]{2,1,0:T(8,128)S(1)}, u32[]{:S(2)}, u32[]{:S(2)}) collective-permute-start(f32[2,192,256]{2,1,0:T(8,128)S(1)} %get-tuple-element.38), channel_id=1, source_target_pairs={{0,4},{4,0},{8,12},{12,8},{1,5},{5,1},{9,13},{13,9},{2,6},{6,2},{1... | collective-permute-start | bytes 1179656 | tf_op jit(solution)/shard_map/ppermute | solution.py:508
  26.8 12.0 %collective-permute-start.5 = (f32[2,192,192]{2,1,0:T(8,128)S(1)}, f32[2,192,192]{2,1,0:T(8,128)S(1)}, u32[]{:S(2)}, u32[]{:S(2)}) collective-permute-start(f32[2,192,192]{2,1,0:T(8,128)S(1)} %get-tuple-element.35.refs_0_.onward), channel_id=1, source_target_pairs={{0,8},{4,12},{8,0},{12,4},{1,9},{5,13},{9,1},{13,5},{2,10},{6,14},... | collective-permute-start | bytes 884744 | tf_op jit(solution)/shard_map/ppermute | solution.py:498
  31.5 10.7 %collective-permute-start.6 = (f32[192,128]{1,0:T(8,128)S(1)}, f32[192,128]{1,0:T(8,128)S(1)}, u32[]{:S(2)}, u32[]{:S(2)}) collective-permute-start(f32[192,128]{1,0:T(8,128)S(1)} %get-tuple-element.43.end), channel_id=1, source_target_pairs={{0,8},{4,12},{8,0},{12,4},{1,9},{5,13},{9,1},{13,5},{2,10},{6,14},... | collective-permute-start | bytes 294920 | tf_op jit(solution)/shard_map/ppermute | solution.py:516
  44.2 1.5 %collective-permute-start.7 = (f32[2,192,128]{2,1,0:T(8,128)S(1)}, f32[2,192,128]{2,1,0:T(8,128)S(1)}, u32[]{:S(2)}, u32[]{:S(2)}) collective-permute-start(f32[2,192,128]{2,1,0:T(8,128)S(1)} %get-tuple-element.49), channel_id=1, source_target_pairs={{0,4},{4,0},{8,12},{12,8},{1,5},{5,1},{9,13},{13,9},{2,6},{6,2},{1... | collective-permute-start | bytes 589832 | tf_op jit(solution)/shard_map/ppermute | solution.py:535
  46.4 4.9 %collective-permute-start.8 = (f32[192,128]{1,0:T(8,128)S(1)}, f32[192,128]{1,0:T(8,128)S(1)}, u32[]{:S(2)}, u32[]{:S(2)}) collective-permute-start(f32[192,128]{1,0:T(8,128)S(1)} %get-tuple-element.51), channel_id=1, source_target_pairs={{0,1},{1,0},{2,3},{3,2},{4,5},{5,4},{6,7},{7,6},{8,9},{9,8},{10,11... | collective-permute-start | bytes 294920 | tf_op jit(solution)/shard_map/ppermute | solution.py:475
  47.4 11.3 %collective-permute-start.9 = (f32[192,128]{1,0:T(8,128)S(1)}, f32[192,128]{1,0:T(8,128)S(1)}, u32[]{:S(2)}, u32[]{:S(2)}) collective-permute-start(f32[192,128]{1,0:T(8,128)S(1)} %get-tuple-element.52), channel_id=1, source_target_pairs={{0,2},{1,3},{2,0},{3,1},{4,6},{5,7},{6,4},{7,5},{8,10},{9,11},{10,... | collective-permute-start | bytes 294920 | tf_op jit(solution)/shard_map/ppermute | solution.py:475
  50.8 7.9 %collective-permute-start.10 = (f32[192,128]{1,0:T(8,128)S(1)}, f32[192,128]{1,0:T(8,128)S(1)}, u32[]{:S(2)}, u32[]{:S(2)}) collective-permute-start(f32[192,128]{1,0:T(8,128)S(1)} %get-tuple-element.53), channel_id=1, source_target_pairs={{0,3},{1,2},{2,1},{3,0},{4,7},{5,6},{6,5},{7,4},{8,11},{9,10},{10,... | collective-permute-start | bytes 294920 | tf_op jit(solution)/shard_map/ppermute | solution.py:475

commit v5 on v4

--- a/solution.py
+++ b/solution.py
@@ -142,9 +142,8 @@
     return tuple(column * blocks[b] * row for b in range(4))
 
 
-def slabs_kernel(layers, vectors, parts, edge, ids_ref, other_ref, kind_hbm, thick_hbm, table_hbm, decay_hbm, *refs):
-    *outs, sum_ref, power_ref, coupling_ref, kind_ref, thick_ref, blocks_ref, decay_ref, sems, block_sems = refs
-    parity = ids_ref[1]
+def slabs_kernel(layers, vectors, parts, edge, ids_ref, other_ref, table_ref, kind_hbm, thick_hbm, decay_hbm, *refs):
+    *outs, sum_ref, power_ref, coupling_ref, kind_ref, thick_ref, decay_ref, sems = refs
     small = [
         pltpu.make_async_copy(kind_hbm, kind_ref, sems.at[0]),
         pltpu.make_async_copy(thick_hbm, thick_ref, sems.at[1]),
@@ -152,25 +151,17 @@
     ]
     for copy in small:
         copy.start()
-    small[0].wait()
-    large = {}
-    for i in range(layers):
-        for j in range(PAIR):
-            kind = jnp.where(parity == j, kind_ref[i], other_ref[0, i].astype(jnp.int32))
-            large[j, i] = pltpu.make_async_copy(table_hbm.at[kind], blocks_ref.at[j, i], block_sems.at[j, i])
-            large[j, i].start()
-    for copy in small[1:]:
+    for copy in small:
         copy.wait()
-    for i in range(layers):
-        for j in range(PAIR):
-            large[j, i].wait()
     scratch = sum_ref, power_ref, coupling_ref
     in_batches(vectors, lambda start, size: slabs_of(
-        layers, parts, start, size, edge, ids_ref, other_ref, thick_ref, blocks_ref, decay_ref, outs, scratch))
-
-
-def slabs_of(layers, parts, start, size, edge, ids_ref, other_ref, thick_ref, blocks_ref, decay_ref, outs, scratch):
-    slab_d, slab_u, slab_ref, gap_ref, *onward = outs
+        layers, parts, start, size, edge, ids_ref, other_ref, kind_ref, thick_ref, table_ref, decay_ref, outs, scratch))
+
+
+def slabs_of(layers, parts, start, size, edge, ids_ref, other_ref, kind_ref, thick_ref, table_ref, decay_ref, outs, scratch):
+    slab_d, slab_u, slab_ref, gap_ref, *edges = outs
+    if edge:
+        onward, end_d, end_u = edges
     m = decay_ref.shape[-1]
     parity, top = ids_ref[1], ids_ref[2] == 0
     keys = [(k, j) for k in range(size) for j in range(PAIR)]
@@ -179,8 +170,9 @@
     for k, j in keys:
         factor = pick(factors, (start + k) * PAIR + parity)
         for i in range(layers):
+            kind = jnp.where(parity == j, kind_ref[i], other_ref[0, i].astype(jnp.int32))
             thick = jnp.where(parity == j, thick_ref[i], other_ref[1, i])
-            segments[k, j, i] = segment(factor, thick, [blocks_ref[j, i, b] for b in range(4)], decay_ref[...])
+            segments[k, j, i] = segment(factor, thick, [table_ref[kind, b] for b in range(4)], decay_ref[...])
     slabs = {(k, j): segments[k, j, 0] for k, j in keys}
     for i in range(1, layers):
         couplings = [dot(slabs[k, j][3], segments[k, j, i][0]) for k, j in keys]
@@ -210,7 +202,10 @@
             first = dot(jnp.where(top, above[3], above[2]), jnp.where(top, below[2], below[0]))
             left = jnp.where(top, below[1], first)
             right = jnp.where(top, first, above[1])
-            onward[0][start + k] = jnp.where(top, below[3], above[0]) + dot(left, dot(gap, right))
+            through = dot(left, gap)
+            onward[start + k] = jnp.where(top, below[3], above[0]) + dot(through, right)
+            end_d[start + k] = through
+            end_u[start + k] = dot(through, above[3]) + jnp.where(top, 0.0, above[2])
 
 
 def maps_kernel(vectors, edge, ids_ref, slab_ref, gap_ref, *refs):
@@ -247,7 +242,7 @@
 
 
 def pack_kernel(share, parts, ids_ref, drive_hbm, position_hbm, kind_hbm, thick_hbm, *outs):
-    *blocks, described, held, drive_ref, position_ref, kind_ref, thick_ref, sems, drive_sems = outs
+    *blocks, described, drive_ref, position_ref, kind_ref, thick_ref, sems, drive_sems = outs
     layers = drive_hbm.shape[1]
     small = [
         pltpu.make_async_copy(position_hbm, position_ref, sems.at[0]),
@@ -269,58 +264,72 @@
     for i in range(layers):
         described[0, i] = kind_ref[i].astype(f32)
         described[1, i] = thick_ref[i]
-    for copy in large.values():
-        copy.wait()
-    for q in range(parts):
-        span = slice(q * share, (q + 1) * share)
-        held[q] = jnp.concatenate(
-            [drive_ref[i, d, :, span] * envelope[:, span] for i in range(layers) for d in range(2)], axis=1
-        )
-    for step in range(parts):
-        blocks[step][...] = held[cell ^ step]
-
-
-def transform_kernel(parts, ids_ref, *refs):
-    blocks, (_, kept, sent) = refs[:parts], refs[parts:]
-    place, parity = ids_ref[0], ids_ref[1]
+    for i in range(layers):
+        for d in range(2):
+            large[i, d].wait()
+        loaded = [drive_ref[i, d] * envelope for d in range(2)]
+        for here in range(parts):
+            @pl.when(cell == here)
+            def _():
+                for step in range(parts):
+                    q = here ^ step
+                    blocks[step][:, 2 * i * share:2 * (i + 1) * share] = jnp.concatenate(
+                        [side[:, q * share:(q + 1) * share] for side in loaded], axis=1
+                    )
+
+
+def transformed(blocks, ids_ref, side, parts):
+    place = ids_ref[0]
     loaded = [b[...] for b in blocks]
     cells = [place ^ step for step in range(parts)]
-    for side, out in ((parity, kept), (1 - parity, sent)):
-        for i in range(out.shape[0]):
-            wave = PAIR * i + side
-            total = cas(wave, cells[0], parts) * loaded[0]
-            for step in range(1, parts):
-                total = total + cas(wave, cells[step], parts) * loaded[step]
-            out[i] = total
-
-
-def sources_kernel(layers, share, vectors, edge, ids_ref, kept, got, slab_d, slab_u, pair_d, pair_u, slabs, *refs):
-    m = kept.shape[1]
-    parity, group = ids_ref[1], ids_ref[2]
-    held = refs[-1]
+    for i in range(parts // PAIR):
+        wave = PAIR * i + side
+        total = cas(wave, cells[0], parts) * loaded[0]
+        for step in range(1, parts):
+            total = total + cas(wave, cells[step], parts) * loaded[step]
+        yield total
+
+
+def transform_kernel(parts, ids_ref, *refs):
+    blocks, sent = refs[:parts], refs[-1]
+    for i, total in enumerate(transformed(blocks, ids_ref, 1 - ids_ref[1], parts)):
+        sent[i] = total
+
+
+def through_slab(layers, share, block, k, j, slab_d, slab_u):
+    m = block.shape[0]
+    up, down = block[:, 0:share], block[:, share:2 * share]
+    for i in range(1, layers):
+        at = 2 * i * share
+        up_b, down_b = block[:, at:at + share], block[:, at + share:at + 2 * share]
+        both = dot(slab_d[k, j, i - 1], down) + dot(slab_u[k, j, i - 1], up_b)
+        up, down = up + both[0:m], down_b + both[m:]
+    return up, down
+
+
+def near_kernel(layers, share, parts, ids_ref, *refs):
+    blocks, (slab_d, slab_u, near) = refs[:parts], refs[parts:]
+    parity = ids_ref[1]
+    for k, block in enumerate(transformed(blocks, ids_ref, parity, parts)):
+        near[k, 0], near[k, 1] = through_slab(layers, share, block, k, parity, slab_d, slab_u)
+
+
+def far_kernel(layers, share, vectors, edge, ids_ref, near, got, slab_d, slab_u, *refs):
+    parity, top = ids_ref[1], ids_ref[2] == 0
+    slabs = refs[2] if edge else refs[0]
     for k in range(vectors):
-        held[parity, k] = kept[k]
-        held[1 - parity, k] = got[k]
-    ends = []
-    for k in range(vectors):
-        pair = []
-        for j in range(PAIR):
-            block = held[j, k]
-            up, down = block[:, 0:share], block[:, share:2 * share]
-            for i in range(1, layers):
-                at = 2 * i * share
-                up_b, down_b = block[:, at:at + share], block[:, at + share:at + 2 * share]
-                both = dot(slab_d[k, j, i - 1], down) + dot(slab_u[k, j, i - 1], up_b)
-                up, down = up + both[0:m], down_b + both[m:]
-            slabs[k, 2 * j] = up
-            slabs[k, 2 * j + 1] = down
-            pair.append((up, down))
-        if edge:
-            rows = pl.ds(pl.multiple_of(jnp.where(group == 0, 3 * m, 0), 8), m)
-            own = jnp.where(group == 0, pair[1][1], pair[0][0])
-            ends.append(own + dot(pair_d[k, rows], pair[0][1]) + dot(pair_u[k, rows], pair[1][0]))
+        up, down = through_slab(layers, share, got[k], k, 1 - parity, slab_d, slab_u)
+        slabs[k, 2 * parity] = near[k, 0]
+        slabs[k, 2 * parity + 1] = near[k, 1]
+        slabs[k, 2 * (1 - parity)] = up
+        slabs[k, 2 * (1 - parity) + 1] = down
     if edge:
-        refs[0][...] = jnp.concatenate(ends, axis=1)
+        end_d, end_u, _, end = refs
+        ends = []
+        for k in range(vectors):
+            own = jnp.where(top, slabs[k, 3], slabs[k, 0])
+            ends.append(own + dot(end_d[k], slabs[k, 1]) + dot(end_u[k], slabs[k, 2]))
+        end[...] = jnp.concatenate(ends, axis=1)
 
 
 def inner_kernel(vectors, slabs, pair_d, pair_u, inner):
@@ -343,18 +352,25 @@
         gap[k] = gaps[k]
 
 
-def fields_kernel(vectors, ids_ref, inner, answer, gap, bounced, crossed, kept, sent, held):
+def rows_of(j, k, inner, answer, inward):
     m = inner.shape[1] // 4
+    rows = pl.ds(pl.multiple_of(2 * j * m, 8), 2 * m)
+    both = inner[k, rows] + dot(answer[k, rows], inward)
+    return jnp.concatenate([both[0:m], both[m:]], axis=1)
+
+
+def sent_kernel(vectors, ids_ref, inner, answer, gate, bounced, crossed, sent, inward_ref):
     share = inner.shape[2]
-    parity = ids_ref[1]
     inward = bounced[...] + crossed[...]
     for k in range(vectors):
-        rows = inner[k] + dot(answer[k], dot(gap[k], inward[:, k * share:(k + 1) * share]))
-        for j in range(PAIR):
-            held[j, k] = jnp.concatenate([rows[2 * j * m:(2 * j + 1) * m], rows[(2 * j + 1) * m:(2 * j + 2) * m]], axis=1)
+        value = dot(gate[k], inward[:, k * share:(k + 1) * share])
+        inward_ref[k] = value
+        sent[k] = rows_of(1 - ids_ref[1], k, inner, answer, value)
+
+
+def kept_kernel(vectors, ids_ref, inner, answer, inward_ref, kept):
     for k in range(vectors):
-        kept[k] = held[parity, k]
-        sent[k] = held[1 - parity, k]
+        kept[k] = rows_of(ids_ref[1], k, inner, answer, inward_ref[k])
 
 
 def return_kernel(parts, ids_ref, kept, got, *blocks):
@@ -372,13 +388,13 @@
 
 
 def unpack_kernel(share, parts, ids_ref, *refs):
-    blocks, (up, down, held) = refs[:parts], refs[parts:]
-    place = ids_ref[0]
-    for step in range(parts):
-        held[place ^ step] = blocks[step][...]
-    for side, out in enumerate((up, down)):
-        span = slice(side * share, (side + 1) * share)
-        out[0, 0] = jnp.concatenate([held[q][:, span] for q in range(parts)], axis=1)
+    blocks, outs = refs[:parts], refs[parts:]
+    for here in range(parts):
+        @pl.when(ids_ref[0] == here)
+        def _():
+            for side, out in enumerate(outs):
+                span = slice(side * share, (side + 1) * share)
+                out[0, 0] = jnp.concatenate([blocks[here ^ q][:, span] for q in range(parts)], axis=1)
 
 
 def vmem():
@@ -478,51 +494,49 @@
     *packed, described = call(
         functools.partial(pack_kernel, share, parts),
         [ids], [], [(m, width)] * parts,
-        [(parts, m, width), (layers, 2, m, columns), pltpu.VMEM((1, columns), jnp.int32), pltpu.SMEM((layers,), jnp.int32),
+        [(layers, 2, m, columns), pltpu.VMEM((1, columns), jnp.int32), pltpu.SMEM((layers,), jnp.int32),
          pltpu.SMEM((layers,), f32), dma((3,)), dma((layers, 2))],
-        small=[(2, layers)], far=[drive, positions[None, :], materials, thickness],
+        1000 * m**3, small=[(2, layers)], far=[drive, positions[None, :], materials, thickness],
     )
     other = lax.ppermute(described, "stack", partner)
     arrived = deal(packed)
 
     squares = [(vectors * PAIR, m, m)] * 3
-    slab_d, slab_u, slab, gap, *onward = call(
+    slab_d, slab_u, slab, gap, *edges = call(
         functools.partial(slabs_kernel, layers, vectors, parts, edge),
-        [ids, other], [],
-        [(vectors, PAIR, layers - 1, 2 * m, m)] * 2 + [(vectors, PAIR, 4, m, m), (vectors, m, m)] + [(vectors, m, m)] * edge,
-        squares + [pltpu.SMEM((layers,), jnp.int32), pltpu.SMEM((layers,), f32), (PAIR, layers, 4, m, m), (1, m),
-                   dma((3,)), dma((PAIR, layers))],
-        3000 * m**3, 32, far=[materials, thickness, table, decay[None, :]],
+        [ids, other], [table],
+        [(vectors, PAIR, layers - 1, 2 * m, m)] * 2 + [(vectors, PAIR, 4, m, m), (vectors, m, m)] + [(vectors, m, m)] * (3 * edge),
+        squares + [pltpu.SMEM((layers,), jnp.int32), pltpu.SMEM((layers,), f32), (1, m), dma((3,))],
+        3000 * m**3, 32, far=[materials, thickness, decay[None, :]],
     )
     if edge:
-        opposite = lax.ppermute(onward[0], "stack", across)
+        opposite = lax.ppermute(edges[0], "stack", across)
+
+    (sent,) = call(functools.partial(transform_kernel, parts), [ids], arrived, [(vectors, m, width)], (), after=[gap])
+    got = lax.ppermute(sent, "stack", partner)
+    (near,) = call(
+        functools.partial(near_kernel, layers, share, parts),
+        [ids], [*arrived, slab_d, slab_u], [(vectors, 2, m, share)], (),
+    )
+    slabs, *end = call(
+        functools.partial(far_kernel, layers, share, vectors, edge),
+        [ids], [near, got, slab_d, slab_u, *edges[1:]],
+        [(vectors, 4, m, share)] + [(m, vectors * share)] * edge, (),
+    )
     pair_d, pair_u, *ends = call(
         functools.partial(maps_kernel, vectors, edge),
-        [ids], [slab, gap], [(vectors, 4 * m, m)] * (3 if edge else 4), (), 500 * m**3, after=onward,
-    )
-
-    kept, sent = call(
-        functools.partial(transform_kernel, parts),
-        [ids], arrived, [(vectors, m, width)] * 2, (), after=[pair_d],
-    )
-    got = lax.ppermute(sent, "stack", partner)
-    slabs, *end = call(
-        functools.partial(sources_kernel, layers, share, vectors, edge),
-        [ids], [kept, got, slab_d, slab_u, pair_d, pair_u],
-        [(vectors, 4, m, share)] + ([(m, vectors * share)] if edge else []),
-        [(PAIR, vectors, m, width)],
+        [ids], [slab, gap], [(vectors, 4 * m, m)] * (3 if edge else 4), (), 500 * m**3, after=end,
     )
     if edge:
         crossed = lax.ppermute(end[0], "stack", across)
         inner, gate, bounced = call(
             functools.partial(boundary_kernel, vectors),
-            [], [slabs, end[0], pair_d, pair_u, onward[0], opposite],
+            [], [slabs, end[0], pair_d, pair_u, edges[0], opposite],
             [(vectors, 4 * m, share), (vectors, m, m), (m, vectors * share)], squares, 1000 * m**3,
         )
-        kept, sent = call(
-            functools.partial(fields_kernel, vectors),
-            [ids], [inner, ends[0], gate, bounced, crossed],
-            [(vectors, m, 2 * share)] * 2, [(PAIR, vectors, m, 2 * share)],
+        sent, inward = call(
+            functools.partial(sent_kernel, vectors), [ids], [inner, ends[0], gate, bounced, crossed],
+            [(vectors, m, 2 * share), (vectors, m, share)], (),
         )
     else:
         (inner,) = call(
@@ -530,15 +544,20 @@
         )
         rows = chain(groups, group, depth, ends[0], ends[1], inner)
         sides = [jnp.concatenate([rows[:, 2 * j * m:(2 * j + 1) * m], rows[:, (2 * j + 1) * m:(2 * j + 2) * m]], 2) for j in range(PAIR)]
-        kept = jnp.where(parity == 0, sides[0], sides[1])
         sent = jnp.where(parity == 0, sides[1], sides[0])
     got = lax.ppermute(sent, "stack", partner)
+    if edge:
+        (kept,) = call(
+            functools.partial(kept_kernel, vectors), [ids], [inner, ends[0], inward], [(vectors, m, 2 * share)], (),
+        )
+    else:
+        kept = jnp.where(parity == 0, sides[0], sides[1])
 
     blocks = call(functools.partial(return_kernel, parts), [ids], [kept, got], [(m, 2 * share)] * parts, ())
     blocks = deal(blocks)
     return call(
         functools.partial(unpack_kernel, share, parts),
-        [ids], blocks, [(1, 1, m, columns)] * 2, [(parts, m, 2 * share)],
+        [ids], blocks, [(1, 1, m, columns)] * 2, (),
     )
 
 

time: 60.3 us -> 59.7 us (0.990)
  waiting for transfers between devices: 16.2 us -> 15.3 us
    ppermute x6, waiting for transfers between devices: 7.86 us -> 10.4 us  [deal(): lax.ppermute(blocks[step], 'bloch', [(i, i ^ step) for i in range(parts)])]
    ppermute x1, waiting for transfers between devices: 5.7 us -> 3.37 us  [shards(): opposite = lax.ppermute(edges[0], 'stack', across)]
    ppermute x6, starting transfers between devices: 10.2 us -> 11.7 us  [deal(): lax.ppermute(blocks[step], 'bloch', [(i, i ^ step) for i in range(parts)])]
    ppermute x2, waiting for transfers between devices: 1.43 us -> 0.35 us  [shards(): got = lax.ppermute(sent, 'stack', partner)]
    ppermute x1, starting transfers between devices: 1.62 us -> 0.58 us  [shards(): crossed = lax.ppermute(end[0], 'stack', across)]
    pallas_call x9 -> x11, Pallas kernels: 29.3 us -> 29.4 us  [call(): pl.pallas_call(kernel, out_shape=tuple((jax.ShapeDtypeStruct(s, f32) for...]
  transfers between devices with their start and end apart: 11 -> 11, of which waited for: 5 -> 6; matrix products, arithmetic and copies ran while one was open for 0% -> 0% of each run, Pallas kernels for 37% -> 37%
where the time goes in v5:
time: 59.7 us; the launch traced here: 59.6 us
  Pallas kernels  29.4 us (49%)
  waiting for transfers between devices  15.3 us (26%)
  starting transfers between devices  14 us (23%)
  between operations  0.76 us (1%)
    pallas_call x11, Pallas kernels, call(): pl.pallas_call(kernel, out_shape=tuple((jax.ShapeDtypeStruct(s, f32) for...  29.4 us
    ppermute x6, starting transfers between devices, deal(): lax.ppermute(blocks[step], 'bloch', [(i, i ^ step) for i in range(parts)])  11.7 us
    ppermute x6, waiting for transfers between devices, deal(): lax.ppermute(blocks[step], 'bloch', [(i, i ^ step) for i in range(parts)])  10.4 us
    ppermute x1, waiting for transfers between devices, shards(): opposite = lax.ppermute(edges[0], 'stack', across)  3.37 us
    ppermute x1, starting transfers between devices, shards(): opposite = lax.ppermute(edges[0], 'stack', across)  1.58 us
  transfers between devices with their start and end apart: 11, of which 6 were waited for; matrix products, arithmetic and copies ran while one was open for 0% of the time, Pallas kernels for 37%

profile of v5, /device:TPU:0, one launch (start us, length us, event | category | flops | bytes accessed | tf_op | source)
XLA Modules:
  0.0 59.6 jit_solution(9613462589281248749)
XLA Ops:
  0.6 0.1 pad_add_fusion.ids_ref
  0.7 0.0 copy-start
  0.7 2.9 %shard_map.77 = (f32[192,256]{1,0:T(8,128)S(1)}, f32[192,256]{1,0:T(8,128)S(1)}, f32[192,256]{1,0:T(8,128)S(1)}, f32[192,256]{1,0:T(8,128)S(1)}, f32[2,2]{1,0:T(2,128)S(1)}) custom-call(s32[3]{0:T(128)S(1)} %pad_add_fusion.ids_ref, f32[1,2,2,192,256]{4,3,2,1,0:T(8,128)} %drive_hbm.1, s32[1,256]{1,0:T(1,128)} %bitcast.5, s32[2]{0:T(128)} %kind_hbm.3, f32[2]{0:T(128)} %thick_hbm.3), custom_call_target="tpu_custom_call" | custom-call | flops 7077888000 | bytes 1573904 | tf_op jit(solution)/shard_map/pallas_call | solution.py:410
  3.6 3.1 %collective-permute-start = (f32[192,256]{1,0:T(8,128)S(1)}, f32[192,256]{1,0:T(8,128)S(1)}, u32[]{:S(2)}, u32[]{:S(2)}) collective-permute-start(f32[192,256]{1,0:T(8,128)S(1)} %get-tuple-element.29), channel_id=1, source_target_pairs={{0,1},{1,0},{2,3},{3,2},{4,5},{5,4},{6,7},{7,6},{8,9},{9,8},{10,11... | collective-permute-start | bytes 589832 | tf_op jit(solution)/shard_map/ppermute | solution.py:491
  6.8 2.6 %collective-permute-start.1 = (f32[192,256]{1,0:T(8,128)S(1)}, f32[192,256]{1,0:T(8,128)S(1)}, u32[]{:S(2)}, u32[]{:S(2)}) collective-permute-start(f32[192,256]{1,0:T(8,128)S(1)} %get-tuple-element.30), channel_id=1, source_target_pairs={{0,2},{1,3},{2,0},{3,1},{4,6},{5,7},{6,4},{7,5},{8,10},{9,11},{10,... | collective-permute-start | bytes 589832 | tf_op jit(solution)/shard_map/ppermute | solution.py:491
  9.3 0.0 collective-permute-start.2
  9.3 0.0 collective-permute-start.3
  9.4 1.2 %collective-permute-done.3.other_ref = f32[2,2]{1,0:T(2,128)S(1)} collective-permute-done((f32[2,2]{1,0:T(2,128)S(1)}, f32[2,2]{1,0:T(2,128)S(1)}, u32[]{:S(2)}, u32[]{:S(2)}) %collective-permute-start.3) | collective-permute-done | bytes 48 | tf_op jit(solution)/shard_map/ppermute | solution.py:501
  10.5 0.0 copy-done
  10.5 11.1 %shard_map.78 = (f32[2,2,1,384,192]{4,3,2,1,0:T(8,128)S(1)}, f32[2,2,1,384,192]{4,3,2,1,0:T(8,128)S(1)}, f32[2,2,4,192,192]{4,3,2,1,0:T(8,128)S(1)}, f32[2,192,1...) custom-call(s32[3]{0:T(128)S(1)} %pad_add_fusion.ids_ref, ...), custom_call_target="tpu_custom_call" | custom-call | flops 21233664000 | bytes 8258320 | tf_op jit(solution)/shard_map/pallas_call | solution.py:410
  21.6 0.0 collective-permute-done.refs_1_
  21.6 2.2 %collective-permute-done.1.refs_2_ = f32[192,256]{1,0:T(8,128)S(1)} collective-permute-done((f32[192,256]{1,0:T(8,128)S(1)}, f32[192,256]{1,0:T(8,128)S(1)}, u32[]{:S(2)}, u32[]{:S(2)}) %collective-permute-start.1) | collective-permute-done | bytes 196640 | tf_op jit(solution)/shard_map/ppermute | solution.py:491
  23.9 0.0 collective-permute-done.2.refs_3_
  23.9 0.7 %shard_map.80 = f32[2,192,256]{2,1,0:T(8,128)S(1)} custom-call(s32[3]{0:T(128)S(1)} %pad_add_fusion.ids_ref, f32[192,256]{1,0:T(8,128)S(1)} %get-tuple-element.28.refs_0_, f32[192,256]{1,0:T(8,128)S(1)} %collective-permute-done.refs_1_, f32[192,256]{1,0:T(8,128)S(1)} %collective-permute-done.1.refs_2_, f32[192,256]{1,0:T(8,128)S(1)} %collective-permute-done.2.refs_3_, ...), custom_call_target="tpu_custom_call" | custom-call | bytes 1179648 | tf_op jit(solution)/shard_map/pallas_call | solution.py:410
  24.5 0.1 collective-permute-start.4
  24.6 1.6 %collective-permute-start.5 = (f32[2,192,192]{2,1,0:T(8,128)S(1)}, f32[2,192,192]{2,1,0:T(8,128)S(1)}, u32[]{:S(2)}, u32[]{:S(2)}) collective-permute-start(f32[2,192,192]{2,1,0:T(8,128)S(1)} %get-tuple-element.43.onward), channel_id=1, source_target_pairs={{0,8},{4,12},{8,0},{12,4},{1,9},{5,13},{9,1},{13,5},{2,10},{6,14},... | collective-permute-start | bytes 884744 | tf_op jit(solution)/shard_map/ppermute | solution.py:513
  26.2 1.5 %shard_map.79.near = f32[2,2,192,64]{3,2,1,0:T(8,128)S(1)} custom-call(s32[3]{0:T(128)S(1)} %pad_add_fusion.ids_ref, f32[192,256]{1,0:T(8,128)S(1)} %get-tuple-element.28.refs_0_, f32[192,256]{1,0:T(8,128)S(1)} %collective-permute-done.refs_1_, f32[192,256]{1,0:T(8,128)S(1)} %collective-permute-done.1.refs_2_, ...), custom_call_target="tpu_custom_call" | custom-call | bytes 3342336 | tf_op jit(solution)/shard_map/pallas_call | solution.py:410
  27.7 0.0 collective-permute-done.4.got
  27.7 2.1 %shard_map.81 = (f32[2,4,192,64]{3,2,1,0:T(8,128)S(1)}, f32[192,128]{1,0:T(8,128)S(1)}) custom-call(s32[3]{0:T(128)S(1)} %pad_add_fusion.ids_ref, f32[2,2,192,64]{3,2,1,0:T(8,128)S(1)} %shard_map.79.near, f32[2,192,256]{2,1,0:T(8,128)S(1)} %collective-permute-done.4.got, f32[2,2,1,384,192]{4,3,2,1,0:T(8,128)S(1)} %get-tuple-element.33.refs_4_.slab_d, ...), custom_call_target="tpu_custom_call" | custom-call | bytes 4030464 | tf_op jit(solution)/shard_map/pallas_call | solution.py:410
  29.8 0.6 collective-permute-start.6
  30.3 2.9 %shard_map.82 = (f32[2,768,192]{2,1,0:T(8,128)S(1)}, f32[2,768,192]{2,1,0:T(8,128)S(1)}, f32[2,768,192]{2,1,0:T(8,128)S(1)}) custom-call(s32[3]{0:T(128)S(1)} %pad_add_fusion.ids_ref, f32[2,2,4,192,192]{4,3,2,1,0:T(8,128)S(1)} %get-tuple-element.40.slab_ref, f32[2,192,192]{2,1,0:T(8,128)S(1)} %get-tuple-element.35.refs_4_.gap_ref, ...), custom_call_target="tpu_custom_call" | custom-call | flops 3538944000 | bytes 6193152 | tf_op jit(solution)/shard_map/pallas_call | solution.py:410
  33.3 3.4 %collective-permute-done.5.arrived = f32[2,192,192]{2,1,0:T(8,128)S(1)} collective-permute-done((f32[2,192,192]{2,1,0:T(8,128)S(1)}, f32[2,192,192]{2,1,0:T(8,128)S(1)}, u32[]{:S(2)}, u32[]{:S(2)}) %collective-permute-start.5) | collective-permute-done | bytes 294944 | tf_op jit(solution)/shard_map/ppermute | solution.py:513
  36.6 3.4 %shard_map.83 = (f32[2,768,64]{2,1,0:T(8,128)S(1)}, f32[2,192,192]{2,1,0:T(8,128)S(1)}, f32[192,128]{1,0:T(8,128)S(1)}) custom-call(f32[2,4,192,64]{3,2,1,0:T(8,128)S(1)} %get-tuple-element.38.slabs, f32[192,128]{1,0:T(8,128)S(1)} %get-tuple-element.39.refs_0_.end, f32[2,768,192]{2,1,0:T(8,128)S(1)} %get-tuple-element.41.pair_d, ...), custom_call_target="tpu_custom_call" | custom-call | flops 7077888000 | bytes 4227072 | tf_op jit(solution)/shard_map/pallas_call | solution.py:410
  40.0 0.0 collective-permute-done.6.crossed
  40.0 1.8 %shard_map.84 = (f32[2,192,128]{2,1,0:T(8,128)S(1)}, f32[2,192,64]{2,1,0:T(8,128)S(1)}) custom-call(s32[3]{0:T(128)S(1)} %pad_add_fusion.ids_ref, f32[2,768,64]{2,1,0:T(8,128)S(1)} %get-tuple-element.44.inner, f32[2,768,192]{2,1,0:T(8,128)S(1)} %get-tuple-element.45.answer, f32[2,192,192]{2,1,0:T(8,128)S(1)} %get-tuple-element.46.gate, ...), custom_call_target="tpu_custom_call" | custom-call | bytes 2359296 | tf_op jit(solution)/shard_map/pallas_call | solution.py:410
  41.8 0.1 collective-permute-start.7
  41.9 1.1 %shard_map.85.kept = f32[2,192,128]{2,1,0:T(8,128)S(1)} custom-call(s32[3]{0:T(128)S(1)} %pad_add_fusion.ids_ref, f32[2,768,64]{2,1,0:T(8,128)S(1)} %get-tuple-element.44.inner, f32[2,768,192]{2,1,0:T(8,128)S(1)} %get-tuple-element.45.answer, f32[2,192,64]{2,1,0:T(8,128)S(1)} %get-tuple-element.48.inward_ref), custom_call_target="tpu_custom_call" | custom-call | bytes 1867776 | tf_op jit(solution)/shard_map/pallas_call | solution.py:410
  43.0 0.3 collective-permute-done.7.got
  43.3 0.7 %shard_map.86 = (f32[192,128]{1,0:T(8,128)S(1)}, f32[192,128]{1,0:T(8,128)S(1)}, f32[192,128]{1,0:T(8,128)S(1)}, f32[192,128]{1,0:T(8,128)S(1)}) custom-call(s32[3]{0:T(128)S(1)} %pad_add_fusion.ids_ref, f32[2,192,128]{2,1,0:T(8,128)S(1)} %shard_map.85.kept, f32[2,192,128]{2,1,0:T(8,128)S(1)} %collective-permute-done.7.got), custom_call_target="tpu_custom_call" | custom-call | bytes 786432 | tf_op jit(solution)/shard_map/pallas_call | solution.py:410
  44.0 3.5 %collective-permute-start.8 = (f32[192,128]{1,0:T(8,128)S(1)}, f32[192,128]{1,0:T(8,128)S(1)}, u32[]{:S(2)}, u32[]{:S(2)}) collective-permute-start(f32[192,128]{1,0:T(8,128)S(1)} %get-tuple-element.51), channel_id=1, source_target_pairs={{0,1},{1,0},{2,3},{3,2},{4,5},{5,4},{6,7},{7,6},{8,9},{9,8},{10,11... | collective-permute-start | bytes 294920 | tf_op jit(solution)/shard_map/ppermute | solution.py:491
  47.4 1.1 %collective-permute-start.9 = (f32[192,128]{1,0:T(8,128)S(1)}, f32[192,128]{1,0:T(8,128)S(1)}, u32[]{:S(2)}, u32[]{:S(2)}) collective-permute-start(f32[192,128]{1,0:T(8,128)S(1)} %get-tuple-element.52), channel_id=1, source_target_pairs={{0,2},{1,3},{2,0},{3,1},{4,6},{5,7},{6,4},{7,5},{8,10},{9,11},{10,... | collective-permute-start | bytes 294920 | tf_op jit(solution)/shard_map/ppermute | solution.py:491
  48.5 1.4 %collective-permute-start.10 = (f32[192,128]{1,0:T(8,128)S(1)}, f32[192,128]{1,0:T(8,128)S(1)}, u32[]{:S(2)}, u32[]{:S(2)}) collective-permute-start(f32[192,128]{1,0:T(8,128)S(1)} %get-tuple-element.53), channel_id=1, source_target_pairs={{0,3},{1,2},{2,1},{3,0},{4,7},{5,6},{6,5},{7,4},{8,11},{9,10},{10,... | collective-permute-start | bytes 294920 | tf_op jit(solution)/shard_map/ppermute | solution.py:491
  49.9 0.7 %collective-permute-done.8.refs_1_ = f32[192,128]{1,0:T(8,128)S(1)} collective-permute-done((f32[192,128]{1,0:T(8,128)S(1)}, f32[192,128]{1,0:T(8,128)S(1)}, u32[]{:S(2)}, u32[]{:S(2)}) %collective-permute-start.8) | collective-permute-done | bytes 98336 | tf_op jit(solution)/shard_map/ppermute | solution.py:491
  50.6 7.5 %collective-permute-done.9.refs_2_ = f32[192,128]{1,0:T(8,128)S(1)} collective-permute-done((f32[192,128]{1,0:T(8,128)S(1)}, f32[192,128]{1,0:T(8,128)S(1)}, u32[]{:S(2)}, u32[]{:S(2)}) %collective-permute-start.9) | collective-permute-done | bytes 98336 | tf_op jit(solution)/shard_map/ppermute | solution.py:491
  58.1 0.0 collective-permute-done.10.refs_3_
  58.1 1.5 %shard_map.87 = (f32[1,1,192,256]{3,2,1,0:T(8,128)}, f32[1,1,192,256]{3,2,1,0:T(8,128)}) custom-call(s32[3]{0:T(128)S(1)} %pad_add_fusion.ids_ref, f32[192,128]{1,0:T(8,128)S(1)} %get-tuple-element.50.refs_0_, f32[192,128]{1,0:T(8,128)S(1)} %collective-permute-done.8.refs_1_, f32[192,128]{1,0:T(8,128)S(1)} %collective-permute-done.9.refs_2_, ...), custom_call_target="tpu_custom_call" | custom-call | bytes 786432 | tf_op jit(solution)/shard_map/pallas_call | solution.py:410
Async XLA Ops:
  0.7 9.8 %copy-start = (f32[4,4,192,192]{3,2,1,0:T(8,128)S(1)}, f32[4,4,192,192]{3,2,1,0:T(8,128)}, u32[]{:S(2)}) copy-start(f32[4,4,192,192]{3,2,1,0:T(8,128)} %table_ref.1) | copy-start | bytes 7077892
  3.6 18.0 %collective-permute-start = (f32[192,256]{1,0:T(8,128)S(1)}, f32[192,256]{1,0:T(8,128)S(1)}, u32[]{:S(2)}, u32[]{:S(2)}) collective-permute-start(f32[192,256]{1,0:T(8,128)S(1)} %get-tuple-element.29), channel_id=1, source_target_pairs={{0,1},{1,0},{2,3},{3,2},{4,5},{5,4},{6,7},{7,6},{8,9},{9,8},{10,11... | collective-permute-start | bytes 589832 | tf_op jit(solution)/shard_map/ppermute | solution.py:491
  6.8 17.1 %collective-permute-start.1 = (f32[192,256]{1,0:T(8,128)S(1)}, f32[192,256]{1,0:T(8,128)S(1)}, u32[]{:S(2)}, u32[]{:S(2)}) collective-permute-start(f32[192,256]{1,0:T(8,128)S(1)} %get-tuple-element.30), channel_id=1, source_target_pairs={{0,2},{1,3},{2,0},{3,1},{4,6},{5,7},{6,4},{7,5},{8,10},{9,11},{10,... | collective-permute-start | bytes 589832 | tf_op jit(solution)/shard_map/ppermute | solution.py:491
  9.3 14.5 %collective-permute-start.2 = (f32[192,256]{1,0:T(8,128)S(1)}, f32[192,256]{1,0:T(8,128)S(1)}, u32[]{:S(2)}, u32[]{:S(2)}) collective-permute-start(f32[192,256]{1,0:T(8,128)S(1)} %get-tuple-element.31), channel_id=1, source_target_pairs={{0,3},{1,2},{2,1},{3,0},{4,7},{5,6},{6,5},{7,4},{8,11},{9,10},{10,... | collective-permute-start | bytes 589832 | tf_op jit(solution)/shard_map/ppermute | solution.py:491
  9.3 1.2 %collective-permute-start.3 = (f32[2,2]{1,0:T(2,128)S(1)}, f32[2,2]{1,0:T(2,128)S(1)}, u32[]{:S(2)}, u32[]{:S(2)}) collective-permute-start(f32[2,2]{1,0:T(2,128)S(1)} %get-tuple-element.32), channel_id=1, source_target_pairs={{0,4},{4,0},{8,12},{12,8},{1,5},{5,1},{9,13},{13,9},{2,6},{6,2},{1... | collective-permute-start | bytes 56 | tf_op jit(solution)/shard_map/ppermute | solution.py:501
  24.5 3.2 %collective-permute-start.4 = (f32[2,192,256]{2,1,0:T(8,128)S(1)}, f32[2,192,256]{2,1,0:T(8,128)S(1)}, u32[]{:S(2)}, u32[]{:S(2)}) collective-permute-start(f32[2,192,256]{2,1,0:T(8,128)S(1)} %shard_map.80), channel_id=1, source_target_pairs={{0,4},{4,0},{8,12},{12,8},{1,5},{5,1},{9,13},{13,9},{2,6},{6,2},{1... | collective-permute-start | bytes 1179656 | tf_op jit(solution)/shard_map/ppermute | solution.py:516
  24.6 12.1 %collective-permute-start.5 = (f32[2,192,192]{2,1,0:T(8,128)S(1)}, f32[2,192,192]{2,1,0:T(8,128)S(1)}, u32[]{:S(2)}, u32[]{:S(2)}) collective-permute-start(f32[2,192,192]{2,1,0:T(8,128)S(1)} %get-tuple-element.43.onward), channel_id=1, source_target_pairs={{0,8},{4,12},{8,0},{12,4},{1,9},{5,13},{9,1},{13,5},{2,10},{6,14},... | collective-permute-start | bytes 884744 | tf_op jit(solution)/shard_map/ppermute | solution.py:513
  29.8 10.3 %collective-permute-start.6 = (f32[192,128]{1,0:T(8,128)S(1)}, f32[192,128]{1,0:T(8,128)S(1)}, u32[]{:S(2)}, u32[]{:S(2)}) collective-permute-start(f32[192,128]{1,0:T(8,128)S(1)} %get-tuple-element.39.refs_0_.end), channel_id=1, source_target_pairs={{0,8},{4,12},{8,0},{12,4},{1,9},{5,13},{9,1},{13,5},{2,10},{6,14},... | collective-permute-start | bytes 294920 | tf_op jit(solution)/shard_map/ppermute | solution.py:531
  41.8 1.5 %collective-permute-start.7 = (f32[2,192,128]{2,1,0:T(8,128)S(1)}, f32[2,192,128]{2,1,0:T(8,128)S(1)}, u32[]{:S(2)}, u32[]{:S(2)}) collective-permute-start(f32[2,192,128]{2,1,0:T(8,128)S(1)} %get-tuple-element.49), channel_id=1, source_target_pairs={{0,4},{4,0},{8,12},{12,8},{1,5},{5,1},{9,13},{13,9},{2,6},{6,2},{1... | collective-permute-start | bytes 589832 | tf_op jit(solution)/shard_map/ppermute | solution.py:548
  44.0 6.7 %collective-permute-start.8 = (f32[192,128]{1,0:T(8,128)S(1)}, f32[192,128]{1,0:T(8,128)S(1)}, u32[]{:S(2)}, u32[]{:S(2)}) collective-permute-start(f32[192,128]{1,0:T(8,128)S(1)} %get-tuple-element.51), channel_id=1, source_target_pairs={{0,1},{1,0},{2,3},{3,2},{4,5},{5,4},{6,7},{7,6},{8,9},{9,8},{10,11... | collective-permute-start | bytes 294920 | tf_op jit(solution)/shard_map/ppermute | solution.py:491
  47.4 10.7 %collective-permute-start.9 = (f32[192,128]{1,0:T(8,128)S(1)}, f32[192,128]{1,0:T(8,128)S(1)}, u32[]{:S(2)}, u32[]{:S(2)}) collective-permute-start(f32[192,128]{1,0:T(8,128)S(1)} %get-tuple-element.52), channel_id=1, source_target_pairs={{0,2},{1,3},{2,0},{3,1},{4,6},{5,7},{6,4},{7,5},{8,10},{9,11},{10,... | collective-permute-start | bytes 294920 | tf_op jit(solution)/shard_map/ppermute | solution.py:491
  48.5 9.6 %collective-permute-start.10 = (f32[192,128]{1,0:T(8,128)S(1)}, f32[192,128]{1,0:T(8,128)S(1)}, u32[]{:S(2)}, u32[]{:S(2)}) collective-permute-start(f32[192,128]{1,0:T(8,128)S(1)} %get-tuple-element.53), channel_id=1, source_target_pairs={{0,3},{1,2},{2,1},{3,0},{4,7},{5,6},{6,5},{7,4},{8,11},{9,10},{10,... | collective-permute-start | bytes 294920 | tf_op jit(solution)/shard_map/ppermute | solution.py:491
